TPU v7x, 32 devices: a whole 2x2x4 slice. The times are simulated.
32 devices in a mesh: expert: 8 (over z, y), dp: 4 (over x, core).
Axes of the slice: x: 2, y: 2, z: 4, core: 2. Of those that a mesh axis runs over, the one named last changes fastest.
Arguments:
- tokens: bfloat16 [4096, 1664], P(('expert', 'dp')), may hold values from -6 to 6
- out_grad: bfloat16 [4096, 1664], P(('expert', 'dp')), may hold values from -6 to 6
- expert_index: int32 [4096, 2], P(('expert', 'dp')), may hold values from 0 to 7, as said below
- slots: int32 [4096, 2], P(('expert', 'dp')), may hold values from -1 to 23, as said below
- combine: bfloat16 [4096, 2], P(('expert', 'dp')), may hold values from 0.099609375 to 1
- w_in: bfloat16 [8, 1664, 4096], P('expert', None, 'dp'), may hold values from -0.15625 to 0.15625
- b_in: float32 [8, 4096], P('expert', 'dp'), may hold values from -3 to 3
- w_out: bfloat16 [8, 4096, 1664], P('expert', 'dp'), may hold values from -0.09375 to 0.09375
Outputs:
- d_tokens: bfloat16 [4096, 1664], P(('expert', 'dp'))
- grad_w_in: float32 [8, 1664, 4096], P('expert', None, 'dp')
- grad_w_out: float32 [8, 4096, 1664], P('expert', 'dp')
- grad_b_in: float32 [8, 4096], P('expert', 'dp')
Inputs may be any that keep to these rules, and one draw needn't show every extreme that they name: `expert_index`: the two experts of a token differ. `slots`: a slot counts the earlier assignments to the same expert among the tokens of the same device, all first choices in token order before all second choices; it is -1 where that count reaches 24 (the assignment is dropped). So an expert takes at most 24 rows from one device, and in every draw some expert takes exactly 24 rows from every device.
All inputs are finite; a program needn't handle non-finite values.
Results may differ from a plain program's by a relative error of at most 0.01.
Values may be sent and summed in bfloat16 or wider, within the bound.
No kernel may reach another device: no remote copies, remote signals or barrier semaphores. Data moves between devices by JAX's collectives and lax.ppermute only.
A program may use at most 128 MiB of HBM per device.

v0:
```python
import jax
import jax.numpy as jnp
from jax import lax
from jax.sharding import PartitionSpec as P

inv_root_two = 0.7071067811865476
inv_root_two_pi = 0.3989422804014327


def gelu_value(values):
    return 0.5 * values * (1.0 + lax.erf(values * inv_root_two))


def gelu_slope(values):
    normal_cdf = 0.5 * (1.0 + lax.erf(values * inv_root_two))
    density = jnp.exp(-0.5 * values * values) * inv_root_two_pi
    return normal_cdf + values * density


def select(chosen, places, expert_count, capacity):
    expert_ids = jnp.arange(expert_count, dtype=jnp.int32)[:, None, None]
    slot_ids = jnp.arange(capacity, dtype=jnp.int32)[None, :, None]
    picks = []
    for member in range(2):
        same_expert = jnp.expand_dims(chosen[..., member], (-3, -2)) == expert_ids
        same_slot = jnp.expand_dims(places[..., member], (-3, -2)) == slot_ids
        picks.append((same_expert & same_slot).astype(jnp.bfloat16))
    return (picks[0], picks[1])


def scaled(weights, grads):
    grad_wide = grads.astype(jnp.float32)
    scaled_first = (weights[..., 0:1].astype(jnp.float32) * grad_wide).astype(jnp.bfloat16)
    scaled_second = (weights[..., 1:2].astype(jnp.float32) * grad_wide).astype(jnp.bfloat16)
    return (scaled_first, scaled_second)


def dispatch(inputs, scaled_first, scaled_second, pick_first, pick_second):
    rows_x = jnp.einsum(
        "recn,rnd->recd", pick_first + pick_second, inputs, preferred_element_type=jnp.float32
    )
    rows_g = jnp.einsum(
        "recn,rnd->recd", pick_first, scaled_first, preferred_element_type=jnp.float32
    )
    rows_g = rows_g + jnp.einsum(
        "recn,rnd->recd", pick_second, scaled_second, preferred_element_type=jnp.float32
    )
    return (rows_x.astype(jnp.bfloat16), rows_g.astype(jnp.bfloat16))


def on_device(tokens, out_grad, expert_index, slots, combine, w_in, b_in, w_out):
    expert_count = lax.axis_size("expert")
    replica_count = lax.axis_size("dp")
    tok_count, feat_width = tokens.shape
    capacity = max(2, (3 * tok_count + 2 * expert_count - 1) // (2 * expert_count))
    own_first, own_second = select(expert_index, slots, expert_count, capacity)
    pooled = (
        lax.all_gather(tokens, "dp", axis=0, tiled=True),
        lax.all_gather(out_grad, "dp", axis=0, tiled=True),
        lax.all_gather(combine, "dp", axis=0, tiled=True),
        lax.all_gather(expert_index, "dp", axis=0, tiled=True),
        lax.all_gather(slots, "dp", axis=0, tiled=True),
    )
    shaped = [array.reshape((replica_count, tok_count) + array.shape[1:]) for array in pooled]
    tok_all, grad_all, weight_all, chosen_all, places_all = shaped
    pick_first, pick_second = select(chosen_all, places_all, expert_count, capacity)
    scaled_first, scaled_second = scaled(weight_all, grad_all)
    send_x, send_g = dispatch(tok_all, scaled_first, scaled_second, pick_first, pick_second)
    rows_x, rows_g = (
        lax.all_to_all(send_x, "expert", split_axis=1, concat_axis=1, tiled=True),
        lax.all_to_all(send_g, "expert", split_axis=1, concat_axis=1, tiled=True),
    )
    rows_x = rows_x.reshape(-1, feat_width)
    rows_g = rows_g.reshape(-1, feat_width)
    first_w = w_in[0]
    second_w = w_out[0]
    pre_act = jnp.dot(rows_x, first_w, preferred_element_type=jnp.float32) + b_in[0]
    hidden = gelu_value(pre_act).astype(jnp.bfloat16)
    grad_second = lax.dot_general(
        hidden, rows_g, (((0,), (0,)), ((), ())), preferred_element_type=jnp.float32
    )
    d_hidden = lax.dot_general(
        rows_g, second_w, (((1,), (1,)), ((), ())), preferred_element_type=jnp.float32
    )
    d_pre = (d_hidden * gelu_slope(pre_act)).astype(jnp.bfloat16)
    grad_bias = jnp.sum(d_pre.astype(jnp.float32), axis=0)
    grad_first = lax.dot_general(
        rows_x, d_pre, (((0,), (0,)), ((), ())), preferred_element_type=jnp.float32
    )
    term = lax.dot_general(
        d_pre, first_w, (((1,), (1,)), ((), ())), preferred_element_type=jnp.float32
    )
    summed = lax.psum_scatter(
        lax.optimization_barrier(term.astype(jnp.bfloat16))
        .astype(jnp.float32)
        .astype(jnp.bfloat16),
        "dp",
        scatter_dimension=0,
        tiled=True,
    )
    d_rows = summed.reshape(expert_count, capacity, feat_width)
    returned = lax.all_to_all(d_rows, "expert", split_axis=0, concat_axis=0, tiled=True)
    d_tokens = jnp.einsum(
        "ecn,ecd->nd", own_first + own_second, returned, preferred_element_type=jnp.float32
    )
    return (d_tokens.astype(jnp.bfloat16), grad_first[None], grad_second[None], grad_bias[None])


def solution(mesh):
    in_specs = (
        P(("expert", "dp"), None),
        P(("expert", "dp"), None),
        P(("expert", "dp"), None),
        P(("expert", "dp"), None),
        P(("expert", "dp"), None),
        P("expert", None, "dp"),
        P("expert", "dp"),
        P("expert", "dp", None),
    )
    out_specs = (
        P(("expert", "dp"), None),
        P("expert", None, "dp"),
        P("expert", "dp", None),
        P("expert", "dp"),
    )
    return jax.shard_map(
        on_device, mesh=mesh, in_specs=in_specs, out_specs=out_specs, check_vma=False
    )
```

profile of v0, /device:TPU:0, one launch (start us, length us, event | category | flops | bytes accessed | tf_op | source)
XLA Modules:
  0.0 241.4 jit_solution(12847972751071568770)
XLA Ops:
  7.2 0.0 all-gather.5.cloned.1.call-start
  7.2 0.7 all-gather.5.cloned.1.call-update
  7.9 6.4 %all_gather.15 = s32[512,2]{0,1:T(2,128)S(1)} all-gather(s32[128,2]{0,1:T(2,128)} %param.10), channel_id=1, replica_groups=mesh['expert'=8,'dp'=4] {'dp'}, dimensions={0}, use_global_device_ids=true | all-gather | bytes 5120 | tf_op jit(solution)/shard_map/all_gather | solution.py:61
  14.3 5.5 %all_gather.16 = s32[512,2]{0,1:T(2,128)S(1)} all-gather(s32[128,2]{0,1:T(2,128)} %param.11), channel_id=1, replica_groups=mesh['expert'=8,'dp'=4] {'dp'}, dimensions={0}, use_global_device_ids=true | all-gather | bytes 5120 | tf_op jit(solution)/shard_map/all_gather | solution.py:62
  19.9 12.8 %all-gather.5.cloned.1.call-done = bf16[512,1664]{1,0:T(8,128)(2,1)} async-done(((bf16[128,1664]{1,0:T(8,128)(2,1)}), bf16[512,1664]{1,0:T(8,128)(2,1)}) %all-gather.5.cloned.1.call-update) | async-done | bytes 1703952 | tf_op jit(solution)/shard_map/all_gather | solution.py:58
  32.7 2.3 convolution_convert_fusion
  35.0 1.7 copy.16
  36.7 5.6 %all-to-all-start.1 = ((bf16[4,8,24,1664]{3,2,0,1:T(8,128)(2,1)}), bf16[4,8,24,1664]{3,2,0,1:T(8,128)(2,1)}, u32[]{:S(2)}, u32[]{:S(2)}) async-start(bf16[4,8,24,1664]{3,2,0,1:T(8,128)(2,1)} %copy.16), calls=%async_computation.1 | async-start | bytes 5111808 | tf_op jit(solution)/shard_map/all_to_all | solution.py:70
  42.4 0.7 all-gather.3.cloned.1.call-update
  43.1 5.0 %all_gather.17 = bf16[512,2]{0,1:T(2,128)(2,1)S(1)} all-gather(bf16[128,2]{0,1:T(2,128)(2,1)S(1)} %copy-done.7), channel_id=1, replica_groups=mesh['expert'=8,'dp'=4] {'dp'}, dimensions={0}, use_global_device_ids=true | all-gather | bytes 2560 | tf_op jit(solution)/shard_map/all_gather | solution.py:60
  48.1 17.5 %all-gather.3.cloned.1.call-done = bf16[512,1664]{1,0:T(8,128)(2,1)} async-done(((bf16[128,1664]{1,0:T(8,128)(2,1)}), bf16[512,1664]{1,0:T(8,128)(2,1)}) %all-gather.3.cloned.1.call-update) | async-done | bytes 1703952 | tf_op jit(solution)/shard_map/all_gather | solution.py:59
  65.6 2.5 %fusion.23 = f32[4,8,24,1664]{3,2,1,0:T(8,128)S(1)} fusion(bf16[4,128,1664]{2,1,0:T(8,128)(2,1)} %bitcast.84, f32[4,128]{1,0:T(4,128)S(1)} %get-tuple-element.9, pred[4,24,128]{2,1,0:T(8,128)(4,1)S(1)} %iota_compare_fusion.1, pred[4,8,128]{2,1,0:T(8,128)(4,1)S(1)} %iota_compare_fusion.3), kind=kOutput, calls=%fused_computation.29 | convolution fusion | flops 329809920 | bytes 6834176 | tf_op jit(solution)/shard_map/recn,rnd->recd/dot_general | solution.py:42
  68.1 0.9 add_convert_fusion
  69.0 1.7 copy.14
  70.7 30.2 %all-to-all-done.1 = bf16[4,8,24,1664]{3,2,0,1:T(8,128)(2,1)} async-done(((bf16[4,8,24,1664]{3,2,0,1:T(8,128)(2,1)}), bf16[4,8,24,1664]{3,2,0,1:T(8,128)(2,1)}, u32[]{:S(2)}, u32[]{:S(2)}) %all-to-all-start.1) | async-done | bytes 2555936 | tf_op jit(solution)/shard_map/all_to_all | solution.py:70
  100.9 4.4 %all-to-all-start = ((bf16[4,8,24,1664]{3,2,0,1:T(8,128)(2,1)}), bf16[4,8,24,1664]{3,2,0,1:T(8,128)(2,1)}, u32[]{:S(2)}, u32[]{:S(2)}) async-start(bf16[4,8,24,1664]{3,2,0,1:T(8,128)(2,1)} %copy.14), calls=%async_computation | async-start | bytes 5111808 | tf_op jit(solution)/shard_map/all_to_all | solution.py:71
  105.3 0.0 reduce-scatter.2.cloned.1.call-start
  105.4 1.9 copy.17
  107.3 1.5 copy-done.2
  108.8 4.7 %fusion.4 = f32[768,1024]{1,0:T(8,128)} fusion(bf16[768,1664]{1,0:T(8,128)(2,1)S(1)} %bitcast.87, bf16[1,1664,1024]{2,1,0:T(8,128)(2,1)S(1)} %copy-done), kind=kOutput, calls=%fused_computation.10 | convolution fusion | flops 2617245696 | bytes 9109504 | tf_op jit(solution)/shard_map/dot_general | solution.py:77
  113.5 49.5 %all-to-all-done = bf16[4,8,24,1664]{3,2,0,1:T(8,128)(2,1)} async-done(((bf16[4,8,24,1664]{3,2,0,1:T(8,128)(2,1)}), bf16[4,8,24,1664]{3,2,0,1:T(8,128)(2,1)}, u32[]{:S(2)}, u32[]{:S(2)}) %all-to-all-start) | async-done | bytes 2555936 | tf_op jit(solution)/shard_map/all_to_all | solution.py:71
  163.0 2.1 copy.15
  165.1 0.6 copy-done.8
  165.7 6.4 %convert_reduce_fusion = (f32[1024]{0:T(1024)}, bf16[768,1024]{1,0:T(8,128)(2,1)S(1)}) fusion(f32[768,1024]{1,0:T(8,128)} %fusion.4, f32[1024]{0:T(1024)S(1)} %bitcast.92, bf16[768,1664]{1,0:T(8,128)(2,1)S(1)} %bitcast.89, bf16[1,1024,1664]{2,1,0:T(8,128)(2,1)S(1)} %copy-done.8), kind=kOutput, calls=%fused_computation.22 | convolution fusion | flops 2627468288 | bytes 10690560 | tf_op jit(solution)/shard_map/dot_general | solution.py:82
  172.2 1.1 copy-done.11
  173.3 4.3 %fusion.8 = bf16[768,1664]{1,0:T(8,128)(2,1)} fusion(bf16[768,1024]{1,0:T(8,128)(2,1)S(1)} %get-tuple-element.15, bf16[1,1664,1024]{2,1,0:T(8,128)(2,1)S(1)} %copy-done), kind=kOutput, calls=%fused_computation.14 | convolution fusion | flops 2618523648 | bytes 7536640 | tf_op jit(solution)/shard_map/dot_general | solution.py:90
  177.7 32.4 %reduce-scatter.2.cloned.1.call-done = bf16[192,1664]{1,0:T(8,128)(2,1)} async-done(((bf16[768,1664]{1,0:T(8,128)(2,1)}), bf16[192,1664]{1,0:T(8,128)(2,1)}) %reduce-scatter.2.cloned.1.call-update) | async-done | bytes 638992 | tf_op jit(solution)/shard_map/reduce_scatter | solution.py:93
  210.2 5.5 %all-to-all-start.2 = ((bf16[8,24,1664]{2,1,0:T(8,128)(2,1)}), bf16[8,24,1664]{2,1,0:T(8,128)(2,1)}, u32[]{:S(2)}, u32[]{:S(2)}) async-start(bf16[8,24,1664]{2,1,0:T(8,128)(2,1)} %bitcast.91), calls=%async_computation.3 | async-start | bytes 1277952 | tf_op jit(solution)/shard_map/all_to_all | solution.py:102
  215.7 8.1 %convolution_bitcast_fusion.1 = f32[1,1664,1024]{2,1,0:T(8,128)} fusion(bf16[768,1664]{1,0:T(8,128)(2,1)} %bitcast.88, bf16[768,1024]{1,0:T(8,128)(2,1)} %copy-done.11), kind=kOutput, calls=%fused_computation.3 | convolution fusion | flops 2617245696 | bytes 10944512 | tf_op jit(solution)/shard_map/dot_general | solution.py:87
  223.8 5.1 %convolution_bitcast_fusion = f32[1,1024,1664]{2,1,0:T(8,128)} fusion(bf16[768,1664]{1,0:T(8,128)(2,1)S(1)} %bitcast.90, f32[768,1024]{1,0:T(8,128)S(1)} %copy-done.10, f32[1024]{0:T(1024)S(1)} %bitcast.93), kind=kOutput, calls=%fused_computation.2 | convolution fusion | flops 2621964288 | bytes 12521472 | tf_op jit(solution)/shard_map/dot_general | solution.py:79
  228.9 3.9 %all-to-all-done.2 = bf16[8,24,1664]{2,1,0:T(8,128)(2,1)} async-done(((bf16[8,24,1664]{2,1,0:T(8,128)(2,1)}), bf16[8,24,1664]{2,1,0:T(8,128)(2,1)}, u32[]{:S(2)}, u32[]{:S(2)}) %all-to-all-start.2) | async-done | bytes 639008 | tf_op jit(solution)/shard_map/all_to_all | solution.py:102
  232.7 2.2 fusion.17
  (37 shorter events, 0.2 us)
Async XLA Ops:
  7.2 101.6 %copy-start = (bf16[1,1664,1024]{2,1,0:T(8,128)(2,1)S(1)}, bf16[1,1664,1024]{2,1,0:T(8,128)(2,1)}, u32[]{:S(2)}) copy-start(bf16[1,1664,1024]{2,1,0:T(8,128)(2,1)} %param.13) | copy-start | bytes 10223620
  7.2 25.5 %all-gather.5.cloned.1.call-start = ((), (), s32[]{:S(2)}) async-start(), calls=%async_computation.5 | async-start | bytes 2129920 | tf_op jit(solution)/shard_map/all_gather | solution.py:58
  36.7 6.4 %copy-start.7 = (bf16[128,2]{0,1:T(2,128)(2,1)S(1)}, bf16[128,2]{0,1:T(2,128)(2,1)}, u32[]{:S(2)}) copy-start(bf16[128,2]{0,1:T(2,128)(2,1)} %param.12) | copy-start | bytes 1540
  36.7 64.2 %all-to-all-start.1 = ((bf16[4,8,24,1664]{3,2,0,1:T(8,128)(2,1)}), bf16[4,8,24,1664]{3,2,0,1:T(8,128)(2,1)}, u32[]{:S(2)}, u32[]{:S(2)}) async-start(bf16[4,8,24,1664]{3,2,0,1:T(8,128)(2,1)} %copy.16), calls=%async_computation.1 | async-start | bytes 5111808 | tf_op jit(solution)/shard_map/all_to_all | solution.py:70
  42.3 23.3 %all-gather.3.cloned.1.call-start = ((), (), s32[]{:S(2)}) async-start(), calls=%async_computation.4 | async-start | bytes 2129920 | tf_op jit(solution)/shard_map/all_gather | solution.py:59
  65.6 2.5 %copy-start.1 = (bf16[512,1664]{1,0:T(8,128)(2,1)S(1)}, bf16[512,1664]{1,0:T(8,128)(2,1)}, u32[]{:S(2)}) copy-start(bf16[512,1664]{1,0:T(8,128)(2,1)} %all-gather.3.cloned.1.call-done) | copy-start | bytes 5111812
  100.9 62.1 %all-to-all-start = ((bf16[4,8,24,1664]{3,2,0,1:T(8,128)(2,1)}), bf16[4,8,24,1664]{3,2,0,1:T(8,128)(2,1)}, u32[]{:S(2)}, u32[]{:S(2)}) async-start(bf16[4,8,24,1664]{3,2,0,1:T(8,128)(2,1)} %copy.14), calls=%async_computation | async-start | bytes 5111808 | tf_op jit(solution)/shard_map/all_to_all | solution.py:71
  105.3 104.8 %reduce-scatter.2.cloned.1.call-start = ((), (), s32[]{:S(2)}) async-start(), calls=%async_computation.6 | async-start | bytes 3194880 | tf_op jit(solution)/shard_map/reduce_scatter | solution.py:93
  107.3 1.5 copy-start.2
  113.5 51.6 %copy-start.9 = (f32[1,1024]{1,0:T(1,128)S(1)}, f32[1,1024]{1,0:T(1,128)}, u32[]{:S(2)}) copy-start(f32[1,1024]{1,0:T(1,128)} %param.14) | copy-start | bytes 12292
  163.0 2.7 %copy-start.8 = (bf16[1,1024,1664]{2,1,0:T(8,128)(2,1)S(1)}, bf16[1,1024,1664]{2,1,0:T(8,128)(2,1)}, u32[]{:S(2)}) copy-start(bf16[1,1024,1664]{2,1,0:T(8,128)(2,1)} %param.15) | copy-start | bytes 10223620
  165.1 7.1 %copy-start.3 = (bf16[4,8,24,1664]{3,2,1,0:T(8,128)(2,1)}, bf16[4,8,24,1664]{3,2,1,0:T(8,128)(2,1)S(1)}, u32[]{:S(2)}) copy-start(bf16[4,8,24,1664]{3,2,1,0:T(8,128)(2,1)S(1)} %copy.15) | copy-start | bytes 7667716
  172.2 1.2 copy-start.11
  173.3 4.4 %copy-start.5 = (s32[128,2]{0,1:T(2,128)S(1)}, s32[128,2]{0,1:T(2,128)}, u32[]{:S(2)}) copy-start(s32[128,2]{0,1:T(2,128)} %param.10) | copy-start | bytes 3076
  173.3 4.4 %copy-start.6 = (s32[128,2]{0,1:T(2,128)S(1)}, s32[128,2]{0,1:T(2,128)}, u32[]{:S(2)}) copy-start(s32[128,2]{0,1:T(2,128)} %param.11) | copy-start | bytes 3076
  210.2 22.6 %all-to-all-start.2 = ((bf16[8,24,1664]{2,1,0:T(8,128)(2,1)}), bf16[8,24,1664]{2,1,0:T(8,128)(2,1)}, u32[]{:S(2)}, u32[]{:S(2)}) async-start(bf16[8,24,1664]{2,1,0:T(8,128)(2,1)} %bitcast.91), calls=%async_computation.3 | async-start | bytes 1277952 | tf_op jit(solution)/shard_map/all_to_all | solution.py:102
  215.7 8.1 %copy-start.4 = (bf16[4,8,24,1664]{3,2,1,0:T(8,128)(2,1)S(1)}, bf16[4,8,24,1664]{3,2,1,0:T(8,128)(2,1)}, u32[]{:S(2)}) copy-start(bf16[4,8,24,1664]{3,2,1,0:T(8,128)(2,1)} %copy-done.3) | copy-start | bytes 7667716
  215.7 8.1 %copy-start.10 = (f32[768,1024]{1,0:T(8,128)S(1)}, f32[768,1024]{1,0:T(8,128)}, u32[]{:S(2)}) copy-start(f32[768,1024]{1,0:T(8,128)} %fusion.4) | copy-start | bytes 9437188
Sparse Core Ops, SparseCore 0:
  9.6 23.0 all-gather.4
  44.7 20.8 all-gather.2
  177.8 32.3 reduce-scatter.1
where the time goes:
time: 242 us; the launch traced here: 241 us
  waiting for transfers between devices  148 us (61%)
  matrix products  36.5 us (15%)
  blocking collectives  16.9 us (7%)
  starting transfers between devices  15.7 us (6%)
  between operations  13.9 us (6%)
  local copies, waits for them, and re-layouts  10.7 us (4%)
    all_to_all x1, waiting for transfers between devices, on_device(): lax.all_to_all(send_g, 'expert', split_axis=1, concat_axis=1, tiled=True)  49.5 us
    reduce_scatter x1, waiting for transfers between devices, on_device(): lax.psum_scatter(lax.optimization_barrier(term.astype(jnp.bfloat16)).asty...  32.4 us
    all_to_all x1, waiting for transfers between devices, on_device(): lax.all_to_all(send_x, 'expert', split_axis=1, concat_axis=1, tiled=True)  30.2 us
    all_gather x1, waiting for transfers between devices, on_device(): lax.all_gather(out_grad, 'dp', axis=0, tiled=True)  17.5 us
    all_gather x1, waiting for transfers between devices, on_device(): lax.all_gather(tokens, 'dp', axis=0, tiled=True)  12.8 us
    dot_general x1, matrix products, on_device(): lax.dot_general(rows_x, d_pre, (((0,), (0,)), ((), ())), preferred_elemen...  8.06 us
    dot_general x1, matrix products, on_device(): lax.dot_general(rows_g, second_w, (((1,), (1,)), ((), ())), preferred_ele...  6.44 us
    all_gather x1, blocking collectives, on_device(): lax.all_gather(expert_index, 'dp', axis=0, tiled=True)  6.39 us
  transfers between devices with their start and end apart: 6, of which 6 were waited for; matrix products, arithmetic and copies ran while one was open for 10% of the time, Pallas kernels for 0%

commit v1 on v0

v1 whole, which is shorter than its diff:
```python
import jax
import jax.numpy as jnp
from jax import lax
from jax.sharding import PartitionSpec as P

inv_root_two = 0.7071067811865476
inv_root_two_pi = 0.3989422804014327


def swap(value, axis, mask):
    size = lax.axis_size(axis)
    return lax.ppermute(value, axis, [(i, i ^ mask) for i in range(size)])


def joined(pieces):
    return pieces[0] if len(pieces) == 1 else jnp.concatenate(pieces, axis=0)


def picks(expert_index, slots, expert_ids, capacity):
    expert_ids = expert_ids[:, None, None]
    slot_ids = jnp.arange(capacity, dtype=jnp.int32)[None, :, None]
    return [
        (expert_index[None, None, :, k] == expert_ids) & (slots[None, None, :, k] == slot_ids)
        for k in range(2)
    ]


def on_device(tokens, out_grad, expert_index, slots, combine, w_in, b_in, w_out):
    experts = lax.axis_size("expert")
    tok_count, width = tokens.shape
    capacity = max(2, (3 * tok_count + 2 * experts - 1) // (2 * experts))
    me = lax.axis_index("expert")
    first_w, second_w, bias = w_in[0], w_out[0], b_in[0]

    order = jnp.bitwise_xor(me, jnp.arange(experts, dtype=jnp.int32))
    pick = picks(expert_index, slots, order, capacity)
    chosen = (pick[0] | pick[1]).astype(jnp.bfloat16).reshape(experts * capacity, tok_count)
    scale = sum(
        jnp.sum(jnp.where(pick[k], combine[None, None, :, k].astype(jnp.float32), 0.0), axis=-1)
        for k in range(2)
    ).reshape(experts * capacity, 1)
    rows_x = jnp.dot(chosen, tokens, preferred_element_type=jnp.float32).astype(jnp.bfloat16)
    rows_g = jnp.dot(chosen, out_grad, preferred_element_type=jnp.float32)
    rows_g = (rows_g * scale).astype(jnp.bfloat16)
    rows = jnp.concatenate([rows_x, rows_g], axis=1)

    def block(k):
        return rows[k * capacity : (k + 1) * capacity]

    across_masks = [2 << i for i in range(lax.axis_size("dp").bit_length() - 2)]
    half, quarter = experts // 2, experts // 4
    near = list(range(half))
    far_one = list(range(half, half + quarter))
    far_two = list(range(half + quarter, experts))
    got = {0: block(0)}
    for k in far_one + near[1:]:
        got[k] = swap(block(k), "expert", k)
    late = rows[(half + quarter) * capacity :]
    late, got[half - 1] = lax.optimization_barrier((late, got[half - 1]))
    for i, k in enumerate(far_two):
        got[k] = swap(late[i * capacity : (i + 1) * capacity], "expert", k)

    groups = [[0], near[1:], far_one, far_two]
    sets = []
    for group in groups:
        pieces = [joined([got[k] for k in group])]
        for mask in across_masks:
            pieces = pieces + [swap(piece, "dp", mask) for piece in pieces]
        sets.append(pieces + [swap(piece, "dp", 1) for piece in pieces])
    sets = [[jnp.concatenate([a, b]) for a, b in zip(sets[0], sets[1])]] + sets[2:]

    hidden_parts, slope_parts, row_parts, back = [], [], [], []
    for pieces in sets:
        chunk = jnp.concatenate(pieces)
        x, g = chunk[:, :width], chunk[:, width:]
        pre_act = jnp.dot(x, first_w, preferred_element_type=jnp.float32) + bias
        cdf = 0.5 * (1.0 + lax.erf(pre_act * inv_root_two))
        hidden = (pre_act * cdf).astype(jnp.bfloat16)
        density = jnp.exp(-0.5 * pre_act * pre_act) * inv_root_two_pi
        d_hidden = lax.dot_general(
            g, second_w, (((1,), (1,)), ((), ())), preferred_element_type=jnp.float32
        )
        d_pre = (d_hidden * (cdf + pre_act * density)).astype(jnp.bfloat16)
        term = lax.dot_general(
            d_pre, first_w, (((1,), (1,)), ((), ())), preferred_element_type=jnp.float32
        ).astype(jnp.bfloat16)
        hidden_parts.append(hidden)
        slope_parts.append(d_pre)
        row_parts.append(chunk)
        for mask in [1] + across_masks[::-1]:
            kept = term.shape[0] // 2
            arrived = swap(term[kept:], "dp", mask)
            term = (term[:kept].astype(jnp.float32) + arrived.astype(jnp.float32)).astype(jnp.bfloat16)
        back.append(term)

    returned = []
    for group, rows_back in zip([near, far_one, far_two], back):
        for i, k in enumerate(group):
            part = rows_back[i * capacity : (i + 1) * capacity]
            returned.append(part if k == 0 else swap(part, "expert", k))
    returned = jnp.concatenate(returned)
    d_tokens = lax.dot_general(
        chosen, returned, (((0,), (0,)), ((), ())), preferred_element_type=jnp.float32
    )

    hidden = jnp.concatenate(hidden_parts)
    d_pre = jnp.concatenate(slope_parts)
    rows_all = jnp.concatenate(row_parts)
    grad_second = lax.dot_general(
        hidden, rows_all[:, width:], (((0,), (0,)), ((), ())), preferred_element_type=jnp.float32
    )
    grad_first = lax.dot_general(
        rows_all[:, :width], d_pre, (((0,), (0,)), ((), ())), preferred_element_type=jnp.float32
    )
    grad_bias = jnp.sum(d_pre.astype(jnp.float32), axis=0)
    return (d_tokens.astype(jnp.bfloat16), grad_first[None], grad_second[None], grad_bias[None])


def solution(mesh):
    in_specs = (
        P(("expert", "dp"), None),
        P(("expert", "dp"), None),
        P(("expert", "dp"), None),
        P(("expert", "dp"), None),
        P(("expert", "dp"), None),
        P("expert", None, "dp"),
        P("expert", "dp"),
        P("expert", "dp", None),
    )
    out_specs = (
        P(("expert", "dp"), None),
        P("expert", None, "dp"),
        P("expert", "dp", None),
        P("expert", "dp"),
    )
    return jax.shard_map(
        on_device, mesh=mesh, in_specs=in_specs, out_specs=out_specs, check_vma=False
    )
```

time: 242 us -> 113 us (0.47)
  waiting for transfers between devices: 148 us -> 43.8 us
  starting transfers between devices: 15.7 us -> 35.8 us
  blocking collectives: 16.9 us -> 0 us
  between operations: 13.9 us -> 1.19 us
  matrix products: 36.5 us -> 26.5 us
  local copies, waits for them, and re-layouts: 10.7 us -> 3.04 us
  other arithmetic: 0.06 us -> 2.49 us
    all_to_all x3 -> x0, waiting for transfers between devices: 83.5 us -> none  [the longest x1 49.5 us: on_device(): lax.all_to_all(send_g, 'expert', split_axis=1, concat_axis=1, tiled=True)]
    ppermute x0 -> x32, waiting for transfers between devices: none -> 43.8 us  [swap(): return lax.ppermute(value, axis, [(i, i ^ mask) for i in range(size)])]
    ppermute x0 -> x32, starting transfers between devices: none -> 35.8 us  [swap(): return lax.ppermute(value, axis, [(i, i ^ mask) for i in range(size)])]
    reduce_scatter x1 -> x0, waiting for transfers between devices: 32.4 us -> none  [on_device(): lax.psum_scatter(lax.optimization_barrier(term.astype(jnp.bfloat16)).asty...]
    all_gather x2 -> x0, waiting for transfers between devices: 30.3 us -> none  [the longest x1 17.5 us: on_device(): lax.all_gather(out_grad, 'dp', axis=0, tiled=True)]
    all_gather x3 -> x0, blocking collectives: 16.9 us -> none  [the longest x1 6.39 us: on_device(): lax.all_gather(expert_index, 'dp', axis=0, tiled=True)]
    all_to_all x3 -> x0, starting transfers between devices: 15.6 us -> none  [the longest x1 5.65 us: on_device(): lax.all_to_all(send_x, 'expert', split_axis=1, concat_axis=1, tiled=True)]
    dot_general x8 -> x11, matrix products: 32.2 us -> 22.3 us  [the longest x1 5.1 us: on_device(): lax.dot_general(hidden, rows_all[:, width:], (((0,), (0,)), ((), ())), pr...]
  transfers between devices with their start and end apart: 6 -> 32, of which waited for: 6 -> 13; matrix products, arithmetic and copies ran while one was open for 10% -> 19% of each run, Pallas kernels for 0% -> 0%
where the time goes in v1:
time: 113 us
  waiting for transfers between devices  43.8 us (39%)
  starting transfers between devices  35.8 us (32%)
  matrix products  26.5 us (23%)
  local copies, waits for them, and re-layouts  3.04 us (3%)
  other arithmetic  2.49 us (2%)
  between operations  1.19 us (1%)
    ppermute x32, waiting for transfers between devices, swap(): return lax.ppermute(value, axis, [(i, i ^ mask) for i in range(size)])  43.8 us
    ppermute x32, starting transfers between devices, swap(): return lax.ppermute(value, axis, [(i, i ^ mask) for i in range(size)])  35.8 us
    dot_general x1, matrix products, on_device(): lax.dot_general(hidden, rows_all[:, width:], (((0,), (0,)), ((), ())), pr...  5.1 us
    dot_general x1, matrix products, on_device(): lax.dot_general(rows_all[:, :width], d_pre, (((0,), (0,)), ((), ())), pre...  4.86 us
    dot_general x3, matrix products, on_device(): lax.dot_general(g, second_w, (((1,), (1,)), ((), ())), preferred_element_...  4.7 us
    dot_general x3, matrix products, on_device(): lax.dot_general(d_pre, first_w, (((1,), (1,)), ((), ())), preferred_eleme...  4.17 us
    dot_general x3, matrix products, on_device(): pre_act = jnp.dot(x, first_w, preferred_element_type=jnp.float32) + bias  3.92 us
  transfers between devices with their start and end apart: 32, of which 13 were waited for; matrix products, arithmetic and copies ran while one was open for 19% of the time, Pallas kernels for 0%

profile of v1, /device:TPU:0, one launch (start us, length us, event | category | flops | bytes accessed | tf_op | source)
XLA Modules:
  0.0 112.8 jit_solution(16321938636503334886)
XLA Ops:
  3.6 1.3 %convolution_convert_fusion = bf16[192,1664]{1,0:T(8,128)(2,1)S(1)} fusion(pred[192,128]{1,0:T(8,128)(4,1)S(1)} %bitcast.78, bf16[128,1664]{1,0:T(8,128)(2,1)} %param.8), kind=kOutput, calls=%fused_computation.27 | convolution fusion | flops 82108416 | bytes 1089536 | tf_op jit(solution)/shard_map/dot_general | solution.py:42
  4.9 1.3 %fusion.29 = bf16[192,1664]{1,0:T(8,128)(2,1)S(1)} fusion(pred[192,128]{1,0:T(8,128)(4,1)S(1)} %bitcast.79, bf16[128,1664]{1,0:T(8,128)(2,1)} %param.9, f32[192]{0:T(256)S(1)} %add.74), kind=kOutput, calls=%fused_computation.28 | convolution fusion | flops 82427904 | bytes 1090304 | tf_op jit(solution)/shard_map/dot_general | solution.py:43
  6.3 3.0 %collective-permute-start.3 = (bf16[24,3328]{1,0:T(8,128)(2,1)S(1)}, bf16[24,3328]{1,0:T(8,128)(2,1)S(1)}, u32[]{:S(2)}, u32[]{:S(2)}) collective-permute-start(bf16[24,3328]{1,0:T(8,128)(2,1)S(1)} %get-tuple-element.15), channel_id=1, source_target_pairs={{0,2},{1,3},{2,0},{3,1},{4,6},{5,7},{6,4},{7,5},{8,10},{9,11},{10,... | collective-permute-start | bytes 479240 | tf_op jit(solution)/shard_map/ppermute | solution.py:12
  9.3 1.5 %collective-permute-start = (bf16[24,3328]{1,0:T(8,128)(2,1)S(1)}, bf16[24,3328]{1,0:T(8,128)(2,1)S(1)}, u32[]{:S(2)}, u32[]{:S(2)}) collective-permute-start(bf16[24,3328]{1,0:T(8,128)(2,1)S(1)} %get-tuple-element.13), channel_id=1, source_target_pairs={{0,4},{4,0},{8,12},{12,8},{16,20},{20,16},{24,28},{28,24},{1,5},{5... | collective-permute-start | bytes 479240 | tf_op jit(solution)/shard_map/ppermute | solution.py:12
  10.8 1.6 %collective-permute-start.1 = (bf16[24,3328]{1,0:T(8,128)(2,1)S(1)}, bf16[24,3328]{1,0:T(8,128)(2,1)S(1)}, u32[]{:S(2)}, u32[]{:S(2)}) collective-permute-start(bf16[24,3328]{1,0:T(8,128)(2,1)S(1)} %get-tuple-element.12), channel_id=1, source_target_pairs={{0,8},{4,12},{8,0},{12,4},{16,24},{20,28},{24,16},{28,20},{1,9},{5... | collective-permute-start | bytes 479240 | tf_op jit(solution)/shard_map/ppermute | solution.py:12
  12.9 3.0 %collective-permute-done = bf16[24,3328]{1,0:T(8,128)(2,1)S(1)} collective-permute-done((bf16[24,3328]{1,0:T(8,128)(2,1)S(1)}, bf16[24,3328]{1,0:T(8,128)(2,1)S(1)}, u32[]{:S(2)}, u32[]{:S(2)}) %collective-permute-start) | collective-permute-done | bytes 159776 | tf_op jit(solution)/shard_map/ppermute | solution.py:12
  15.8 2.6 %collective-permute-start.14 = (bf16[24,3328]{1,0:T(8,128)(2,1)S(1)}, bf16[24,3328]{1,0:T(8,128)(2,1)S(1)}, u32[]{:S(2)}, u32[]{:S(2)}) collective-permute-start(bf16[24,3328]{1,0:T(8,128)(2,1)S(1)} %get-tuple-element.16), channel_id=1, source_target_pairs={{0,16},{4,20},{8,24},{12,28},{16,0},{20,4},{24,8},{28,12},{1,17},{... | collective-permute-start | bytes 479240 | tf_op jit(solution)/shard_map/ppermute | solution.py:12
  18.5 4.1 %collective-permute-done.2 = bf16[24,3328]{1,0:T(8,128)(2,1)S(1)} collective-permute-done((bf16[24,3328]{1,0:T(8,128)(2,1)S(1)}, bf16[24,3328]{1,0:T(8,128)(2,1)S(1)}, u32[]{:S(2)}, u32[]{:S(2)}) %collective-permute-start.2) | collective-permute-done | bytes 159776 | tf_op jit(solution)/shard_map/ppermute | solution.py:12
  22.5 2.2 %collective-permute-start.15 = (bf16[24,3328]{1,0:T(8,128)(2,1)S(1)}, bf16[24,3328]{1,0:T(8,128)(2,1)S(1)}, u32[]{:S(2)}, u32[]{:S(2)}) collective-permute-start(bf16[24,3328]{1,0:T(8,128)(2,1)S(1)} %get-tuple-element.10), channel_id=1, source_target_pairs={{0,20},{4,16},{8,28},{12,24},{16,4},{20,0},{24,12},{28,8},{1,21},{... | collective-permute-start | bytes 479240 | tf_op jit(solution)/shard_map/ppermute | solution.py:12
  25.5 10.6 %collective-permute-done.4 = bf16[72,3328]{1,0:T(8,128)(2,1)S(1)} collective-permute-done((bf16[72,3328]{1,0:T(8,128)(2,1)S(1)}, bf16[72,3328]{1,0:T(8,128)(2,1)S(1)}, u32[]{:S(2)}, u32[]{:S(2)}) %collective-permute-start.4) | collective-permute-done | bytes 479264 | tf_op jit(solution)/shard_map/ppermute | solution.py:12
  36.1 1.3 %collective-permute-start.23 = (bf16[24,3328]{1,0:T(8,128)(2,1)S(1)}, bf16[24,3328]{1,0:T(8,128)(2,1)S(1)}, u32[]{:S(2)}, u32[]{:S(2)}) collective-permute-start(bf16[24,3328]{1,0:T(8,128)(2,1)S(1)} %get-tuple-element.36), channel_id=1, source_target_pairs={{0,24},{4,28},{8,16},{12,20},{16,8},{20,12},{24,0},{28,4},{1,25},{... | collective-permute-start | bytes 479240 | tf_op jit(solution)/shard_map/ppermute | solution.py:12
  39.0 3.6 %collective-permute-start.24 = (bf16[24,3328]{1,0:T(8,128)(2,1)S(1)}, bf16[24,3328]{1,0:T(8,128)(2,1)S(1)}, u32[]{:S(2)}, u32[]{:S(2)}) collective-permute-start(bf16[24,3328]{1,0:T(8,128)(2,1)S(1)} %get-tuple-element.35), channel_id=1, source_target_pairs={{0,28},{4,24},{8,20},{12,16},{16,12},{20,8},{24,4},{28,0},{1,29},{... | collective-permute-start | bytes 479240 | tf_op jit(solution)/shard_map/ppermute | solution.py:12
  43.5 1.8 %multiply_convert_fusion = (bf16[384,1024]{1,0:T(8,128)(2,1)S(1)}, f32[384,1024]{1,0:T(8,128)S(1)}) fusion(f32[1024]{0:T(1024)S(1)} %bitcast.82, bf16[1,1664,1024]{2,1,0:T(8,128)(2,1)S(1)} %copy-done, bf16[384,3328]{1,0:T(8,128)(2,1)S(1)} %get-tuple-element.18), kind=kOutput, calls=%fused_computation.49 | convolution fusion | flops 1310982144 | bytes 7049216 | tf_op jit(solution)/shard_map/dot_general | solution.py:76
  45.4 1.9 %fusion.35 = bf16[384,1024]{1,0:T(8,128)(2,1)S(1)} fusion(f32[384,1024]{1,0:T(8,128)S(1)} %get-tuple-element.85, bf16[1,1024,1664]{2,1,0:T(8,128)(2,1)S(1)} %copy-done.1, bf16[384,3328]{1,0:T(8,128)(2,1)S(1)} %get-tuple-element.18), kind=kOutput, calls=%fused_computation.42 | convolution fusion | flops 1312555008 | bytes 7045120 | tf_op jit(solution)/shard_map/dot_general | solution.py:80
  47.3 1.6 %fusion.18 = bf16[384,1664]{1,0:T(8,128)(2,1)S(1)} fusion(bf16[384,1024]{1,0:T(8,128)(2,1)S(1)} %fusion.35, bf16[1,1664,1024]{2,1,0:T(8,128)(2,1)S(1)} %copy-done), kind=kOutput, calls=%fused_computation.21 | convolution fusion | flops 1309261824 | bytes 5472256 | tf_op jit(solution)/shard_map/dot_general | solution.py:84
  49.5 2.6 %collective-permute-done.16 = bf16[48,3328]{1,0:T(8,128)(2,1)S(1)} collective-permute-done((bf16[48,3328]{1,0:T(8,128)(2,1)S(1)}, bf16[48,3328]{1,0:T(8,128)(2,1)S(1)}, u32[]{:S(2)}, u32[]{:S(2)}) %collective-permute-start.16) | collective-permute-done | bytes 319520 | tf_op jit(solution)/shard_map/ppermute | solution.py:12
  52.3 1.5 %collective-permute-done.18 = bf16[48,3328]{1,0:T(8,128)(2,1)S(1)} collective-permute-done((bf16[48,3328]{1,0:T(8,128)(2,1)S(1)}, bf16[48,3328]{1,0:T(8,128)(2,1)S(1)}, u32[]{:S(2)}, u32[]{:S(2)}) %collective-permute-start.18) | collective-permute-done | bytes 319520 | tf_op jit(solution)/shard_map/ppermute | solution.py:12
  55.6 1.3 %fusion.63 = bf16[192,1024]{1,0:T(8,128)(2,1)S(1)} fusion(bf16[1,1024,1664]{2,1,0:T(8,128)(2,1)S(1)} %copy-done.1, f32[192,1024]{1,0:T(8,128)S(1)} %get-tuple-element.83, bf16[192,3328]{1,0:T(8,128)(2,1)S(1)} %get-tuple-element.30), kind=kOutput, calls=%fused_computation.60 | convolution fusion | flops 656277504 | bytes 5226496 | tf_op jit(solution)/shard_map/dot_general | solution.py:80
  57.0 1.3 %fusion.23 = bf16[192,1664]{1,0:T(8,128)(2,1)S(1)} fusion(bf16[192,1024]{1,0:T(8,128)(2,1)S(1)} %fusion.63, bf16[1,1664,1024]{2,1,0:T(8,128)(2,1)S(1)} %copy-done), kind=kOutput, calls=%fused_computation.25 | convolution fusion | flops 654630912 | bytes 4440064 | tf_op jit(solution)/shard_map/dot_general | solution.py:84
  59.0 1.5 %collective-permute-start.10 = (bf16[96,1664]{1,0:T(8,128)(2,1)S(1)}, bf16[96,1664]{1,0:T(8,128)(2,1)S(1)}, u32[]{:S(2)}, u32[]{:S(2)}) collective-permute-start(bf16[96,1664]{1,0:T(8,128)(2,1)S(1)} %slice.181), channel_id=1, source_target_pairs={{0,2},{1,3},{2,0},{3,1},{4,6},{5,7},{6,4},{7,5},{8,10},{9,11},{10,... | collective-permute-start | bytes 958472 | tf_op jit(solution)/shard_map/ppermute | solution.py:12
  61.7 9.5 %collective-permute-done.10 = bf16[96,1664]{1,0:T(8,128)(2,1)S(1)} collective-permute-done((bf16[96,1664]{1,0:T(8,128)(2,1)S(1)}, bf16[96,1664]{1,0:T(8,128)(2,1)S(1)}, u32[]{:S(2)}, u32[]{:S(2)}) %collective-permute-start.10) | collective-permute-done | bytes 319520 | tf_op jit(solution)/shard_map/ppermute | solution.py:12
  72.9 2.0 %collective-permute-start.13 = (bf16[24,1664]{1,0:T(8,128)(2,1)S(1)}, bf16[24,1664]{1,0:T(8,128)(2,1)S(1)}, u32[]{:S(2)}, u32[]{:S(2)}) collective-permute-start(bf16[24,1664]{1,0:T(8,128)(2,1)S(1)} %get-tuple-element.37), channel_id=1, source_target_pairs={{0,12},{4,8},{8,4},{12,0},{16,28},{20,24},{24,20},{28,16},{1,13},{... | collective-permute-start | bytes 239624 | tf_op jit(solution)/shard_map/ppermute | solution.py:12
  76.4 1.9 %collective-permute-start.21 = (bf16[24,1664]{1,0:T(8,128)(2,1)S(1)}, bf16[24,1664]{1,0:T(8,128)(2,1)S(1)}, u32[]{:S(2)}, u32[]{:S(2)}) collective-permute-start(bf16[24,1664]{1,0:T(8,128)(2,1)S(1)} %get-tuple-element.71), channel_id=1, source_target_pairs={{0,16},{4,20},{8,24},{12,28},{16,0},{20,4},{24,8},{28,12},{1,17},{... | collective-permute-start | bytes 239624 | tf_op jit(solution)/shard_map/ppermute | solution.py:12
  78.3 2.1 %collective-permute-start.22 = (bf16[24,1664]{1,0:T(8,128)(2,1)S(1)}, bf16[24,1664]{1,0:T(8,128)(2,1)S(1)}, u32[]{:S(2)}, u32[]{:S(2)}) collective-permute-start(bf16[24,1664]{1,0:T(8,128)(2,1)S(1)} %get-tuple-element.70), channel_id=1, source_target_pairs={{0,20},{4,16},{8,28},{12,24},{16,4},{20,0},{24,12},{28,8},{1,21},{... | collective-permute-start | bytes 239624 | tf_op jit(solution)/shard_map/ppermute | solution.py:12
  80.5 3.2 %collective-permute-done.21 = bf16[24,1664]{1,0:T(8,128)(2,1)S(1)} collective-permute-done((bf16[24,1664]{1,0:T(8,128)(2,1)S(1)}, bf16[24,1664]{1,0:T(8,128)(2,1)S(1)}, u32[]{:S(2)}, u32[]{:S(2)}) %collective-permute-start.21) | collective-permute-done | bytes 79904 | tf_op jit(solution)/shard_map/ppermute | solution.py:12
  83.7 2.2 %collective-permute-done.22 = bf16[24,1664]{1,0:T(8,128)(2,1)S(1)} collective-permute-done((bf16[24,1664]{1,0:T(8,128)(2,1)S(1)}, bf16[24,1664]{1,0:T(8,128)(2,1)S(1)}, u32[]{:S(2)}, u32[]{:S(2)}) %collective-permute-start.22) | collective-permute-done | bytes 79904 | tf_op jit(solution)/shard_map/ppermute | solution.py:12
  87.1 1.5 %fusion.60 = bf16[192,1024]{1,0:T(8,128)(2,1)S(1)} fusion(bf16[1,1024,1664]{2,1,0:T(8,128)(2,1)S(1)} %copy-done.1, f32[192,1024]{1,0:T(8,128)S(1)} %get-tuple-element.81, bf16[192,3328]{1,0:T(8,128)(2,1)S(1)} %get-tuple-element.24), kind=kOutput, calls=%fused_computation.59 | convolution fusion | flops 656277504 | bytes 5226496 | tf_op jit(solution)/shard_map/dot_general | solution.py:80
  90.0 4.9 %convolution_bitcast_fusion.1 = f32[1,1664,1024]{2,1,0:T(8,128)} fusion(bf16[768,3328]{1,0:T(8,128)(2,1)S(1)} %get-tuple-element.23, bf16[192,1024]{1,0:T(8,128)(2,1)S(1)} %fusion.60, bf16[192,1024]{1,0:T(8,128)(2,1)S(1)} %fusion.63, bf16[384,1024]{1,0:T(8,128)(2,1)S(1)} %fusion.35), kind=kOutput, calls=%fused_computation.1 | convolution fusion | flops 2621964288 | bytes 10944512 | tf_op jit(solution)/shard_map/dot_general | solution.py:112
  95.5 5.1 %convolution_bitcast_fusion = f32[1,1024,1664]{2,1,0:T(8,128)} fusion(bf16[768,3328]{1,0:T(8,128)(2,1)S(1)} %get-tuple-element.23, bf16[192,1024]{1,0:T(8,128)(2,1)S(1)} %get-tuple-element.80, bf16[192,1024]{1,0:T(8,128)(2,1)S(1)} %get-tuple-element.82, bf16[384,1024]{1,0:T(8,128)(2,1)S(1)} %get-tuple-element.84), kind=kOutput, calls=%fused_computation | convolution fusion | flops 2621964288 | bytes 10944512 | tf_op jit(solution)/shard_map/dot_general | solution.py:109
  101.5 2.2 %collective-permute-start.30 = (bf16[24,1664]{1,0:T(8,128)(2,1)S(1)}, bf16[24,1664]{1,0:T(8,128)(2,1)S(1)}, u32[]{:S(2)}, u32[]{:S(2)}) collective-permute-start(bf16[24,1664]{1,0:T(8,128)(2,1)S(1)} %get-tuple-element.69), channel_id=1, source_target_pairs={{0,24},{4,28},{8,16},{12,20},{16,8},{20,12},{24,0},{28,4},{1,25},{... | collective-permute-start | bytes 239624 | tf_op jit(solution)/shard_map/ppermute | solution.py:12
  104.6 2.8 %collective-permute-start.31 = (bf16[24,1664]{1,0:T(8,128)(2,1)S(1)}, bf16[24,1664]{1,0:T(8,128)(2,1)S(1)}, u32[]{:S(2)}, u32[]{:S(2)}) collective-permute-start(bf16[24,1664]{1,0:T(8,128)(2,1)S(1)} %get-tuple-element.68), channel_id=1, source_target_pairs={{0,28},{4,24},{8,20},{12,16},{16,12},{20,8},{24,4},{28,0},{1,29},{... | collective-permute-start | bytes 239624 | tf_op jit(solution)/shard_map/ppermute | solution.py:12
  107.9 3.8 %collective-permute-done.31 = bf16[24,1664]{1,0:T(8,128)(2,1)S(1)} collective-permute-done((bf16[24,1664]{1,0:T(8,128)(2,1)S(1)}, bf16[24,1664]{1,0:T(8,128)(2,1)S(1)}, u32[]{:S(2)}, u32[]{:S(2)}) %collective-permute-start.31) | collective-permute-done | bytes 79904 | tf_op jit(solution)/shard_map/ppermute | solution.py:12
  (109 shorter events, 20.6 us)
Async XLA Ops:
  6.3 19.1 %collective-permute-start.3 = (bf16[24,3328]{1,0:T(8,128)(2,1)S(1)}, bf16[24,3328]{1,0:T(8,128)(2,1)S(1)}, u32[]{:S(2)}, u32[]{:S(2)}) collective-permute-start(bf16[24,3328]{1,0:T(8,128)(2,1)S(1)} %get-tuple-element.15), channel_id=1, source_target_pairs={{0,2},{1,3},{2,0},{3,1},{4,6},{5,7},{6,4},{7,5},{8,10},{9,11},{10,... | collective-permute-start | bytes 479240 | tf_op jit(solution)/shard_map/ppermute | solution.py:12
  9.3 28.2 %collective-permute-start.5 = (bf16[24,3328]{1,0:T(8,128)(2,1)S(1)}, bf16[24,3328]{1,0:T(8,128)(2,1)S(1)}, u32[]{:S(2)}, u32[]{:S(2)}) collective-permute-start(bf16[24,3328]{1,0:T(8,128)(2,1)S(1)} %get-tuple-element.15), channel_id=1, source_target_pairs={{0,1},{1,0},{2,3},{3,2},{4,5},{5,4},{6,7},{7,6},{8,9},{9,8},{10,11... | collective-permute-start | bytes 479240 | tf_op jit(solution)/shard_map/ppermute | solution.py:12
  9.3 6.5 %collective-permute-start = (bf16[24,3328]{1,0:T(8,128)(2,1)S(1)}, bf16[24,3328]{1,0:T(8,128)(2,1)S(1)}, u32[]{:S(2)}, u32[]{:S(2)}) collective-permute-start(bf16[24,3328]{1,0:T(8,128)(2,1)S(1)} %get-tuple-element.13), channel_id=1, source_target_pairs={{0,4},{4,0},{8,12},{12,8},{16,20},{20,16},{24,28},{28,24},{1,5},{5... | collective-permute-start | bytes 479240 | tf_op jit(solution)/shard_map/ppermute | solution.py:12
  10.8 13.9 %collective-permute-start.1 = (bf16[24,3328]{1,0:T(8,128)(2,1)S(1)}, bf16[24,3328]{1,0:T(8,128)(2,1)S(1)}, u32[]{:S(2)}, u32[]{:S(2)}) collective-permute-start(bf16[24,3328]{1,0:T(8,128)(2,1)S(1)} %get-tuple-element.12), channel_id=1, source_target_pairs={{0,8},{4,12},{8,0},{12,4},{16,24},{20,28},{24,16},{28,20},{1,9},{5... | collective-permute-start | bytes 479240 | tf_op jit(solution)/shard_map/ppermute | solution.py:12
  12.4 10.1 %collective-permute-start.2 = (bf16[24,3328]{1,0:T(8,128)(2,1)S(1)}, bf16[24,3328]{1,0:T(8,128)(2,1)S(1)}, u32[]{:S(2)}, u32[]{:S(2)}) collective-permute-start(bf16[24,3328]{1,0:T(8,128)(2,1)S(1)} %get-tuple-element.11), channel_id=1, source_target_pairs={{0,12},{4,8},{8,4},{12,0},{16,28},{20,24},{24,20},{28,16},{1,13},{... | collective-permute-start | bytes 479240 | tf_op jit(solution)/shard_map/ppermute | solution.py:12
  15.8 26.9 %collective-permute-start.14 = (bf16[24,3328]{1,0:T(8,128)(2,1)S(1)}, bf16[24,3328]{1,0:T(8,128)(2,1)S(1)}, u32[]{:S(2)}, u32[]{:S(2)}) collective-permute-start(bf16[24,3328]{1,0:T(8,128)(2,1)S(1)} %get-tuple-element.16), channel_id=1, source_target_pairs={{0,16},{4,20},{8,24},{12,28},{16,0},{20,4},{24,8},{28,12},{1,17},{... | collective-permute-start | bytes 479240 | tf_op jit(solution)/shard_map/ppermute | solution.py:12
  22.5 20.2 %collective-permute-start.15 = (bf16[24,3328]{1,0:T(8,128)(2,1)S(1)}, bf16[24,3328]{1,0:T(8,128)(2,1)S(1)}, u32[]{:S(2)}, u32[]{:S(2)}) collective-permute-start(bf16[24,3328]{1,0:T(8,128)(2,1)S(1)} %get-tuple-element.10), channel_id=1, source_target_pairs={{0,20},{4,16},{8,28},{12,24},{16,4},{20,0},{24,12},{28,8},{1,21},{... | collective-permute-start | bytes 479240 | tf_op jit(solution)/shard_map/ppermute | solution.py:12
  24.8 11.4 %collective-permute-start.4 = (bf16[72,3328]{1,0:T(8,128)(2,1)S(1)}, bf16[72,3328]{1,0:T(8,128)(2,1)S(1)}, u32[]{:S(2)}, u32[]{:S(2)}) collective-permute-start(bf16[72,3328]{1,0:T(8,128)(2,1)S(1)} %get-tuple-element.61), channel_id=1, source_target_pairs={{0,2},{1,3},{2,0},{3,1},{4,6},{5,7},{6,4},{7,5},{8,10},{9,11},{10,... | collective-permute-start | bytes 1437704 | tf_op jit(solution)/shard_map/ppermute | solution.py:12
  25.4 12.3 %collective-permute-start.6 = (bf16[72,3328]{1,0:T(8,128)(2,1)S(1)}, bf16[72,3328]{1,0:T(8,128)(2,1)S(1)}, u32[]{:S(2)}, u32[]{:S(2)}) collective-permute-start(bf16[72,3328]{1,0:T(8,128)(2,1)S(1)} %get-tuple-element.61), channel_id=1, source_target_pairs={{0,1},{1,0},{2,3},{3,2},{4,5},{5,4},{6,7},{7,6},{8,9},{9,8},{10,11... | collective-permute-start | bytes 1437704 | tf_op jit(solution)/shard_map/ppermute | solution.py:12
  36.1 17.7 %collective-permute-start.23 = (bf16[24,3328]{1,0:T(8,128)(2,1)S(1)}, bf16[24,3328]{1,0:T(8,128)(2,1)S(1)}, u32[]{:S(2)}, u32[]{:S(2)}) collective-permute-start(bf16[24,3328]{1,0:T(8,128)(2,1)S(1)} %get-tuple-element.36), channel_id=1, source_target_pairs={{0,24},{4,28},{8,16},{12,20},{16,8},{20,12},{24,0},{28,4},{1,25},{... | collective-permute-start | bytes 479240 | tf_op jit(solution)/shard_map/ppermute | solution.py:12
  37.6 1.5 %collective-permute-start.7 = (bf16[24,3328]{1,0:T(8,128)(2,1)S(1)}, bf16[24,3328]{1,0:T(8,128)(2,1)S(1)}, u32[]{:S(2)}, u32[]{:S(2)}) collective-permute-start(bf16[24,3328]{1,0:T(8,128)(2,1)S(1)} %collective-permute-done.3), channel_id=1, source_target_pairs={{0,1},{1,0},{2,3},{3,2},{4,5},{5,4},{6,7},{7,6},{8,9},{9,8},{10,11... | collective-permute-start | bytes 479240 | tf_op jit(solution)/shard_map/ppermute | solution.py:12
  37.7 4.9 %collective-permute-start.8 = (bf16[72,3328]{1,0:T(8,128)(2,1)S(1)}, bf16[72,3328]{1,0:T(8,128)(2,1)S(1)}, u32[]{:S(2)}, u32[]{:S(2)}) collective-permute-start(bf16[72,3328]{1,0:T(8,128)(2,1)S(1)} %collective-permute-done.4), channel_id=1, source_target_pairs={{0,1},{1,0},{2,3},{3,2},{4,5},{5,4},{6,7},{7,6},{8,9},{9,8},{10,11... | collective-permute-start | bytes 1437704 | tf_op jit(solution)/shard_map/ppermute | solution.py:12
  39.0 14.9 %collective-permute-start.24 = (bf16[24,3328]{1,0:T(8,128)(2,1)S(1)}, bf16[24,3328]{1,0:T(8,128)(2,1)S(1)}, u32[]{:S(2)}, u32[]{:S(2)}) collective-permute-start(bf16[24,3328]{1,0:T(8,128)(2,1)S(1)} %get-tuple-element.35), channel_id=1, source_target_pairs={{0,28},{4,24},{8,20},{12,16},{16,12},{20,8},{24,4},{28,0},{1,29},{... | collective-permute-start | bytes 479240 | tf_op jit(solution)/shard_map/ppermute | solution.py:12
  42.8 9.4 %collective-permute-start.16 = (bf16[48,3328]{1,0:T(8,128)(2,1)S(1)}, bf16[48,3328]{1,0:T(8,128)(2,1)S(1)}, u32[]{:S(2)}, u32[]{:S(2)}) collective-permute-start(bf16[48,3328]{1,0:T(8,128)(2,1)S(1)} %get-tuple-element.49), channel_id=1, source_target_pairs={{0,2},{1,3},{2,0},{3,1},{4,6},{5,7},{6,4},{7,5},{8,10},{9,11},{10,... | collective-permute-start | bytes 958472 | tf_op jit(solution)/shard_map/ppermute | solution.py:12
  43.4 8.8 %collective-permute-start.17 = (bf16[48,3328]{1,0:T(8,128)(2,1)S(1)}, bf16[48,3328]{1,0:T(8,128)(2,1)S(1)}, u32[]{:S(2)}, u32[]{:S(2)}) collective-permute-start(bf16[48,3328]{1,0:T(8,128)(2,1)S(1)} %get-tuple-element.49), channel_id=1, source_target_pairs={{0,1},{1,0},{2,3},{3,2},{4,5},{5,4},{6,7},{7,6},{8,9},{9,8},{10,11... | collective-permute-start | bytes 958472 | tf_op jit(solution)/shard_map/ppermute | solution.py:12
  49.0 9.9 %collective-permute-start.9 = (bf16[192,1664]{1,0:T(8,128)(2,1)S(1)}, bf16[192,1664]{1,0:T(8,128)(2,1)S(1)}, u32[]{:S(2)}, u32[]{:S(2)}) collective-permute-start(bf16[192,1664]{1,0:T(8,128)(2,1)S(1)} %slice.179), channel_id=1, source_target_pairs={{0,1},{1,0},{2,3},{3,2},{4,5},{5,4},{6,7},{7,6},{8,9},{9,8},{10,11... | collective-permute-start | bytes 1916936 | tf_op jit(solution)/shard_map/ppermute | solution.py:12
  52.2 1.6 %collective-permute-start.18 = (bf16[48,3328]{1,0:T(8,128)(2,1)S(1)}, bf16[48,3328]{1,0:T(8,128)(2,1)S(1)}, u32[]{:S(2)}, u32[]{:S(2)}) collective-permute-start(bf16[48,3328]{1,0:T(8,128)(2,1)S(1)} %collective-permute-done.16), channel_id=1, source_target_pairs={{0,1},{1,0},{2,3},{3,2},{4,5},{5,4},{6,7},{7,6},{8,9},{9,8},{10,11... | collective-permute-start | bytes 958472 | tf_op jit(solution)/shard_map/ppermute | solution.py:12
  54.0 18.9 %collective-permute-start.25 = (bf16[48,3328]{1,0:T(8,128)(2,1)S(1)}, bf16[48,3328]{1,0:T(8,128)(2,1)S(1)}, u32[]{:S(2)}, u32[]{:S(2)}) collective-permute-start(bf16[48,3328]{1,0:T(8,128)(2,1)S(1)} %get-tuple-element.43), channel_id=1, source_target_pairs={{0,2},{1,3},{2,0},{3,1},{4,6},{5,7},{6,4},{7,5},{8,10},{9,11},{10,... | collective-permute-start | bytes 958472 | tf_op jit(solution)/shard_map/ppermute | solution.py:12
  54.6 20.4 %collective-permute-start.26 = (bf16[48,3328]{1,0:T(8,128)(2,1)S(1)}, bf16[48,3328]{1,0:T(8,128)(2,1)S(1)}, u32[]{:S(2)}, u32[]{:S(2)}) collective-permute-start(bf16[48,3328]{1,0:T(8,128)(2,1)S(1)} %get-tuple-element.43), channel_id=1, source_target_pairs={{0,1},{1,0},{2,3},{3,2},{4,5},{5,4},{6,7},{7,6},{8,9},{9,8},{10,11... | collective-permute-start | bytes 958472 | tf_op jit(solution)/shard_map/ppermute | solution.py:12
  58.3 2.3 %collective-permute-start.19 = (bf16[96,1664]{1,0:T(8,128)(2,1)S(1)}, bf16[96,1664]{1,0:T(8,128)(2,1)S(1)}, u32[]{:S(2)}, u32[]{:S(2)}) collective-permute-start(bf16[96,1664]{1,0:T(8,128)(2,1)S(1)} %slice.191), channel_id=1, source_target_pairs={{0,1},{1,0},{2,3},{3,2},{4,5},{5,4},{6,7},{7,6},{8,9},{9,8},{10,11... | collective-permute-start | bytes 958472 | tf_op jit(solution)/shard_map/ppermute | solution.py:12
  59.0 12.2 %collective-permute-start.10 = (bf16[96,1664]{1,0:T(8,128)(2,1)S(1)}, bf16[96,1664]{1,0:T(8,128)(2,1)S(1)}, u32[]{:S(2)}, u32[]{:S(2)}) collective-permute-start(bf16[96,1664]{1,0:T(8,128)(2,1)S(1)} %slice.181), channel_id=1, source_target_pairs={{0,2},{1,3},{2,0},{3,1},{4,6},{5,7},{6,4},{7,5},{8,10},{9,11},{10,... | collective-permute-start | bytes 958472 | tf_op jit(solution)/shard_map/ppermute | solution.py:12
  60.7 15.6 %collective-permute-start.20 = (bf16[48,1664]{1,0:T(8,128)(2,1)S(1)}, bf16[48,1664]{1,0:T(8,128)(2,1)S(1)}, u32[]{:S(2)}, u32[]{:S(2)}) collective-permute-start(bf16[48,1664]{1,0:T(8,128)(2,1)S(1)} %slice.193), channel_id=1, source_target_pairs={{0,2},{1,3},{2,0},{3,1},{4,6},{5,7},{6,4},{7,5},{8,10},{9,11},{10,... | collective-permute-start | bytes 479240 | tf_op jit(solution)/shard_map/ppermute | solution.py:12
  71.4 4.9 %collective-permute-start.11 = (bf16[24,1664]{1,0:T(8,128)(2,1)S(1)}, bf16[24,1664]{1,0:T(8,128)(2,1)S(1)}, u32[]{:S(2)}, u32[]{:S(2)}) collective-permute-start(bf16[24,1664]{1,0:T(8,128)(2,1)S(1)} %get-tuple-element.39), channel_id=1, source_target_pairs={{0,4},{4,0},{8,12},{12,8},{16,20},{20,16},{24,28},{28,24},{1,5},{5... | collective-permute-start | bytes 239624 | tf_op jit(solution)/shard_map/ppermute | solution.py:12
  71.8 4.5 %collective-permute-start.12 = (bf16[24,1664]{1,0:T(8,128)(2,1)S(1)}, bf16[24,1664]{1,0:T(8,128)(2,1)S(1)}, u32[]{:S(2)}, u32[]{:S(2)}) collective-permute-start(bf16[24,1664]{1,0:T(8,128)(2,1)S(1)} %get-tuple-element.38), channel_id=1, source_target_pairs={{0,8},{4,12},{8,0},{12,4},{16,24},{20,28},{24,16},{28,20},{1,9},{5... | collective-permute-start | bytes 239624 | tf_op jit(solution)/shard_map/ppermute | solution.py:12
  72.9 5.4 %collective-permute-start.13 = (bf16[24,1664]{1,0:T(8,128)(2,1)S(1)}, bf16[24,1664]{1,0:T(8,128)(2,1)S(1)}, u32[]{:S(2)}, u32[]{:S(2)}) collective-permute-start(bf16[24,1664]{1,0:T(8,128)(2,1)S(1)} %get-tuple-element.37), channel_id=1, source_target_pairs={{0,12},{4,8},{8,4},{12,0},{16,28},{20,24},{24,20},{28,16},{1,13},{... | collective-permute-start | bytes 239624 | tf_op jit(solution)/shard_map/ppermute | solution.py:12
  75.0 11.0 %collective-permute-start.27 = (bf16[48,3328]{1,0:T(8,128)(2,1)S(1)}, bf16[48,3328]{1,0:T(8,128)(2,1)S(1)}, u32[]{:S(2)}, u32[]{:S(2)}) collective-permute-start(bf16[48,3328]{1,0:T(8,128)(2,1)S(1)} %collective-permute-done.25), channel_id=1, source_target_pairs={{0,1},{1,0},{2,3},{3,2},{4,5},{5,4},{6,7},{7,6},{8,9},{9,8},{10,11... | collective-permute-start | bytes 958472 | tf_op jit(solution)/shard_map/ppermute | solution.py:12
  76.4 7.3 %collective-permute-start.21 = (bf16[24,1664]{1,0:T(8,128)(2,1)S(1)}, bf16[24,1664]{1,0:T(8,128)(2,1)S(1)}, u32[]{:S(2)}, u32[]{:S(2)}) collective-permute-start(bf16[24,1664]{1,0:T(8,128)(2,1)S(1)} %get-tuple-element.71), channel_id=1, source_target_pairs={{0,16},{4,20},{8,24},{12,28},{16,0},{20,4},{24,8},{28,12},{1,17},{... | collective-permute-start | bytes 239624 | tf_op jit(solution)/shard_map/ppermute | solution.py:12
  78.3 7.6 %collective-permute-start.22 = (bf16[24,1664]{1,0:T(8,128)(2,1)S(1)}, bf16[24,1664]{1,0:T(8,128)(2,1)S(1)}, u32[]{:S(2)}, u32[]{:S(2)}) collective-permute-start(bf16[24,1664]{1,0:T(8,128)(2,1)S(1)} %get-tuple-element.70), channel_id=1, source_target_pairs={{0,20},{4,16},{8,28},{12,24},{16,4},{20,0},{24,12},{28,8},{1,21},{... | collective-permute-start | bytes 239624 | tf_op jit(solution)/shard_map/ppermute | solution.py:12
  89.9 4.9 %collective-permute-start.28 = (bf16[96,1664]{1,0:T(8,128)(2,1)S(1)}, bf16[96,1664]{1,0:T(8,128)(2,1)S(1)}, u32[]{:S(2)}, u32[]{:S(2)}) collective-permute-start(bf16[96,1664]{1,0:T(8,128)(2,1)S(1)} %slice.199), channel_id=1, source_target_pairs={{0,1},{1,0},{2,3},{3,2},{4,5},{5,4},{6,7},{7,6},{8,9},{9,8},{10,11... | collective-permute-start | bytes 958472 | tf_op jit(solution)/shard_map/ppermute | solution.py:12
  94.9 6.6 %collective-permute-start.29 = (bf16[48,1664]{1,0:T(8,128)(2,1)S(1)}, bf16[48,1664]{1,0:T(8,128)(2,1)S(1)}, u32[]{:S(2)}, u32[]{:S(2)}) collective-permute-start(bf16[48,1664]{1,0:T(8,128)(2,1)S(1)} %slice.201), channel_id=1, source_target_pairs={{0,2},{1,3},{2,0},{3,1},{4,6},{5,7},{6,4},{7,5},{8,10},{9,11},{10,... | collective-permute-start | bytes 479240 | tf_op jit(solution)/shard_map/ppermute | solution.py:12
  101.5 6.3 %collective-permute-start.30 = (bf16[24,1664]{1,0:T(8,128)(2,1)S(1)}, bf16[24,1664]{1,0:T(8,128)(2,1)S(1)}, u32[]{:S(2)}, u32[]{:S(2)}) collective-permute-start(bf16[24,1664]{1,0:T(8,128)(2,1)S(1)} %get-tuple-element.69), channel_id=1, source_target_pairs={{0,24},{4,28},{8,16},{12,20},{16,8},{20,12},{24,0},{28,4},{1,25},{... | collective-permute-start | bytes 239624 | tf_op jit(solution)/shard_map/ppermute | solution.py:12
  104.6 7.1 %collective-permute-start.31 = (bf16[24,1664]{1,0:T(8,128)(2,1)S(1)}, bf16[24,1664]{1,0:T(8,128)(2,1)S(1)}, u32[]{:S(2)}, u32[]{:S(2)}) collective-permute-start(bf16[24,1664]{1,0:T(8,128)(2,1)S(1)} %get-tuple-element.68), channel_id=1, source_target_pairs={{0,28},{4,24},{8,20},{12,16},{16,12},{20,8},{24,4},{28,0},{1,29},{... | collective-permute-start | bytes 239624 | tf_op jit(solution)/shard_map/ppermute | solution.py:12
  (3 other events, 50.6 us)

commit v2 on v1

v2 whole, which is shorter than its diff:
```python
import functools

import jax
import jax.numpy as jnp
from jax import lax
from jax.experimental import pallas as pl
from jax.experimental.pallas import tpu as pltpu
from jax.sharding import PartitionSpec as P

inv_root_two = 0.7071067811865476
inv_root_two_pi = 0.3989422804014327


def swap(value, axis, mask):
    size = lax.axis_size(axis)
    return lax.ppermute(value, axis, [(i, i ^ mask) for i in range(size)])


def joined(pieces):
    return pieces[0] if len(pieces) == 1 else jnp.concatenate(pieces, axis=0)


def after(value, *needed):
    return lax.optimization_barrier((value,) + needed)[0]


def dispatch_kernel(capacity, me, tokens, out_grad, index, slots, weights, rows, chosen, *scratch):
    held, sems = scratch[:-1], scratch[-1]
    copies = [
        pltpu.make_async_copy(source, target, sems.at[i])
        for i, (source, target) in enumerate(zip((index, slots, weights, tokens, out_grad), held))
    ]
    for copy in copies:
        copy.start()
    index_held, slots_held, weights_held, tokens_held, grad_held = held
    count, tok_count = chosen.shape
    width = tokens.shape[1]
    row = lax.broadcasted_iota(jnp.int32, (count, tok_count), 0)
    step = ((row.astype(jnp.float32) + 0.5) * (1.0 / capacity)).astype(jnp.int32)
    slot = row - step * capacity
    expert = step ^ me[0]
    for copy in copies[:3]:
        copy.wait()
    taken = [
        (index_held[k : k + 1, :] == expert) & (slots_held[k : k + 1, :] == slot) for k in range(2)
    ]
    weight = weights_held[...].astype(jnp.float32)
    scale = sum(jnp.where(taken[k], weight[k : k + 1, :], 0.0) for k in range(2))
    scale = jnp.sum(scale, axis=1, keepdims=True)
    one_hot = jnp.where(taken[0] | taken[1], 1.0, 0.0).astype(jnp.bfloat16)
    chosen[...] = one_hot
    copies[3].wait()
    picked = jnp.dot(one_hot, tokens_held[...], preferred_element_type=jnp.float32)
    rows[:, :width] = picked.astype(jnp.bfloat16)
    copies[4].wait()
    picked = jnp.dot(one_hot, grad_held[...], preferred_element_type=jnp.float32)
    rows[:, width:] = (picked * scale).astype(jnp.bfloat16)


def dispatch_call(capacity, me, tokens, out_grad, index, slots, weights):
    tok_count, width = tokens.shape
    count = lax.axis_size("expert") * capacity
    arrays = (index, slots, weights, tokens, out_grad)
    in_vmem = pl.BlockSpec(memory_space=pltpu.VMEM)
    return pl.pallas_call(
        functools.partial(dispatch_kernel, capacity),
        out_shape=[
            jax.ShapeDtypeStruct((count, 2 * width), jnp.bfloat16),
            jax.ShapeDtypeStruct((count, tok_count), jnp.bfloat16),
        ],
        in_specs=[pl.BlockSpec(memory_space=pltpu.SMEM)] + [pl.BlockSpec(memory_space=pltpu.HBM)] * 5,
        out_specs=[in_vmem] * 2,
        scratch_shapes=[pltpu.VMEM(x.shape, x.dtype) for x in arrays]
        + [pltpu.SemaphoreType.DMA((5,))],
        compiler_params=pltpu.CompilerParams(vmem_limit_bytes=16 << 20),
        cost_estimate=pl.CostEstimate(flops=0, bytes_accessed=0, transcendentals=0),
    )(me, tokens, out_grad, index, slots, weights)


contract_last = (((1,), (1,)), ((), ()))


def chunk_kernel(step, rows, w_in, bias, w_out, hidden, d_pre, kept, leaving, total):
    width, units = w_in.shape
    half = kept.shape[0]
    ones = jnp.ones((8, rows.shape[0]), jnp.bfloat16)
    for j in range(0, units, step):
        part = slice(j, j + step)
        pre_act = jnp.dot(rows[:, :width], w_in[:, part], preferred_element_type=jnp.float32)
        pre_act = pre_act + bias[:, part]
        d_hidden = lax.dot_general(
            rows[:, width:], w_out[part, :], contract_last, preferred_element_type=jnp.float32
        )
        cdf = 0.5 * (1.0 + lax.erf(pre_act * inv_root_two))
        hidden[:, part] = (pre_act * cdf).astype(jnp.bfloat16)
        density = jnp.exp(-0.5 * pre_act * pre_act) * inv_root_two_pi
        d_pre[:, part] = (d_hidden * (cdf + pre_act * density)).astype(jnp.bfloat16)
        total[:, part] = jnp.dot(ones, d_pre[:, part], preferred_element_type=jnp.float32)
    term = lax.dot_general(
        d_pre[...], w_in[...], contract_last, preferred_element_type=jnp.float32
    ).astype(jnp.bfloat16)
    kept[...] = term[:half]
    leaving[...] = term[half:]


def chunk_call(rows, w_in, bias, w_out):
    count = rows.shape[0]
    width, units = w_in.shape
    in_vmem = pl.BlockSpec(memory_space=pltpu.VMEM)
    shapes = [(count, units), (count, units), (count // 2, width), (count // 2, width)]
    return pl.pallas_call(
        functools.partial(chunk_kernel, min(512, units)),
        out_shape=[jax.ShapeDtypeStruct(shape, jnp.bfloat16) for shape in shapes]
        + [jax.ShapeDtypeStruct((8, units), jnp.float32)],
        in_specs=[in_vmem] * 4,
        out_specs=[in_vmem] * 5,
        compiler_params=pltpu.CompilerParams(vmem_limit_bytes=24 << 20),
        cost_estimate=pl.CostEstimate(flops=0, bytes_accessed=0, transcendentals=0),
    )(rows, w_in, bias, w_out)


def on_device(tokens, out_grad, expert_index, slots, combine, w_in, b_in, w_out):
    experts = lax.axis_size("expert")
    tok_count, width = tokens.shape
    capacity = max(2, (3 * tok_count + 2 * experts - 1) // (2 * experts))
    me = lax.axis_index("expert")
    first_w, second_w = w_in[0], w_out[0]

    rows, chosen = dispatch_call(
        capacity, me.reshape(1), tokens, out_grad, expert_index.T, slots.T, combine.T
    )

    def block(k):
        return rows[k * capacity : (k + 1) * capacity]

    across_masks = [2 << i for i in range(lax.axis_size("dp").bit_length() - 2)]
    half, quarter = experts // 2, experts // 4
    def spread(value):
        pieces = [value]
        for mask in across_masks:
            pieces = pieces + [swap(piece, "dp", mask) for piece in pieces]
        return pieces

    near, far_one, far_two = range(half), range(half, half + quarter), range(half + quarter, experts)
    got = {0: block(0)}
    for k in range(1, experts):
        got[k] = swap(block(k), "expert", k)
    groups = [near, far_one, far_two]
    runs = [[near], [far_one], [far_two]]
    sets = [[spread(joined([got[k] for k in run])) for run in part] for part in runs]
    columns = []
    for part in sets:
        columns.append(joined([run[i] for i in range(len(part[0])) for run in part]))

    made = []
    for column in columns:
        rows_all = jnp.concatenate([column, swap(column, "dp", 1)])
        made.append((rows_all,) + tuple(chunk_call(rows_all, first_w, b_in, second_w)))
    row_parts, hidden_parts, slope_parts = [[m[i] for m in made] for i in range(3)]

    def first_sum(kept, leaving):
        return (kept.astype(jnp.float32) + swap(leaving, "dp", 1).astype(jnp.float32)).astype(jnp.bfloat16)

    def rest_sum(term, *needed):
        for mask in across_masks[::-1]:
            middle = term.shape[0] // 2
            arrived = swap(term[middle:], "dp", mask)
            if needed:
                arrived = after(arrived, *needed)
            term = (term[:middle].astype(jnp.float32) + arrived.astype(jnp.float32)).astype(jnp.bfloat16)
        return term

    sums = [first_sum(m[3], m[4]) for m in made]
    far_back = [rest_sum(sums[i], made[0][3]) for i in (1, 2)]
    hidden_parts[0] = after(hidden_parts[0], sums[0], far_back[0])
    hidden = jnp.concatenate(hidden_parts)
    rows_all = jnp.concatenate(row_parts)
    grad_second = lax.dot_general(
        hidden, rows_all[:, width:], (((0,), (0,)), ((), ())), preferred_element_type=jnp.float32
    )
    near_back = rest_sum(sums[0], grad_second)
    def part(value, i):
        return value[i * capacity : (i + 1) * capacity]

    returned = {}
    for group, value in zip((far_one, far_two), far_back):
        for i, k in enumerate(group):
            leaving = part(value, i)
            if k in far_one or k in far_two:
                leaving = after(leaving, sums[0])
            returned[k] = swap(leaving, "expert", k)
    slope_parts[0] = after(slope_parts[0], near_back, *[returned[k] for k in far_one])
    d_pre = jnp.concatenate(slope_parts)
    grad_first = lax.dot_general(
        rows_all[:, :width], d_pre, (((0,), (0,)), ((), ())), preferred_element_type=jnp.float32
    )

    returned[0] = part(near_back, 0)
    for k in range(1, half):
        leaving = part(near_back, k)
        if k > 1:
            leaving = after(leaving, returned[half + (k - 2) % quarter])
        returned[k] = swap(leaving, "expert", k)
    returned = jnp.concatenate([returned[k] for k in range(experts)])
    d_tokens = lax.dot_general(
        chosen, returned, (((0,), (0,)), ((), ())), preferred_element_type=jnp.float32
    )
    grad_bias = sum(m[5][:1] for m in made)
    return (d_tokens.astype(jnp.bfloat16), grad_first[None], grad_second[None], grad_bias)


def solution(mesh):
    in_specs = (
        P(("expert", "dp"), None),
        P(("expert", "dp"), None),
        P(("expert", "dp"), None),
        P(("expert", "dp"), None),
        P(("expert", "dp"), None),
        P("expert", None, "dp"),
        P("expert", "dp"),
        P("expert", "dp", None),
    )
    out_specs = (
        P(("expert", "dp"), None),
        P("expert", None, "dp"),
        P("expert", "dp", None),
        P("expert", "dp"),
    )
    return jax.shard_map(
        on_device, mesh=mesh, in_specs=in_specs, out_specs=out_specs, check_vma=False
    )
```

time: 113 us -> 97.4 us (0.86)
  matrix products: 26.5 us -> 11 us
  waiting for transfers between devices: 43.8 us -> 30.4 us
  Pallas kernels: 0 us -> 12.7 us
  local copies, waits for them, and re-layouts: 3.04 us -> 6.1 us
  starting transfers between devices: 35.8 us -> 34.5 us
    dot_general x11 -> x0, matrix products: 15.4 us -> none  [the longest x3 4.7 us: on_device(): lax.dot_general(g, second_w, (((1,), (1,)), ((), ())), preferred_element_...]
    ppermute x32 -> x26, waiting for transfers between devices: 43.8 us -> 30.4 us  [swap(): return lax.ppermute(value, axis, [(i, i ^ mask) for i in range(size)])]
    pallas_call x0 -> x4, Pallas kernels: none -> 12.7 us  [the longest x3 11.4 us: chunk_call(): pl.pallas_call(functools.partial(chunk_kernel, min(512, units)), out_shap...]
    unnamed x31 -> x34, local copies, waits for them, and re-layouts: 0.94 us -> 5.82 us
    eq x2 -> x0, local copies, waits for them, and re-layouts: 1.74 us -> none  [the longest x1 0.89 us: picks(): expert_index[None, None, :, k] == expert_ids]
    ppermute x32 -> x26, starting transfers between devices: 35.8 us -> 34.5 us  [swap(): return lax.ppermute(value, axis, [(i, i ^ mask) for i in range(size)])]
  transfers between devices with their start and end apart: 32 -> 26, of which waited for: 13 -> 6; matrix products, arithmetic and copies ran while one was open for 19% -> 12% of each run, Pallas kernels for 0% -> 12%
where the time goes in v2:
time: 97.4 us; the launch traced here: 97.2 us
  starting transfers between devices  34.5 us (35%)
  waiting for transfers between devices  30.4 us (31%)
  Pallas kernels  12.7 us (13%)
  matrix products  11 us (11%)
  local copies, waits for them, and re-layouts  6.1 us (6%)
  other arithmetic  1.45 us (1%)
  between operations  1.03 us (1%)
    ppermute x26, starting transfers between devices, swap(): return lax.ppermute(value, axis, [(i, i ^ mask) for i in range(size)])  34.5 us
    ppermute x26, waiting for transfers between devices, swap(): return lax.ppermute(value, axis, [(i, i ^ mask) for i in range(size)])  30.4 us
    pallas_call x3, Pallas kernels, chunk_call(): pl.pallas_call(functools.partial(chunk_kernel, min(512, units)), out_shap...  11.4 us
    unnamed x34, local copies, waits for them, and re-layouts  5.82 us
    dot_general x1, matrix products, on_device(): lax.dot_general(hidden, rows_all[:, width:], (((0,), (0,)), ((), ())), pr...  5.1 us
    dot_general x1, matrix products, on_device(): lax.dot_general(rows_all[:, :width], d_pre, (((0,), (0,)), ((), ())), pre...  4.82 us
  transfers between devices with their start and end apart: 26, of which 6 were waited for; matrix products, arithmetic and copies ran while one was open for 12% of the time, Pallas kernels for 12%

profile of v2, /device:TPU:0, one launch (start us, length us, event | category | flops | bytes accessed | tf_op | source)
XLA Modules:
  0.0 97.2 jit_solution(16013828662084361915)
XLA Ops:
  0.6 1.0 %copy-done.2 = bf16[128,1664]{1,0:T(8,128)(2,1)S(1)} copy-done((bf16[128,1664]{1,0:T(8,128)(2,1)S(1)}, bf16[128,1664]{1,0:T(8,128)(2,1)}, u32[]{:S(2)}) %copy-start.2) | copy-done | bytes 426008
  1.6 1.0 %copy-done.3 = bf16[128,1664]{1,0:T(8,128)(2,1)S(1)} copy-done((bf16[128,1664]{1,0:T(8,128)(2,1)S(1)}, bf16[128,1664]{1,0:T(8,128)(2,1)}, u32[]{:S(2)}) %copy-start.3) | copy-done | bytes 426008
  2.7 0.7 copy-done.5
  4.7 1.3 %shard_map.111 = (bf16[192,3328]{1,0:T(8,128)(2,1)S(1)}, bf16[192,128]{1,0:T(8,128)(2,1)S(1)}) custom-call(s32[1]{0:T(128)} %bitcast.me, bf16[128,1664]{1,0:T(8,128)(2,1)S(1)} %copy-done.2, bf16[128,1664]{1,0:T(8,128)(2,1)S(1)} %copy-done.3, s32[2,128]{1,0:T(2,128)S(1)} %bitcast.17, s32[2,128]{1,0:T(2,128)S(1)} %bitcast.18, bf16[2,128]{1,0:T(2,128)(2,1)S(1)} %bitcast.19), custom_call_target="tpu_custom_call" | custom-call | tf_op jit(solution)/shard_map/pallas_call | solution.py:65
  6.1 3.0 %collective-permute-start = (bf16[24,3328]{1,0:T(8,128)(2,1)S(1)}, bf16[24,3328]{1,0:T(8,128)(2,1)S(1)}, u32[]{:S(2)}, u32[]{:S(2)}) collective-permute-start(bf16[24,3328]{1,0:T(8,128)(2,1)S(1)} %get-tuple-element.69), channel_id=1, source_target_pairs={{0,4},{4,0},{8,12},{12,8},{16,20},{20,16},{24,28},{28,24},{1,5},{5... | collective-permute-start | bytes 479240 | tf_op jit(solution)/shard_map/ppermute | solution.py:16
  9.1 1.6 %collective-permute-start.1 = (bf16[24,3328]{1,0:T(8,128)(2,1)S(1)}, bf16[24,3328]{1,0:T(8,128)(2,1)S(1)}, u32[]{:S(2)}, u32[]{:S(2)}) collective-permute-start(bf16[24,3328]{1,0:T(8,128)(2,1)S(1)} %get-tuple-element.68), channel_id=1, source_target_pairs={{0,8},{4,12},{8,0},{12,4},{16,24},{20,28},{24,16},{28,20},{1,9},{5... | collective-permute-start | bytes 479240 | tf_op jit(solution)/shard_map/ppermute | solution.py:16
  10.7 3.0 %collective-permute-start.7 = (bf16[24,3328]{1,0:T(8,128)(2,1)S(1)}, bf16[24,3328]{1,0:T(8,128)(2,1)S(1)}, u32[]{:S(2)}, u32[]{:S(2)}) collective-permute-start(bf16[24,3328]{1,0:T(8,128)(2,1)S(1)} %get-tuple-element.66), channel_id=1, source_target_pairs={{0,16},{4,20},{8,24},{12,28},{16,0},{20,4},{24,8},{28,12},{1,17},{... | collective-permute-start | bytes 479240 | tf_op jit(solution)/shard_map/ppermute | solution.py:16
  13.7 1.3 %collective-permute-start.8 = (bf16[24,3328]{1,0:T(8,128)(2,1)S(1)}, bf16[24,3328]{1,0:T(8,128)(2,1)S(1)}, u32[]{:S(2)}, u32[]{:S(2)}) collective-permute-start(bf16[24,3328]{1,0:T(8,128)(2,1)S(1)} %get-tuple-element.65), channel_id=1, source_target_pairs={{0,20},{4,16},{8,28},{12,24},{16,4},{20,0},{24,12},{28,8},{1,21},{... | collective-permute-start | bytes 479240 | tf_op jit(solution)/shard_map/ppermute | solution.py:16
  15.0 3.6 %collective-permute-start.13 = (bf16[24,3328]{1,0:T(8,128)(2,1)S(1)}, bf16[24,3328]{1,0:T(8,128)(2,1)S(1)}, u32[]{:S(2)}, u32[]{:S(2)}) collective-permute-start(bf16[24,3328]{1,0:T(8,128)(2,1)S(1)} %get-tuple-element.64), channel_id=1, source_target_pairs={{0,24},{4,28},{8,16},{12,20},{16,8},{20,12},{24,0},{28,4},{1,25},{... | collective-permute-start | bytes 479240 | tf_op jit(solution)/shard_map/ppermute | solution.py:16
  18.6 3.4 %collective-permute-done.1 = bf16[24,3328]{1,0:T(8,128)(2,1)S(1)} collective-permute-done((bf16[24,3328]{1,0:T(8,128)(2,1)S(1)}, bf16[24,3328]{1,0:T(8,128)(2,1)S(1)}, u32[]{:S(2)}, u32[]{:S(2)}) %collective-permute-start.1) | collective-permute-done | bytes 159776 | tf_op jit(solution)/shard_map/ppermute | solution.py:16
  22.0 1.1 %collective-permute-start.14 = (bf16[24,3328]{1,0:T(8,128)(2,1)S(1)}, bf16[24,3328]{1,0:T(8,128)(2,1)S(1)}, u32[]{:S(2)}, u32[]{:S(2)}) collective-permute-start(bf16[24,3328]{1,0:T(8,128)(2,1)S(1)} %get-tuple-element.60), channel_id=1, source_target_pairs={{0,28},{4,24},{8,20},{12,16},{16,12},{20,8},{24,4},{28,0},{1,29},{... | collective-permute-start | bytes 479240 | tf_op jit(solution)/shard_map/ppermute | solution.py:16
  23.4 1.7 %collective-permute-start.3 = (bf16[96,3328]{1,0:T(8,128)(2,1)S(1)}, bf16[96,3328]{1,0:T(8,128)(2,1)S(1)}, u32[]{:S(2)}, u32[]{:S(2)}) collective-permute-start(bf16[96,3328]{1,0:T(8,128)(2,1)S(1)} %pad_maximum_fusion.2), channel_id=1, source_target_pairs={{0,2},{1,3},{2,0},{3,1},{4,6},{5,7},{6,4},{7,5},{8,10},{9,11},{10,... | collective-permute-start | bytes 1916936 | tf_op jit(solution)/shard_map/ppermute | solution.py:16
  25.1 11.7 %collective-permute-done.8 = bf16[24,3328]{1,0:T(8,128)(2,1)S(1)} collective-permute-done((bf16[24,3328]{1,0:T(8,128)(2,1)S(1)}, bf16[24,3328]{1,0:T(8,128)(2,1)S(1)}, u32[]{:S(2)}, u32[]{:S(2)}) %collective-permute-start.8) | collective-permute-done | bytes 159776 | tf_op jit(solution)/shard_map/ppermute | solution.py:16
  36.8 1.6 %collective-permute-start.9 = (bf16[48,3328]{1,0:T(8,128)(2,1)S(1)}, bf16[48,3328]{1,0:T(8,128)(2,1)S(1)}, u32[]{:S(2)}, u32[]{:S(2)}) collective-permute-start(bf16[48,3328]{1,0:T(8,128)(2,1)S(1)} %pad_maximum_fusion.5), channel_id=1, source_target_pairs={{0,2},{1,3},{2,0},{3,1},{4,6},{5,7},{6,4},{7,5},{8,10},{9,11},{10,... | collective-permute-start | bytes 958472 | tf_op jit(solution)/shard_map/ppermute | solution.py:16
  39.1 8.4 %collective-permute-done.9 = bf16[48,3328]{1,0:T(8,128)(2,1)S(1)} collective-permute-done((bf16[48,3328]{1,0:T(8,128)(2,1)S(1)}, bf16[48,3328]{1,0:T(8,128)(2,1)S(1)}, u32[]{:S(2)}, u32[]{:S(2)}) %collective-permute-start.9) | collective-permute-done | bytes 319520 | tf_op jit(solution)/shard_map/ppermute | solution.py:16
  47.7 4.8 %collective-permute-done.15 = bf16[48,3328]{1,0:T(8,128)(2,1)S(1)} collective-permute-done((bf16[48,3328]{1,0:T(8,128)(2,1)S(1)}, bf16[48,3328]{1,0:T(8,128)(2,1)S(1)}, u32[]{:S(2)}, u32[]{:S(2)}) %collective-permute-start.15) | collective-permute-done | bytes 319520 | tf_op jit(solution)/shard_map/ppermute | solution.py:16
  53.5 1.2 %copy-done = bf16[1,1664,1024]{2,1,0:T(8,128)(2,1)S(1)} copy-done((bf16[1,1664,1024]{2,1,0:T(8,128)(2,1)S(1)}, bf16[1,1664,1024]{2,1,0:T(8,128)(2,1)}, u32[]{:S(2)}) %copy-start) | copy-done | bytes 3407896
  54.6 3.3 %shard_map.113 = (bf16[192,1024]{1,0:T(8,128)(2,1)S(1)}, bf16[192,1024]{1,0:T(8,128)(2,1)S(1)}, bf16[96,1664]{1,0:T(8,128)(2,1)S(1)}, bf16[96,1664]{1,0:T(8,128)(2,1)S(1)}, f32[8,1024]{1,0:T(8,128)S(1)}) custom-call(bf16[192,3328]{1,0:T(8,128)(2,1)S(1)} %pad_maximum_fusion.rows, bf16[1664,1024]{1,0:T(8,128)(2,1)S(1)} %bitcast.11, f32[1,1024]{1,0:T(1,128)S(1)} %copy-done.4, ...), custom_call_target="tpu_custom_call" | custom-call | tf_op jit(solution)/shard_map/pallas_call | solution.py:111
  58.6 3.3 %shard_map.114 = (bf16[192,1024]{1,0:T(8,128)(2,1)S(1)}, bf16[192,1024]{1,0:T(8,128)(2,1)S(1)}, bf16[96,1664]{1,0:T(8,128)(2,1)S(1)}, bf16[96,1664]{1,0:T(8,128)(2,1)S(1)}, f32[8,1024]{1,0:T(8,128)S(1)}) custom-call(bf16[192,3328]{1,0:T(8,128)(2,1)S(1)} %pad_maximum_fusion.1.rows, bf16[1664,1024]{1,0:T(8,128)(2,1)S(1)} %bitcast.12, f32[1,1024]{1,0:T(1,128)S(1)} %copy-done.4, ...), custom_call_target="tpu_custom_call" | custom-call | tf_op jit(solution)/shard_map/pallas_call | solution.py:111
  62.0 1.5 %collective-permute-start.12 = (bf16[48,1664]{1,0:T(8,128)(2,1)S(1)}, bf16[48,1664]{1,0:T(8,128)(2,1)S(1)}, u32[]{:S(2)}, u32[]{:S(2)}) collective-permute-start(bf16[48,1664]{1,0:T(8,128)(2,1)S(1)} %slice.111), channel_id=1, source_target_pairs={{0,2},{1,3},{2,0},{3,1},{4,6},{5,7},{6,4},{7,5},{8,10},{9,11},{10,... | collective-permute-start | bytes 479240 | tf_op jit(solution)/shard_map/ppermute | solution.py:16
  63.7 1.5 %collective-permute-start.23 = (bf16[48,1664]{1,0:T(8,128)(2,1)S(1)}, bf16[48,1664]{1,0:T(8,128)(2,1)S(1)}, u32[]{:S(2)}, u32[]{:S(2)}) collective-permute-start(bf16[48,1664]{1,0:T(8,128)(2,1)S(1)} %slice.120), channel_id=1, source_target_pairs={{0,2},{1,3},{2,0},{3,1},{4,6},{5,7},{6,4},{7,5},{8,10},{9,11},{10,... | collective-permute-start | bytes 479240 | tf_op jit(solution)/shard_map/ppermute | solution.py:16
  65.3 4.8 %shard_map.112 = (bf16[384,1024]{1,0:T(8,128)(2,1)S(1)}, bf16[384,1024]{1,0:T(8,128)(2,1)S(1)}, bf16[192,1664]{1,0:T(8,128)(2,1)S(1)}, bf16[192,1664]{1,0:T(8,128)(2,1)S(1)}, f32[8,1024]{1,0:T(8,128)S(1)}) custom-call(bf16[384,3328]{1,0:T(8,128)(2,1)S(1)} %get-tuple-element.72.rows, bf16[1664,1024]{1,0:T(8,128)(2,1)S(1)} %bitcast.13, ...), custom_call_target="tpu_custom_call" | custom-call | tf_op jit(solution)/shard_map/pallas_call | solution.py:111
  70.3 1.7 %collective-permute-done.23 = bf16[48,1664]{1,0:T(8,128)(2,1)S(1)} collective-permute-done((bf16[48,1664]{1,0:T(8,128)(2,1)S(1)}, bf16[48,1664]{1,0:T(8,128)(2,1)S(1)}, u32[]{:S(2)}, u32[]{:S(2)}) %collective-permute-start.23) | collective-permute-done | bytes 159776 | tf_op jit(solution)/shard_map/ppermute | solution.py:16
  73.2 1.5 %collective-permute-start.6 = (bf16[96,1664]{1,0:T(8,128)(2,1)S(1)}, bf16[96,1664]{1,0:T(8,128)(2,1)S(1)}, u32[]{:S(2)}, u32[]{:S(2)}) collective-permute-start(bf16[96,1664]{1,0:T(8,128)(2,1)S(1)} %slice.109), channel_id=1, source_target_pairs={{0,2},{1,3},{2,0},{3,1},{4,6},{5,7},{6,4},{7,5},{8,10},{9,11},{10,... | collective-permute-start | bytes 958472 | tf_op jit(solution)/shard_map/ppermute | solution.py:16
  75.1 3.6 %collective-permute-start.20 = (bf16[24,1664]{1,0:T(8,128)(2,1)S(1)}, bf16[24,1664]{1,0:T(8,128)(2,1)S(1)}, u32[]{:S(2)}, u32[]{:S(2)}) collective-permute-start(bf16[24,1664]{1,0:T(8,128)(2,1)S(1)} %get-tuple-element.46), channel_id=1, source_target_pairs={{0,20},{4,16},{8,28},{12,24},{16,4},{20,0},{24,12},{28,8},{1,21},{... | collective-permute-start | bytes 239624 | tf_op jit(solution)/shard_map/ppermute | solution.py:16
  78.7 2.2 %collective-permute-start.24 = (bf16[24,1664]{1,0:T(8,128)(2,1)S(1)}, bf16[24,1664]{1,0:T(8,128)(2,1)S(1)}, u32[]{:S(2)}, u32[]{:S(2)}) collective-permute-start(bf16[24,1664]{1,0:T(8,128)(2,1)S(1)} %get-tuple-element.51), channel_id=1, source_target_pairs={{0,24},{4,28},{8,16},{12,20},{16,8},{20,12},{24,0},{28,4},{1,25},{... | collective-permute-start | bytes 239624 | tf_op jit(solution)/shard_map/ppermute | solution.py:16
  80.9 1.5 %collective-permute-start.25 = (bf16[24,1664]{1,0:T(8,128)(2,1)S(1)}, bf16[24,1664]{1,0:T(8,128)(2,1)S(1)}, u32[]{:S(2)}, u32[]{:S(2)}) collective-permute-start(bf16[24,1664]{1,0:T(8,128)(2,1)S(1)} %get-tuple-element.52), channel_id=1, source_target_pairs={{0,28},{4,24},{8,20},{12,16},{16,12},{20,8},{24,4},{28,0},{1,29},{... | collective-permute-start | bytes 239624 | tf_op jit(solution)/shard_map/ppermute | solution.py:16
  82.3 5.1 %fusion.1 = f32[1024,1664]{1,0:T(8,128)} fusion(bf16[768,3328]{1,0:T(8,128)(2,1)S(1)} %constant_dynamic-update-slice_fusion.11, bf16[192,1024]{1,0:T(8,128)(2,1)S(1)} %get-tuple-element.42, bf16[192,1024]{1,0:T(8,128)(2,1)S(1)} %get-tuple-element.41, bf16[384,1024]{1,0:T(8,128)(2,1)S(1)} %get-tuple-element.40), kind=kOutput, calls=%fused_computation.2 | convolution fusion | flops 2621964288 | bytes 10944512 | tf_op jit(solution)/shard_map/dot_general | solution.py:178
  87.5 1.7 %collective-permute-start.17 = (bf16[24,1664]{1,0:T(8,128)(2,1)S(1)}, bf16[24,1664]{1,0:T(8,128)(2,1)S(1)}, u32[]{:S(2)}, u32[]{:S(2)}) collective-permute-start(bf16[24,1664]{1,0:T(8,128)(2,1)S(1)} %get-tuple-element.78), channel_id=1, source_target_pairs={{0,4},{4,0},{8,12},{12,8},{16,20},{20,16},{24,28},{28,24},{1,5},{5... | collective-permute-start | bytes 239624 | tf_op jit(solution)/shard_map/ppermute | solution.py:16
  89.2 1.8 %collective-permute-start.21 = (bf16[24,1664]{1,0:T(8,128)(2,1)S(1)}, bf16[24,1664]{1,0:T(8,128)(2,1)S(1)}, u32[]{:S(2)}, u32[]{:S(2)}) collective-permute-start(bf16[24,1664]{1,0:T(8,128)(2,1)S(1)} %get-tuple-element.47), channel_id=1, source_target_pairs={{0,12},{4,8},{8,4},{12,0},{16,28},{20,24},{24,20},{28,16},{1,13},{... | collective-permute-start | bytes 239624 | tf_op jit(solution)/shard_map/ppermute | solution.py:16
  91.1 4.8 %convolution_bitcast_fusion = f32[1,1664,1024]{2,1,0:T(8,128)} fusion(bf16[768,3328]{1,0:T(8,128)(2,1)S(1)} %constant_dynamic-update-slice_fusion.11, bf16[192,1024]{1,0:T(8,128)(2,1)S(1)} %get-tuple-element.56, bf16[192,1024]{1,0:T(8,128)(2,1)S(1)} %get-tuple-element.55, bf16[384,1024]{1,0:T(8,128)(2,1)S(1)} %get-tuple-element.54), kind=kOutput, calls=%fused_computation | convolution fusion | flops 2621964288 | bytes 10944512 | tf_op jit(solution)/shard_map/dot_general | solution.py:194
  96.1 1.1 %convolution_convert_fusion = bf16[128,1664]{1,0:T(8,128)(2,1)} fusion(bf16[192,128]{1,0:T(8,128)(2,1)S(1)} %get-tuple-element.32, bf16[192,1664]{1,0:T(8,128)(2,1)S(1)} %constant_dynamic-update-slice_fusion.25), kind=kOutput, calls=%fused_computation.4 | convolution fusion | flops 82001920 | bytes 1114112 | tf_op jit(solution)/shard_map/dot_general | solution.py:205
  (84 shorter events, 6.4 us)
Async XLA Ops:
  0.6 1.0 %copy-start.2 = (bf16[128,1664]{1,0:T(8,128)(2,1)S(1)}, bf16[128,1664]{1,0:T(8,128)(2,1)}, u32[]{:S(2)}) copy-start(bf16[128,1664]{1,0:T(8,128)(2,1)} %tokens.1) | copy-start | bytes 1277956
  1.6 1.0 %copy-start.3 = (bf16[128,1664]{1,0:T(8,128)(2,1)S(1)}, bf16[128,1664]{1,0:T(8,128)(2,1)}, u32[]{:S(2)}) copy-start(bf16[128,1664]{1,0:T(8,128)(2,1)} %out_grad.1) | copy-start | bytes 1277956
  3.3 0.7 copy-start.6
  6.1 8.9 %collective-permute-start = (bf16[24,3328]{1,0:T(8,128)(2,1)S(1)}, bf16[24,3328]{1,0:T(8,128)(2,1)S(1)}, u32[]{:S(2)}, u32[]{:S(2)}) collective-permute-start(bf16[24,3328]{1,0:T(8,128)(2,1)S(1)} %get-tuple-element.69), channel_id=1, source_target_pairs={{0,4},{4,0},{8,12},{12,8},{16,20},{20,16},{24,28},{28,24},{1,5},{5... | collective-permute-start | bytes 479240 | tf_op jit(solution)/shard_map/ppermute | solution.py:16
  9.1 12.8 %collective-permute-start.1 = (bf16[24,3328]{1,0:T(8,128)(2,1)S(1)}, bf16[24,3328]{1,0:T(8,128)(2,1)S(1)}, u32[]{:S(2)}, u32[]{:S(2)}) collective-permute-start(bf16[24,3328]{1,0:T(8,128)(2,1)S(1)} %get-tuple-element.68), channel_id=1, source_target_pairs={{0,8},{4,12},{8,0},{12,4},{16,24},{20,28},{24,16},{28,20},{1,9},{5... | collective-permute-start | bytes 479240 | tf_op jit(solution)/shard_map/ppermute | solution.py:16
  10.7 12.6 %collective-permute-start.2 = (bf16[24,3328]{1,0:T(8,128)(2,1)S(1)}, bf16[24,3328]{1,0:T(8,128)(2,1)S(1)}, u32[]{:S(2)}, u32[]{:S(2)}) collective-permute-start(bf16[24,3328]{1,0:T(8,128)(2,1)S(1)} %get-tuple-element.67), channel_id=1, source_target_pairs={{0,12},{4,8},{8,4},{12,0},{16,28},{20,24},{24,20},{28,16},{1,13},{... | collective-permute-start | bytes 479240 | tf_op jit(solution)/shard_map/ppermute | solution.py:16
  10.7 14.4 %collective-permute-start.7 = (bf16[24,3328]{1,0:T(8,128)(2,1)S(1)}, bf16[24,3328]{1,0:T(8,128)(2,1)S(1)}, u32[]{:S(2)}, u32[]{:S(2)}) collective-permute-start(bf16[24,3328]{1,0:T(8,128)(2,1)S(1)} %get-tuple-element.66), channel_id=1, source_target_pairs={{0,16},{4,20},{8,24},{12,28},{16,0},{20,4},{24,8},{28,12},{1,17},{... | collective-permute-start | bytes 479240 | tf_op jit(solution)/shard_map/ppermute | solution.py:16
  13.7 23.1 %collective-permute-start.8 = (bf16[24,3328]{1,0:T(8,128)(2,1)S(1)}, bf16[24,3328]{1,0:T(8,128)(2,1)S(1)}, u32[]{:S(2)}, u32[]{:S(2)}) collective-permute-start(bf16[24,3328]{1,0:T(8,128)(2,1)S(1)} %get-tuple-element.65), channel_id=1, source_target_pairs={{0,20},{4,16},{8,28},{12,24},{16,4},{20,0},{24,12},{28,8},{1,21},{... | collective-permute-start | bytes 479240 | tf_op jit(solution)/shard_map/ppermute | solution.py:16
  15.0 23.4 %collective-permute-start.13 = (bf16[24,3328]{1,0:T(8,128)(2,1)S(1)}, bf16[24,3328]{1,0:T(8,128)(2,1)S(1)}, u32[]{:S(2)}, u32[]{:S(2)}) collective-permute-start(bf16[24,3328]{1,0:T(8,128)(2,1)S(1)} %get-tuple-element.64), channel_id=1, source_target_pairs={{0,24},{4,28},{8,16},{12,20},{16,8},{20,12},{24,0},{28,4},{1,25},{... | collective-permute-start | bytes 479240 | tf_op jit(solution)/shard_map/ppermute | solution.py:16
  22.0 16.4 %collective-permute-start.14 = (bf16[24,3328]{1,0:T(8,128)(2,1)S(1)}, bf16[24,3328]{1,0:T(8,128)(2,1)S(1)}, u32[]{:S(2)}, u32[]{:S(2)}) collective-permute-start(bf16[24,3328]{1,0:T(8,128)(2,1)S(1)} %get-tuple-element.60), channel_id=1, source_target_pairs={{0,28},{4,24},{8,20},{12,16},{16,12},{20,8},{24,4},{28,0},{1,29},{... | collective-permute-start | bytes 479240 | tf_op jit(solution)/shard_map/ppermute | solution.py:16
  23.4 29.3 %collective-permute-start.3 = (bf16[96,3328]{1,0:T(8,128)(2,1)S(1)}, bf16[96,3328]{1,0:T(8,128)(2,1)S(1)}, u32[]{:S(2)}, u32[]{:S(2)}) collective-permute-start(bf16[96,3328]{1,0:T(8,128)(2,1)S(1)} %pad_maximum_fusion.2), channel_id=1, source_target_pairs={{0,2},{1,3},{2,0},{3,1},{4,6},{5,7},{6,4},{7,5},{8,10},{9,11},{10,... | collective-permute-start | bytes 1916936 | tf_op jit(solution)/shard_map/ppermute | solution.py:16
  36.8 10.8 %collective-permute-start.9 = (bf16[48,3328]{1,0:T(8,128)(2,1)S(1)}, bf16[48,3328]{1,0:T(8,128)(2,1)S(1)}, u32[]{:S(2)}, u32[]{:S(2)}) collective-permute-start(bf16[48,3328]{1,0:T(8,128)(2,1)S(1)} %pad_maximum_fusion.5), channel_id=1, source_target_pairs={{0,2},{1,3},{2,0},{3,1},{4,6},{5,7},{6,4},{7,5},{8,10},{9,11},{10,... | collective-permute-start | bytes 958472 | tf_op jit(solution)/shard_map/ppermute | solution.py:16
  38.4 14.1 %collective-permute-start.15 = (bf16[48,3328]{1,0:T(8,128)(2,1)S(1)}, bf16[48,3328]{1,0:T(8,128)(2,1)S(1)}, u32[]{:S(2)}, u32[]{:S(2)}) collective-permute-start(bf16[48,3328]{1,0:T(8,128)(2,1)S(1)} %pad_maximum_fusion.6), channel_id=1, source_target_pairs={{0,2},{1,3},{2,0},{3,1},{4,6},{5,7},{6,4},{7,5},{8,10},{9,11},{10,... | collective-permute-start | bytes 958472 | tf_op jit(solution)/shard_map/ppermute | solution.py:16
  47.6 5.9 %copy-start.1 = (bf16[1,1024,1664]{2,1,0:T(8,128)(2,1)S(1)}, bf16[1,1024,1664]{2,1,0:T(8,128)(2,1)}, u32[]{:S(2)}) copy-start(bf16[1,1024,1664]{2,1,0:T(8,128)(2,1)} %param.15) | copy-start | bytes 10223620
  47.6 5.7 %collective-permute-start.10 = (bf16[96,3328]{1,0:T(8,128)(2,1)S(1)}, bf16[96,3328]{1,0:T(8,128)(2,1)S(1)}, u32[]{:S(2)}, u32[]{:S(2)}) collective-permute-start(bf16[96,3328]{1,0:T(8,128)(2,1)S(1)} %pad_maximum_fusion.3), channel_id=1, source_target_pairs={{0,1},{1,0},{2,3},{3,2},{4,5},{5,4},{6,7},{7,6},{8,9},{9,8},{10,11... | collective-permute-start | bytes 1916936 | tf_op jit(solution)/shard_map/ppermute | solution.py:16
  52.6 5.9 %collective-permute-start.16 = (bf16[96,3328]{1,0:T(8,128)(2,1)S(1)}, bf16[96,3328]{1,0:T(8,128)(2,1)S(1)}, u32[]{:S(2)}, u32[]{:S(2)}) collective-permute-start(bf16[96,3328]{1,0:T(8,128)(2,1)S(1)} %pad_maximum_fusion.4), channel_id=1, source_target_pairs={{0,1},{1,0},{2,3},{3,2},{4,5},{5,4},{6,7},{7,6},{8,9},{9,8},{10,11... | collective-permute-start | bytes 1916936 | tf_op jit(solution)/shard_map/ppermute | solution.py:16
  52.7 2.0 %copy-start = (bf16[1,1664,1024]{2,1,0:T(8,128)(2,1)S(1)}, bf16[1,1664,1024]{2,1,0:T(8,128)(2,1)}, u32[]{:S(2)}) copy-start(bf16[1,1664,1024]{2,1,0:T(8,128)(2,1)} %param.13) | copy-start | bytes 10223620
  52.7 2.0 %copy-start.4 = (f32[1,1024]{1,0:T(1,128)S(1)}, f32[1,1024]{1,0:T(1,128)}, u32[]{:S(2)}) copy-start(f32[1,1024]{1,0:T(1,128)} %bias.5) | copy-start | bytes 12292
  52.8 12.3 %collective-permute-start.4 = (bf16[192,3328]{1,0:T(8,128)(2,1)S(1)}, bf16[192,3328]{1,0:T(8,128)(2,1)S(1)}, u32[]{:S(2)}, u32[]{:S(2)}) collective-permute-start(bf16[192,3328]{1,0:T(8,128)(2,1)S(1)} %get-tuple-element.75), channel_id=1, source_target_pairs={{0,1},{1,0},{2,3},{3,2},{4,5},{5,4},{6,7},{7,6},{8,9},{9,8},{10,11... | collective-permute-start | bytes 3833864 | tf_op jit(solution)/shard_map/ppermute | solution.py:16
  57.9 4.0 %collective-permute-start.11 = (bf16[96,1664]{1,0:T(8,128)(2,1)S(1)}, bf16[96,1664]{1,0:T(8,128)(2,1)S(1)}, u32[]{:S(2)}, u32[]{:S(2)}) collective-permute-start(bf16[96,1664]{1,0:T(8,128)(2,1)S(1)} %get-tuple-element.38), channel_id=1, source_target_pairs={{0,1},{1,0},{2,3},{3,2},{4,5},{5,4},{6,7},{7,6},{8,9},{9,8},{10,11... | collective-permute-start | bytes 958472 | tf_op jit(solution)/shard_map/ppermute | solution.py:16
  61.8 1.7 %collective-permute-start.22 = (bf16[96,1664]{1,0:T(8,128)(2,1)S(1)}, bf16[96,1664]{1,0:T(8,128)(2,1)S(1)}, u32[]{:S(2)}, u32[]{:S(2)}) collective-permute-start(bf16[96,1664]{1,0:T(8,128)(2,1)S(1)} %get-tuple-element.49), channel_id=1, source_target_pairs={{0,1},{1,0},{2,3},{3,2},{4,5},{5,4},{6,7},{7,6},{8,9},{9,8},{10,11... | collective-permute-start | bytes 958472 | tf_op jit(solution)/shard_map/ppermute | solution.py:16
  62.0 8.2 %collective-permute-start.12 = (bf16[48,1664]{1,0:T(8,128)(2,1)S(1)}, bf16[48,1664]{1,0:T(8,128)(2,1)S(1)}, u32[]{:S(2)}, u32[]{:S(2)}) collective-permute-start(bf16[48,1664]{1,0:T(8,128)(2,1)S(1)} %slice.111), channel_id=1, source_target_pairs={{0,2},{1,3},{2,0},{3,1},{4,6},{5,7},{6,4},{7,5},{8,10},{9,11},{10,... | collective-permute-start | bytes 479240 | tf_op jit(solution)/shard_map/ppermute | solution.py:16
  63.7 8.4 %collective-permute-start.23 = (bf16[48,1664]{1,0:T(8,128)(2,1)S(1)}, bf16[48,1664]{1,0:T(8,128)(2,1)S(1)}, u32[]{:S(2)}, u32[]{:S(2)}) collective-permute-start(bf16[48,1664]{1,0:T(8,128)(2,1)S(1)} %slice.120), channel_id=1, source_target_pairs={{0,2},{1,3},{2,0},{3,1},{4,6},{5,7},{6,4},{7,5},{8,10},{9,11},{10,... | collective-permute-start | bytes 479240 | tf_op jit(solution)/shard_map/ppermute | solution.py:16
  70.2 2.8 %collective-permute-start.5 = (bf16[192,1664]{1,0:T(8,128)(2,1)S(1)}, bf16[192,1664]{1,0:T(8,128)(2,1)S(1)}, u32[]{:S(2)}, u32[]{:S(2)}) collective-permute-start(bf16[192,1664]{1,0:T(8,128)(2,1)S(1)} %get-tuple-element.35), channel_id=1, source_target_pairs={{0,1},{1,0},{2,3},{3,2},{4,5},{5,4},{6,7},{7,6},{8,9},{9,8},{10,11... | collective-permute-start | bytes 1916936 | tf_op jit(solution)/shard_map/ppermute | solution.py:16
  73.2 14.3 %collective-permute-start.6 = (bf16[96,1664]{1,0:T(8,128)(2,1)S(1)}, bf16[96,1664]{1,0:T(8,128)(2,1)S(1)}, u32[]{:S(2)}, u32[]{:S(2)}) collective-permute-start(bf16[96,1664]{1,0:T(8,128)(2,1)S(1)} %slice.109), channel_id=1, source_target_pairs={{0,2},{1,3},{2,0},{3,1},{4,6},{5,7},{6,4},{7,5},{8,10},{9,11},{10,... | collective-permute-start | bytes 958472 | tf_op jit(solution)/shard_map/ppermute | solution.py:16
  74.7 14.6 %collective-permute-start.18 = (bf16[24,1664]{1,0:T(8,128)(2,1)S(1)}, bf16[24,1664]{1,0:T(8,128)(2,1)S(1)}, u32[]{:S(2)}, u32[]{:S(2)}) collective-permute-start(bf16[24,1664]{1,0:T(8,128)(2,1)S(1)} %get-tuple-element.44), channel_id=1, source_target_pairs={{0,16},{4,20},{8,24},{12,28},{16,0},{20,4},{24,8},{28,12},{1,17},{... | collective-permute-start | bytes 239624 | tf_op jit(solution)/shard_map/ppermute | solution.py:16
  75.1 14.1 %collective-permute-start.20 = (bf16[24,1664]{1,0:T(8,128)(2,1)S(1)}, bf16[24,1664]{1,0:T(8,128)(2,1)S(1)}, u32[]{:S(2)}, u32[]{:S(2)}) collective-permute-start(bf16[24,1664]{1,0:T(8,128)(2,1)S(1)} %get-tuple-element.46), channel_id=1, source_target_pairs={{0,20},{4,16},{8,28},{12,24},{16,4},{20,0},{24,12},{28,8},{1,21},{... | collective-permute-start | bytes 239624 | tf_op jit(solution)/shard_map/ppermute | solution.py:16
  78.7 17.4 %collective-permute-start.24 = (bf16[24,1664]{1,0:T(8,128)(2,1)S(1)}, bf16[24,1664]{1,0:T(8,128)(2,1)S(1)}, u32[]{:S(2)}, u32[]{:S(2)}) collective-permute-start(bf16[24,1664]{1,0:T(8,128)(2,1)S(1)} %get-tuple-element.51), channel_id=1, source_target_pairs={{0,24},{4,28},{8,16},{12,20},{16,8},{20,12},{24,0},{28,4},{1,25},{... | collective-permute-start | bytes 239624 | tf_op jit(solution)/shard_map/ppermute | solution.py:16
  80.9 15.2 %collective-permute-start.25 = (bf16[24,1664]{1,0:T(8,128)(2,1)S(1)}, bf16[24,1664]{1,0:T(8,128)(2,1)S(1)}, u32[]{:S(2)}, u32[]{:S(2)}) collective-permute-start(bf16[24,1664]{1,0:T(8,128)(2,1)S(1)} %get-tuple-element.52), channel_id=1, source_target_pairs={{0,28},{4,24},{8,20},{12,16},{16,12},{20,8},{24,4},{28,0},{1,29},{... | collective-permute-start | bytes 239624 | tf_op jit(solution)/shard_map/ppermute | solution.py:16
  87.5 8.4 %collective-permute-start.17 = (bf16[24,1664]{1,0:T(8,128)(2,1)S(1)}, bf16[24,1664]{1,0:T(8,128)(2,1)S(1)}, u32[]{:S(2)}, u32[]{:S(2)}) collective-permute-start(bf16[24,1664]{1,0:T(8,128)(2,1)S(1)} %get-tuple-element.78), channel_id=1, source_target_pairs={{0,4},{4,0},{8,12},{12,8},{16,20},{20,16},{24,28},{28,24},{1,5},{5... | collective-permute-start | bytes 239624 | tf_op jit(solution)/shard_map/ppermute | solution.py:16
  89.2 6.7 %collective-permute-start.19 = (bf16[24,1664]{1,0:T(8,128)(2,1)S(1)}, bf16[24,1664]{1,0:T(8,128)(2,1)S(1)}, u32[]{:S(2)}, u32[]{:S(2)}) collective-permute-start(bf16[24,1664]{1,0:T(8,128)(2,1)S(1)} %get-tuple-element.45), channel_id=1, source_target_pairs={{0,8},{4,12},{8,0},{12,4},{16,24},{20,28},{24,16},{28,20},{1,9},{5... | collective-permute-start | bytes 239624 | tf_op jit(solution)/shard_map/ppermute | solution.py:16
  89.2 6.7 %collective-permute-start.21 = (bf16[24,1664]{1,0:T(8,128)(2,1)S(1)}, bf16[24,1664]{1,0:T(8,128)(2,1)S(1)}, u32[]{:S(2)}, u32[]{:S(2)}) collective-permute-start(bf16[24,1664]{1,0:T(8,128)(2,1)S(1)} %get-tuple-element.47), channel_id=1, source_target_pairs={{0,12},{4,8},{8,4},{12,0},{16,28},{20,24},{24,20},{28,16},{1,13},{... | collective-permute-start | bytes 239624 | tf_op jit(solution)/shard_map/ppermute | solution.py:16
  (2 other events, 1.3 us)

commit v3 on v2

--- a/solution.py
+++ b/solution.py
@@ -24,8 +24,8 @@
     return lax.optimization_barrier((value,) + needed)[0]
 
 
-def dispatch_kernel(capacity, me, tokens, out_grad, index, slots, weights, rows, chosen, *scratch):
-    held, sems = scratch[:-1], scratch[-1]
+def dispatch_kernel(capacity, me, tokens, out_grad, index, slots, weights, chosen, *refs):
+    blocks, held, sems = refs[:-6], refs[-6:-1], refs[-1]
     copies = [
         pltpu.make_async_copy(source, target, sems.at[i])
         for i, (source, target) in enumerate(zip((index, slots, weights, tokens, out_grad), held))
@@ -51,10 +51,13 @@
     chosen[...] = one_hot
     copies[3].wait()
     picked = jnp.dot(one_hot, tokens_held[...], preferred_element_type=jnp.float32)
-    rows[:, :width] = picked.astype(jnp.bfloat16)
+    for k, block in enumerate(blocks):
+        block[:, :width] = picked[k * capacity : (k + 1) * capacity].astype(jnp.bfloat16)
     copies[4].wait()
     picked = jnp.dot(one_hot, grad_held[...], preferred_element_type=jnp.float32)
-    rows[:, width:] = (picked * scale).astype(jnp.bfloat16)
+    picked = (picked * scale).astype(jnp.bfloat16)
+    for k, block in enumerate(blocks):
+        block[:, width:] = picked[k * capacity : (k + 1) * capacity]
 
 
 def dispatch_call(capacity, me, tokens, out_grad, index, slots, weights):
@@ -65,14 +68,14 @@
     return pl.pallas_call(
         functools.partial(dispatch_kernel, capacity),
         out_shape=[
-            jax.ShapeDtypeStruct((count, 2 * width), jnp.bfloat16),
             jax.ShapeDtypeStruct((count, tok_count), jnp.bfloat16),
-        ],
-        in_specs=[pl.BlockSpec(memory_space=pltpu.SMEM)] + [pl.BlockSpec(memory_space=pltpu.HBM)] * 5,
-        out_specs=[in_vmem] * 2,
+        ]
+        + [jax.ShapeDtypeStruct((capacity, 2 * width), jnp.bfloat16)] * lax.axis_size("expert"),
+        in_specs=[pl.BlockSpec(memory_space=pltpu.SMEM)] + [pl.BlockSpec(memory_space=pl.ANY)] * 5,
+        out_specs=[in_vmem] * (1 + lax.axis_size("expert")),
         scratch_shapes=[pltpu.VMEM(x.shape, x.dtype) for x in arrays]
         + [pltpu.SemaphoreType.DMA((5,))],
-        compiler_params=pltpu.CompilerParams(vmem_limit_bytes=16 << 20),
+        compiler_params=pltpu.CompilerParams(vmem_limit_bytes=58 << 20),
         cost_estimate=pl.CostEstimate(flops=0, bytes_accessed=0, transcendentals=0),
     )(me, tokens, out_grad, index, slots, weights)
 
@@ -126,12 +129,9 @@
     me = lax.axis_index("expert")
     first_w, second_w = w_in[0], w_out[0]
 
-    rows, chosen = dispatch_call(
+    chosen, *sent = dispatch_call(
         capacity, me.reshape(1), tokens, out_grad, expert_index.T, slots.T, combine.T
     )
-
-    def block(k):
-        return rows[k * capacity : (k + 1) * capacity]
 
     across_masks = [2 << i for i in range(lax.axis_size("dp").bit_length() - 2)]
     half, quarter = experts // 2, experts // 4
@@ -142,9 +142,9 @@
         return pieces
 
     near, far_one, far_two = range(half), range(half, half + quarter), range(half + quarter, experts)
-    got = {0: block(0)}
+    got = {0: sent[0]}
     for k in range(1, experts):
-        got[k] = swap(block(k), "expert", k)
+        got[k] = swap(sent[k], "expert", k)
     groups = [near, far_one, far_two]
     runs = [[near], [far_one], [far_two]]
     sets = [[spread(joined([got[k] for k in run])) for run in part] for part in runs]

time: 97.4 us -> 95.9 us (0.985)
  local copies, waits for them, and re-layouts: 6.1 us -> 2.92 us
  Pallas kernels: 12.7 us -> 14.2 us
    unnamed x34 -> x27, local copies, waits for them, and re-layouts: 5.82 us -> 2.76 us
    pallas_call x1, Pallas kernels: 1.31 us -> 2.79 us  [dispatch_call(): pl.pallas_call(functools.partial(dispatch_kernel, capacity), out_shape=[j...]
  transfers between devices with their start and end apart: 26 -> 26, of which waited for: 6 -> 6; matrix products, arithmetic and copies ran while one was open for 12% -> 14% of each run, Pallas kernels for 12% -> 12%
where the time goes in v3:
time: 95.9 us; the launch traced here: 95.8 us
  starting transfers between devices  34.5 us (36%)
  waiting for transfers between devices  29.6 us (31%)
  Pallas kernels  14.2 us (15%)
  matrix products  11 us (11%)
  local copies, waits for them, and re-layouts  2.92 us (3%)
  other arithmetic  2.35 us (2%)
  between operations  1.21 us (1%)
    ppermute x26, starting transfers between devices, swap(): return lax.ppermute(value, axis, [(i, i ^ mask) for i in range(size)])  34.5 us
    ppermute x26, waiting for transfers between devices, swap(): return lax.ppermute(value, axis, [(i, i ^ mask) for i in range(size)])  29.6 us
    pallas_call x3, Pallas kernels, chunk_call(): pl.pallas_call(functools.partial(chunk_kernel, min(512, units)), out_shap...  11.4 us
    dot_general x1, matrix products, on_device(): lax.dot_general(hidden, rows_all[:, width:], (((0,), (0,)), ((), ())), pr...  5.08 us
    dot_general x1, matrix products, on_device(): lax.dot_general(rows_all[:, :width], d_pre, (((0,), (0,)), ((), ())), pre...  4.82 us
    pallas_call x1, Pallas kernels, dispatch_call(): pl.pallas_call(functools.partial(dispatch_kernel, capacity), out_shape=[j...  2.79 us
    unnamed x27, local copies, waits for them, and re-layouts  2.76 us
  transfers between devices with their start and end apart: 26, of which 6 were waited for; matrix products, arithmetic and copies ran while one was open for 14% of the time, Pallas kernels for 12%

profile of v3, /device:TPU:0, one launch (start us, length us, event | category | flops | bytes accessed | tf_op | source)
XLA Modules:
  0.0 95.8 jit_solution(15375929592265921227)
XLA Ops:
  0.6 2.8 %shard_map.111 = (bf16[192,128]{1,0:T(8,128)(2,1)}, bf16[24,3328]{1,0:T(8,128)(2,1)}, bf16[24,3328]{1,0:T(8,128)(2,1)}, bf16[24,3328]{1,0:T(8,128)(2,1)}, bf16[2...) custom-call(s32[1]{0:T(128)} %bitcast.me, ...), custom_call_target="tpu_custom_call" | custom-call | tf_op jit(solution)/shard_map/pallas_call | solution.py:68
  3.4 3.0 %collective-permute-start = (bf16[24,3328]{1,0:T(8,128)(2,1)}, bf16[24,3328]{1,0:T(8,128)(2,1)S(1)}, u32[]{:S(2)}, u32[]{:S(2)}) collective-permute-start(bf16[24,3328]{1,0:T(8,128)(2,1)} %get-tuple-element.41), channel_id=1, source_target_pairs={{0,4},{4,0},{8,12},{12,8},{16,20},{20,16},{24,28},{28,24},{1,5},{5... | collective-permute-start | bytes 479240 | tf_op jit(solution)/shard_map/ppermute | solution.py:16
  6.5 1.6 %collective-permute-start.1 = (bf16[24,3328]{1,0:T(8,128)(2,1)}, bf16[24,3328]{1,0:T(8,128)(2,1)S(1)}, u32[]{:S(2)}, u32[]{:S(2)}) collective-permute-start(bf16[24,3328]{1,0:T(8,128)(2,1)} %get-tuple-element.42), channel_id=1, source_target_pairs={{0,8},{4,12},{8,0},{12,4},{16,24},{20,28},{24,16},{28,20},{1,9},{5... | collective-permute-start | bytes 479240 | tf_op jit(solution)/shard_map/ppermute | solution.py:16
  8.0 3.0 %collective-permute-start.7 = (bf16[24,3328]{1,0:T(8,128)(2,1)}, bf16[24,3328]{1,0:T(8,128)(2,1)S(1)}, u32[]{:S(2)}, u32[]{:S(2)}) collective-permute-start(bf16[24,3328]{1,0:T(8,128)(2,1)} %get-tuple-element.47), channel_id=1, source_target_pairs={{0,16},{4,20},{8,24},{12,28},{16,0},{20,4},{24,8},{28,12},{1,17},{... | collective-permute-start | bytes 479240 | tf_op jit(solution)/shard_map/ppermute | solution.py:16
  11.0 1.3 %collective-permute-start.8 = (bf16[24,3328]{1,0:T(8,128)(2,1)}, bf16[24,3328]{1,0:T(8,128)(2,1)S(1)}, u32[]{:S(2)}, u32[]{:S(2)}) collective-permute-start(bf16[24,3328]{1,0:T(8,128)(2,1)} %get-tuple-element.48), channel_id=1, source_target_pairs={{0,20},{4,16},{8,28},{12,24},{16,4},{20,0},{24,12},{28,8},{1,21},{... | collective-permute-start | bytes 479240 | tf_op jit(solution)/shard_map/ppermute | solution.py:16
  12.3 0.9 constant_dynamic-update-slice_fusion.24
  13.3 3.7 %collective-permute-start.13 = (bf16[24,3328]{1,0:T(8,128)(2,1)}, bf16[24,3328]{1,0:T(8,128)(2,1)S(1)}, u32[]{:S(2)}, u32[]{:S(2)}) collective-permute-start(bf16[24,3328]{1,0:T(8,128)(2,1)} %get-tuple-element.54), channel_id=1, source_target_pairs={{0,24},{4,28},{8,16},{12,20},{16,8},{20,12},{24,0},{28,4},{1,25},{... | collective-permute-start | bytes 479240 | tf_op jit(solution)/shard_map/ppermute | solution.py:16
  16.9 2.5 %collective-permute-done.1 = bf16[24,3328]{1,0:T(8,128)(2,1)S(1)} collective-permute-done((bf16[24,3328]{1,0:T(8,128)(2,1)}, bf16[24,3328]{1,0:T(8,128)(2,1)S(1)}, u32[]{:S(2)}, u32[]{:S(2)}) %collective-permute-start.1) | collective-permute-done | bytes 159776 | tf_op jit(solution)/shard_map/ppermute | solution.py:16
  19.5 1.1 %collective-permute-start.14 = (bf16[24,3328]{1,0:T(8,128)(2,1)}, bf16[24,3328]{1,0:T(8,128)(2,1)S(1)}, u32[]{:S(2)}, u32[]{:S(2)}) collective-permute-start(bf16[24,3328]{1,0:T(8,128)(2,1)} %get-tuple-element.55), channel_id=1, source_target_pairs={{0,28},{4,24},{8,20},{12,16},{16,12},{20,8},{24,4},{28,0},{1,29},{... | collective-permute-start | bytes 479240 | tf_op jit(solution)/shard_map/ppermute | solution.py:16
  20.9 1.0 pad_maximum_fusion.2
  21.8 1.7 %collective-permute-start.3 = (bf16[96,3328]{1,0:T(8,128)(2,1)S(1)}, bf16[96,3328]{1,0:T(8,128)(2,1)S(1)}, u32[]{:S(2)}, u32[]{:S(2)}) collective-permute-start(bf16[96,3328]{1,0:T(8,128)(2,1)S(1)} %pad_maximum_fusion.2), channel_id=1, source_target_pairs={{0,2},{1,3},{2,0},{3,1},{4,6},{5,7},{6,4},{7,5},{8,10},{9,11},{10,... | collective-permute-start | bytes 1916936 | tf_op jit(solution)/shard_map/ppermute | solution.py:16
  23.5 10.8 %collective-permute-done.8 = bf16[24,3328]{1,0:T(8,128)(2,1)S(1)} collective-permute-done((bf16[24,3328]{1,0:T(8,128)(2,1)}, bf16[24,3328]{1,0:T(8,128)(2,1)S(1)}, u32[]{:S(2)}, u32[]{:S(2)}) %collective-permute-start.8) | collective-permute-done | bytes 159776 | tf_op jit(solution)/shard_map/ppermute | solution.py:16
  34.3 1.6 %collective-permute-start.9 = (bf16[48,3328]{1,0:T(8,128)(2,1)S(1)}, bf16[48,3328]{1,0:T(8,128)(2,1)S(1)}, u32[]{:S(2)}, u32[]{:S(2)}) collective-permute-start(bf16[48,3328]{1,0:T(8,128)(2,1)S(1)} %pad_maximum_fusion.5), channel_id=1, source_target_pairs={{0,2},{1,3},{2,0},{3,1},{4,6},{5,7},{6,4},{7,5},{8,10},{9,11},{10,... | collective-permute-start | bytes 958472 | tf_op jit(solution)/shard_map/ppermute | solution.py:16
  36.7 9.4 %collective-permute-done.9 = bf16[48,3328]{1,0:T(8,128)(2,1)S(1)} collective-permute-done((bf16[48,3328]{1,0:T(8,128)(2,1)S(1)}, bf16[48,3328]{1,0:T(8,128)(2,1)S(1)}, u32[]{:S(2)}, u32[]{:S(2)}) %collective-permute-start.9) | collective-permute-done | bytes 319520 | tf_op jit(solution)/shard_map/ppermute | solution.py:16
  46.2 4.8 %collective-permute-done.15 = bf16[48,3328]{1,0:T(8,128)(2,1)S(1)} collective-permute-done((bf16[48,3328]{1,0:T(8,128)(2,1)S(1)}, bf16[48,3328]{1,0:T(8,128)(2,1)S(1)}, u32[]{:S(2)}, u32[]{:S(2)}) %collective-permute-start.15) | collective-permute-done | bytes 319520 | tf_op jit(solution)/shard_map/ppermute | solution.py:16
  51.9 1.2 %copy-done = bf16[1,1664,1024]{2,1,0:T(8,128)(2,1)S(1)} copy-done((bf16[1,1664,1024]{2,1,0:T(8,128)(2,1)S(1)}, bf16[1,1664,1024]{2,1,0:T(8,128)(2,1)}, u32[]{:S(2)}) %copy-start) | copy-done | bytes 3407896
  53.1 3.3 %shard_map.113 = (bf16[192,1024]{1,0:T(8,128)(2,1)S(1)}, bf16[192,1024]{1,0:T(8,128)(2,1)S(1)}, bf16[96,1664]{1,0:T(8,128)(2,1)S(1)}, bf16[96,1664]{1,0:T(8,128)(2,1)S(1)}, f32[8,1024]{1,0:T(8,128)S(1)}) custom-call(bf16[192,3328]{1,0:T(8,128)(2,1)S(1)} %pad_maximum_fusion.rows, bf16[1664,1024]{1,0:T(8,128)(2,1)S(1)} %bitcast.11, f32[1,1024]{1,0:T(1,128)S(1)} %copy-done.2, ...), custom_call_target="tpu_custom_call" | custom-call | tf_op jit(solution)/shard_map/pallas_call | solution.py:114
  57.0 3.3 %shard_map.114 = (bf16[192,1024]{1,0:T(8,128)(2,1)S(1)}, bf16[192,1024]{1,0:T(8,128)(2,1)S(1)}, bf16[96,1664]{1,0:T(8,128)(2,1)S(1)}, bf16[96,1664]{1,0:T(8,128)(2,1)S(1)}, f32[8,1024]{1,0:T(8,128)S(1)}) custom-call(bf16[192,3328]{1,0:T(8,128)(2,1)S(1)} %pad_maximum_fusion.1.rows, bf16[1664,1024]{1,0:T(8,128)(2,1)S(1)} %bitcast.12, f32[1,1024]{1,0:T(1,128)S(1)} %copy-done.2, ...), custom_call_target="tpu_custom_call" | custom-call | tf_op jit(solution)/shard_map/pallas_call | solution.py:114
  60.5 1.5 %collective-permute-start.12 = (bf16[48,1664]{1,0:T(8,128)(2,1)S(1)}, bf16[48,1664]{1,0:T(8,128)(2,1)S(1)}, u32[]{:S(2)}, u32[]{:S(2)}) collective-permute-start(bf16[48,1664]{1,0:T(8,128)(2,1)S(1)} %slice.79), channel_id=1, source_target_pairs={{0,2},{1,3},{2,0},{3,1},{4,6},{5,7},{6,4},{7,5},{8,10},{9,11},{10,... | collective-permute-start | bytes 479240 | tf_op jit(solution)/shard_map/ppermute | solution.py:16
  62.1 1.5 %collective-permute-start.23 = (bf16[48,1664]{1,0:T(8,128)(2,1)S(1)}, bf16[48,1664]{1,0:T(8,128)(2,1)S(1)}, u32[]{:S(2)}, u32[]{:S(2)}) collective-permute-start(bf16[48,1664]{1,0:T(8,128)(2,1)S(1)} %slice.88), channel_id=1, source_target_pairs={{0,2},{1,3},{2,0},{3,1},{4,6},{5,7},{6,4},{7,5},{8,10},{9,11},{10,... | collective-permute-start | bytes 479240 | tf_op jit(solution)/shard_map/ppermute | solution.py:16
  63.7 4.8 %shard_map.112 = (bf16[384,1024]{1,0:T(8,128)(2,1)S(1)}, bf16[384,1024]{1,0:T(8,128)(2,1)S(1)}, bf16[192,1664]{1,0:T(8,128)(2,1)S(1)}, bf16[192,1664]{1,0:T(8,128)(2,1)S(1)}, f32[8,1024]{1,0:T(8,128)S(1)}) custom-call(bf16[384,3328]{1,0:T(8,128)(2,1)S(1)} %get-tuple-element.75.rows, bf16[1664,1024]{1,0:T(8,128)(2,1)S(1)} %bitcast.13, ...), custom_call_target="tpu_custom_call" | custom-call | tf_op jit(solution)/shard_map/pallas_call | solution.py:114
  68.7 1.7 %collective-permute-done.23 = bf16[48,1664]{1,0:T(8,128)(2,1)S(1)} collective-permute-done((bf16[48,1664]{1,0:T(8,128)(2,1)S(1)}, bf16[48,1664]{1,0:T(8,128)(2,1)S(1)}, u32[]{:S(2)}, u32[]{:S(2)}) %collective-permute-start.23) | collective-permute-done | bytes 159776 | tf_op jit(solution)/shard_map/ppermute | solution.py:16
  70.9 0.6 slice_add_fusion
  71.8 1.5 %collective-permute-start.6 = (bf16[96,1664]{1,0:T(8,128)(2,1)S(1)}, bf16[96,1664]{1,0:T(8,128)(2,1)S(1)}, u32[]{:S(2)}, u32[]{:S(2)}) collective-permute-start(bf16[96,1664]{1,0:T(8,128)(2,1)S(1)} %slice.77), channel_id=1, source_target_pairs={{0,2},{1,3},{2,0},{3,1},{4,6},{5,7},{6,4},{7,5},{8,10},{9,11},{10,... | collective-permute-start | bytes 958472 | tf_op jit(solution)/shard_map/ppermute | solution.py:16
  73.8 3.5 %collective-permute-start.20 = (bf16[24,1664]{1,0:T(8,128)(2,1)S(1)}, bf16[24,1664]{1,0:T(8,128)(2,1)S(1)}, u32[]{:S(2)}, u32[]{:S(2)}) collective-permute-start(bf16[24,1664]{1,0:T(8,128)(2,1)S(1)} %get-tuple-element.60), channel_id=1, source_target_pairs={{0,20},{4,16},{8,28},{12,24},{16,4},{20,0},{24,12},{28,8},{1,21},{... | collective-permute-start | bytes 239624 | tf_op jit(solution)/shard_map/ppermute | solution.py:16
  77.3 2.2 %collective-permute-start.24 = (bf16[24,1664]{1,0:T(8,128)(2,1)S(1)}, bf16[24,1664]{1,0:T(8,128)(2,1)S(1)}, u32[]{:S(2)}, u32[]{:S(2)}) collective-permute-start(bf16[24,1664]{1,0:T(8,128)(2,1)S(1)} %get-tuple-element.65), channel_id=1, source_target_pairs={{0,24},{4,28},{8,16},{12,20},{16,8},{20,12},{24,0},{28,4},{1,25},{... | collective-permute-start | bytes 239624 | tf_op jit(solution)/shard_map/ppermute | solution.py:16
  79.5 1.5 %collective-permute-start.25 = (bf16[24,1664]{1,0:T(8,128)(2,1)S(1)}, bf16[24,1664]{1,0:T(8,128)(2,1)S(1)}, u32[]{:S(2)}, u32[]{:S(2)}) collective-permute-start(bf16[24,1664]{1,0:T(8,128)(2,1)S(1)} %get-tuple-element.66), channel_id=1, source_target_pairs={{0,28},{4,24},{8,20},{12,16},{16,12},{20,8},{24,4},{28,0},{1,29},{... | collective-permute-start | bytes 239624 | tf_op jit(solution)/shard_map/ppermute | solution.py:16
  80.9 5.1 %fusion.1 = f32[1024,1664]{1,0:T(8,128)} fusion(bf16[768,3328]{1,0:T(8,128)(2,1)S(1)} %constant_dynamic-update-slice_fusion.11, bf16[192,1024]{1,0:T(8,128)(2,1)S(1)} %get-tuple-element.56, bf16[192,1024]{1,0:T(8,128)(2,1)S(1)} %get-tuple-element.53, bf16[384,1024]{1,0:T(8,128)(2,1)S(1)} %get-tuple-element.52), kind=kOutput, calls=%fused_computation.2 | convolution fusion | flops 2621964288 | bytes 10944512 | tf_op jit(solution)/shard_map/dot_general | solution.py:178
  86.1 1.7 %collective-permute-start.17 = (bf16[24,1664]{1,0:T(8,128)(2,1)S(1)}, bf16[24,1664]{1,0:T(8,128)(2,1)S(1)}, u32[]{:S(2)}, u32[]{:S(2)}) collective-permute-start(bf16[24,1664]{1,0:T(8,128)(2,1)S(1)} %get-tuple-element.81), channel_id=1, source_target_pairs={{0,4},{4,0},{8,12},{12,8},{16,20},{20,16},{24,28},{28,24},{1,5},{5... | collective-permute-start | bytes 239624 | tf_op jit(solution)/shard_map/ppermute | solution.py:16
  87.9 1.8 %collective-permute-start.21 = (bf16[24,1664]{1,0:T(8,128)(2,1)S(1)}, bf16[24,1664]{1,0:T(8,128)(2,1)S(1)}, u32[]{:S(2)}, u32[]{:S(2)}) collective-permute-start(bf16[24,1664]{1,0:T(8,128)(2,1)S(1)} %get-tuple-element.61), channel_id=1, source_target_pairs={{0,12},{4,8},{8,4},{12,0},{16,28},{20,24},{24,20},{28,16},{1,13},{... | collective-permute-start | bytes 239624 | tf_op jit(solution)/shard_map/ppermute | solution.py:16
  89.7 4.8 %convolution_bitcast_fusion = f32[1,1664,1024]{2,1,0:T(8,128)} fusion(bf16[768,3328]{1,0:T(8,128)(2,1)S(1)} %constant_dynamic-update-slice_fusion.11, bf16[192,1024]{1,0:T(8,128)(2,1)S(1)} %get-tuple-element.70, bf16[192,1024]{1,0:T(8,128)(2,1)S(1)} %get-tuple-element.69, bf16[384,1024]{1,0:T(8,128)(2,1)S(1)} %get-tuple-element.68), kind=kOutput, calls=%fused_computation | convolution fusion | flops 2621964288 | bytes 10944512 | tf_op jit(solution)/shard_map/dot_general | solution.py:194
  94.7 1.1 %convolution_convert_fusion = bf16[128,1664]{1,0:T(8,128)(2,1)} fusion(bf16[192,128]{1,0:T(8,128)(2,1)S(1)} %copy-done.3, bf16[192,1664]{1,0:T(8,128)(2,1)S(1)} %constant_dynamic-update-slice_fusion.25), kind=kOutput, calls=%fused_computation.4 | convolution fusion | flops 82001920 | bytes 1114112 | tf_op jit(solution)/shard_map/dot_general | solution.py:205
  (76 shorter events, 4.4 us)
Async XLA Ops:
  3.4 9.8 %collective-permute-start = (bf16[24,3328]{1,0:T(8,128)(2,1)}, bf16[24,3328]{1,0:T(8,128)(2,1)S(1)}, u32[]{:S(2)}, u32[]{:S(2)}) collective-permute-start(bf16[24,3328]{1,0:T(8,128)(2,1)} %get-tuple-element.41), channel_id=1, source_target_pairs={{0,4},{4,0},{8,12},{12,8},{16,20},{20,16},{24,28},{28,24},{1,5},{5... | collective-permute-start | bytes 479240 | tf_op jit(solution)/shard_map/ppermute | solution.py:16
  6.5 13.0 %collective-permute-start.1 = (bf16[24,3328]{1,0:T(8,128)(2,1)}, bf16[24,3328]{1,0:T(8,128)(2,1)S(1)}, u32[]{:S(2)}, u32[]{:S(2)}) collective-permute-start(bf16[24,3328]{1,0:T(8,128)(2,1)} %get-tuple-element.42), channel_id=1, source_target_pairs={{0,8},{4,12},{8,0},{12,4},{16,24},{20,28},{24,16},{28,20},{1,9},{5... | collective-permute-start | bytes 479240 | tf_op jit(solution)/shard_map/ppermute | solution.py:16
  8.0 12.8 %collective-permute-start.2 = (bf16[24,3328]{1,0:T(8,128)(2,1)}, bf16[24,3328]{1,0:T(8,128)(2,1)S(1)}, u32[]{:S(2)}, u32[]{:S(2)}) collective-permute-start(bf16[24,3328]{1,0:T(8,128)(2,1)} %get-tuple-element.43), channel_id=1, source_target_pairs={{0,12},{4,8},{8,4},{12,0},{16,28},{20,24},{24,20},{28,16},{1,13},{... | collective-permute-start | bytes 479240 | tf_op jit(solution)/shard_map/ppermute | solution.py:16
  8.0 15.5 %collective-permute-start.7 = (bf16[24,3328]{1,0:T(8,128)(2,1)}, bf16[24,3328]{1,0:T(8,128)(2,1)S(1)}, u32[]{:S(2)}, u32[]{:S(2)}) collective-permute-start(bf16[24,3328]{1,0:T(8,128)(2,1)} %get-tuple-element.47), channel_id=1, source_target_pairs={{0,16},{4,20},{8,24},{12,28},{16,0},{20,4},{24,8},{28,12},{1,17},{... | collective-permute-start | bytes 479240 | tf_op jit(solution)/shard_map/ppermute | solution.py:16
  11.0 23.3 %collective-permute-start.8 = (bf16[24,3328]{1,0:T(8,128)(2,1)}, bf16[24,3328]{1,0:T(8,128)(2,1)S(1)}, u32[]{:S(2)}, u32[]{:S(2)}) collective-permute-start(bf16[24,3328]{1,0:T(8,128)(2,1)} %get-tuple-element.48), channel_id=1, source_target_pairs={{0,20},{4,16},{8,28},{12,24},{16,4},{20,0},{24,12},{28,8},{1,21},{... | collective-permute-start | bytes 479240 | tf_op jit(solution)/shard_map/ppermute | solution.py:16
  13.3 22.6 %collective-permute-start.13 = (bf16[24,3328]{1,0:T(8,128)(2,1)}, bf16[24,3328]{1,0:T(8,128)(2,1)S(1)}, u32[]{:S(2)}, u32[]{:S(2)}) collective-permute-start(bf16[24,3328]{1,0:T(8,128)(2,1)} %get-tuple-element.54), channel_id=1, source_target_pairs={{0,24},{4,28},{8,16},{12,20},{16,8},{20,12},{24,0},{28,4},{1,25},{... | collective-permute-start | bytes 479240 | tf_op jit(solution)/shard_map/ppermute | solution.py:16
  19.5 16.4 %collective-permute-start.14 = (bf16[24,3328]{1,0:T(8,128)(2,1)}, bf16[24,3328]{1,0:T(8,128)(2,1)S(1)}, u32[]{:S(2)}, u32[]{:S(2)}) collective-permute-start(bf16[24,3328]{1,0:T(8,128)(2,1)} %get-tuple-element.55), channel_id=1, source_target_pairs={{0,28},{4,24},{8,20},{12,16},{16,12},{20,8},{24,4},{28,0},{1,29},{... | collective-permute-start | bytes 479240 | tf_op jit(solution)/shard_map/ppermute | solution.py:16
  21.8 29.3 %collective-permute-start.3 = (bf16[96,3328]{1,0:T(8,128)(2,1)S(1)}, bf16[96,3328]{1,0:T(8,128)(2,1)S(1)}, u32[]{:S(2)}, u32[]{:S(2)}) collective-permute-start(bf16[96,3328]{1,0:T(8,128)(2,1)S(1)} %pad_maximum_fusion.2), channel_id=1, source_target_pairs={{0,2},{1,3},{2,0},{3,1},{4,6},{5,7},{6,4},{7,5},{8,10},{9,11},{10,... | collective-permute-start | bytes 1916936 | tf_op jit(solution)/shard_map/ppermute | solution.py:16
  34.3 11.7 %collective-permute-start.9 = (bf16[48,3328]{1,0:T(8,128)(2,1)S(1)}, bf16[48,3328]{1,0:T(8,128)(2,1)S(1)}, u32[]{:S(2)}, u32[]{:S(2)}) collective-permute-start(bf16[48,3328]{1,0:T(8,128)(2,1)S(1)} %pad_maximum_fusion.5), channel_id=1, source_target_pairs={{0,2},{1,3},{2,0},{3,1},{4,6},{5,7},{6,4},{7,5},{8,10},{9,11},{10,... | collective-permute-start | bytes 958472 | tf_op jit(solution)/shard_map/ppermute | solution.py:16
  36.0 15.0 %collective-permute-start.15 = (bf16[48,3328]{1,0:T(8,128)(2,1)S(1)}, bf16[48,3328]{1,0:T(8,128)(2,1)S(1)}, u32[]{:S(2)}, u32[]{:S(2)}) collective-permute-start(bf16[48,3328]{1,0:T(8,128)(2,1)S(1)} %pad_maximum_fusion.6), channel_id=1, source_target_pairs={{0,2},{1,3},{2,0},{3,1},{4,6},{5,7},{6,4},{7,5},{8,10},{9,11},{10,... | collective-permute-start | bytes 958472 | tf_op jit(solution)/shard_map/ppermute | solution.py:16
  46.0 5.9 %copy-start.1 = (bf16[1,1024,1664]{2,1,0:T(8,128)(2,1)S(1)}, bf16[1,1024,1664]{2,1,0:T(8,128)(2,1)}, u32[]{:S(2)}) copy-start(bf16[1,1024,1664]{2,1,0:T(8,128)(2,1)} %param.15) | copy-start | bytes 10223620
  46.1 5.7 %collective-permute-start.10 = (bf16[96,3328]{1,0:T(8,128)(2,1)S(1)}, bf16[96,3328]{1,0:T(8,128)(2,1)S(1)}, u32[]{:S(2)}, u32[]{:S(2)}) collective-permute-start(bf16[96,3328]{1,0:T(8,128)(2,1)S(1)} %pad_maximum_fusion.3), channel_id=1, source_target_pairs={{0,1},{1,0},{2,3},{3,2},{4,5},{5,4},{6,7},{7,6},{8,9},{9,8},{10,11... | collective-permute-start | bytes 1916936 | tf_op jit(solution)/shard_map/ppermute | solution.py:16
  51.0 5.9 %collective-permute-start.16 = (bf16[96,3328]{1,0:T(8,128)(2,1)S(1)}, bf16[96,3328]{1,0:T(8,128)(2,1)S(1)}, u32[]{:S(2)}, u32[]{:S(2)}) collective-permute-start(bf16[96,3328]{1,0:T(8,128)(2,1)S(1)} %pad_maximum_fusion.4), channel_id=1, source_target_pairs={{0,1},{1,0},{2,3},{3,2},{4,5},{5,4},{6,7},{7,6},{8,9},{9,8},{10,11... | collective-permute-start | bytes 1916936 | tf_op jit(solution)/shard_map/ppermute | solution.py:16
  51.1 2.0 %copy-start = (bf16[1,1664,1024]{2,1,0:T(8,128)(2,1)S(1)}, bf16[1,1664,1024]{2,1,0:T(8,128)(2,1)}, u32[]{:S(2)}) copy-start(bf16[1,1664,1024]{2,1,0:T(8,128)(2,1)} %param.13) | copy-start | bytes 10223620
  51.1 2.0 %copy-start.2 = (f32[1,1024]{1,0:T(1,128)S(1)}, f32[1,1024]{1,0:T(1,128)}, u32[]{:S(2)}) copy-start(f32[1,1024]{1,0:T(1,128)} %bias.5) | copy-start | bytes 12292
  51.3 12.3 %collective-permute-start.4 = (bf16[192,3328]{1,0:T(8,128)(2,1)S(1)}, bf16[192,3328]{1,0:T(8,128)(2,1)S(1)}, u32[]{:S(2)}, u32[]{:S(2)}) collective-permute-start(bf16[192,3328]{1,0:T(8,128)(2,1)S(1)} %get-tuple-element.78), channel_id=1, source_target_pairs={{0,1},{1,0},{2,3},{3,2},{4,5},{5,4},{6,7},{7,6},{8,9},{9,8},{10,11... | collective-permute-start | bytes 3833864 | tf_op jit(solution)/shard_map/ppermute | solution.py:16
  56.4 4.0 %collective-permute-start.11 = (bf16[96,1664]{1,0:T(8,128)(2,1)S(1)}, bf16[96,1664]{1,0:T(8,128)(2,1)S(1)}, u32[]{:S(2)}, u32[]{:S(2)}) collective-permute-start(bf16[96,1664]{1,0:T(8,128)(2,1)S(1)} %get-tuple-element.50), channel_id=1, source_target_pairs={{0,1},{1,0},{2,3},{3,2},{4,5},{5,4},{6,7},{7,6},{8,9},{9,8},{10,11... | collective-permute-start | bytes 958472 | tf_op jit(solution)/shard_map/ppermute | solution.py:16
  60.3 1.7 %collective-permute-start.22 = (bf16[96,1664]{1,0:T(8,128)(2,1)S(1)}, bf16[96,1664]{1,0:T(8,128)(2,1)S(1)}, u32[]{:S(2)}, u32[]{:S(2)}) collective-permute-start(bf16[96,1664]{1,0:T(8,128)(2,1)S(1)} %get-tuple-element.63), channel_id=1, source_target_pairs={{0,1},{1,0},{2,3},{3,2},{4,5},{5,4},{6,7},{7,6},{8,9},{9,8},{10,11... | collective-permute-start | bytes 958472 | tf_op jit(solution)/shard_map/ppermute | solution.py:16
  60.5 8.2 %collective-permute-start.12 = (bf16[48,1664]{1,0:T(8,128)(2,1)S(1)}, bf16[48,1664]{1,0:T(8,128)(2,1)S(1)}, u32[]{:S(2)}, u32[]{:S(2)}) collective-permute-start(bf16[48,1664]{1,0:T(8,128)(2,1)S(1)} %slice.79), channel_id=1, source_target_pairs={{0,2},{1,3},{2,0},{3,1},{4,6},{5,7},{6,4},{7,5},{8,10},{9,11},{10,... | collective-permute-start | bytes 479240 | tf_op jit(solution)/shard_map/ppermute | solution.py:16
  62.1 8.4 %collective-permute-start.23 = (bf16[48,1664]{1,0:T(8,128)(2,1)S(1)}, bf16[48,1664]{1,0:T(8,128)(2,1)S(1)}, u32[]{:S(2)}, u32[]{:S(2)}) collective-permute-start(bf16[48,1664]{1,0:T(8,128)(2,1)S(1)} %slice.88), channel_id=1, source_target_pairs={{0,2},{1,3},{2,0},{3,1},{4,6},{5,7},{6,4},{7,5},{8,10},{9,11},{10,... | collective-permute-start | bytes 479240 | tf_op jit(solution)/shard_map/ppermute | solution.py:16
  68.6 3.0 %collective-permute-start.5 = (bf16[192,1664]{1,0:T(8,128)(2,1)S(1)}, bf16[192,1664]{1,0:T(8,128)(2,1)S(1)}, u32[]{:S(2)}, u32[]{:S(2)}) collective-permute-start(bf16[192,1664]{1,0:T(8,128)(2,1)S(1)} %get-tuple-element.45), channel_id=1, source_target_pairs={{0,1},{1,0},{2,3},{3,2},{4,5},{5,4},{6,7},{7,6},{8,9},{9,8},{10,11... | collective-permute-start | bytes 1916936 | tf_op jit(solution)/shard_map/ppermute | solution.py:16
  71.8 14.2 %collective-permute-start.6 = (bf16[96,1664]{1,0:T(8,128)(2,1)S(1)}, bf16[96,1664]{1,0:T(8,128)(2,1)S(1)}, u32[]{:S(2)}, u32[]{:S(2)}) collective-permute-start(bf16[96,1664]{1,0:T(8,128)(2,1)S(1)} %slice.77), channel_id=1, source_target_pairs={{0,2},{1,3},{2,0},{3,1},{4,6},{5,7},{6,4},{7,5},{8,10},{9,11},{10,... | collective-permute-start | bytes 958472 | tf_op jit(solution)/shard_map/ppermute | solution.py:16
  73.3 14.6 %collective-permute-start.18 = (bf16[24,1664]{1,0:T(8,128)(2,1)S(1)}, bf16[24,1664]{1,0:T(8,128)(2,1)S(1)}, u32[]{:S(2)}, u32[]{:S(2)}) collective-permute-start(bf16[24,1664]{1,0:T(8,128)(2,1)S(1)} %get-tuple-element.58), channel_id=1, source_target_pairs={{0,16},{4,20},{8,24},{12,28},{16,0},{20,4},{24,8},{28,12},{1,17},{... | collective-permute-start | bytes 239624 | tf_op jit(solution)/shard_map/ppermute | solution.py:16
  73.8 14.0 %collective-permute-start.20 = (bf16[24,1664]{1,0:T(8,128)(2,1)S(1)}, bf16[24,1664]{1,0:T(8,128)(2,1)S(1)}, u32[]{:S(2)}, u32[]{:S(2)}) collective-permute-start(bf16[24,1664]{1,0:T(8,128)(2,1)S(1)} %get-tuple-element.60), channel_id=1, source_target_pairs={{0,20},{4,16},{8,28},{12,24},{16,4},{20,0},{24,12},{28,8},{1,21},{... | collective-permute-start | bytes 239624 | tf_op jit(solution)/shard_map/ppermute | solution.py:16
  77.3 17.3 %collective-permute-start.24 = (bf16[24,1664]{1,0:T(8,128)(2,1)S(1)}, bf16[24,1664]{1,0:T(8,128)(2,1)S(1)}, u32[]{:S(2)}, u32[]{:S(2)}) collective-permute-start(bf16[24,1664]{1,0:T(8,128)(2,1)S(1)} %get-tuple-element.65), channel_id=1, source_target_pairs={{0,24},{4,28},{8,16},{12,20},{16,8},{20,12},{24,0},{28,4},{1,25},{... | collective-permute-start | bytes 239624 | tf_op jit(solution)/shard_map/ppermute | solution.py:16
  79.5 15.2 %collective-permute-start.25 = (bf16[24,1664]{1,0:T(8,128)(2,1)S(1)}, bf16[24,1664]{1,0:T(8,128)(2,1)S(1)}, u32[]{:S(2)}, u32[]{:S(2)}) collective-permute-start(bf16[24,1664]{1,0:T(8,128)(2,1)S(1)} %get-tuple-element.66), channel_id=1, source_target_pairs={{0,28},{4,24},{8,20},{12,16},{16,12},{20,8},{24,4},{28,0},{1,29},{... | collective-permute-start | bytes 239624 | tf_op jit(solution)/shard_map/ppermute | solution.py:16
  86.1 8.4 %collective-permute-start.17 = (bf16[24,1664]{1,0:T(8,128)(2,1)S(1)}, bf16[24,1664]{1,0:T(8,128)(2,1)S(1)}, u32[]{:S(2)}, u32[]{:S(2)}) collective-permute-start(bf16[24,1664]{1,0:T(8,128)(2,1)S(1)} %get-tuple-element.81), channel_id=1, source_target_pairs={{0,4},{4,0},{8,12},{12,8},{16,20},{20,16},{24,28},{28,24},{1,5},{5... | collective-permute-start | bytes 239624 | tf_op jit(solution)/shard_map/ppermute | solution.py:16
  87.8 6.7 %collective-permute-start.19 = (bf16[24,1664]{1,0:T(8,128)(2,1)S(1)}, bf16[24,1664]{1,0:T(8,128)(2,1)S(1)}, u32[]{:S(2)}, u32[]{:S(2)}) collective-permute-start(bf16[24,1664]{1,0:T(8,128)(2,1)S(1)} %get-tuple-element.59), channel_id=1, source_target_pairs={{0,8},{4,12},{8,0},{12,4},{16,24},{20,28},{24,16},{28,20},{1,9},{5... | collective-permute-start | bytes 239624 | tf_op jit(solution)/shard_map/ppermute | solution.py:16
  87.9 6.7 %collective-permute-start.21 = (bf16[24,1664]{1,0:T(8,128)(2,1)S(1)}, bf16[24,1664]{1,0:T(8,128)(2,1)S(1)}, u32[]{:S(2)}, u32[]{:S(2)}) collective-permute-start(bf16[24,1664]{1,0:T(8,128)(2,1)S(1)} %get-tuple-element.61), channel_id=1, source_target_pairs={{0,12},{4,8},{8,4},{12,0},{16,28},{20,24},{24,20},{28,16},{1,13},{... | collective-permute-start | bytes 239624 | tf_op jit(solution)/shard_map/ppermute | solution.py:16
  89.7 5.0 %copy-start.3 = (bf16[192,128]{1,0:T(8,128)(2,1)S(1)}, bf16[192,128]{1,0:T(8,128)(2,1)}, u32[]{:S(2)}) copy-start(bf16[192,128]{1,0:T(8,128)(2,1)} %get-tuple-element.39) | copy-start | bytes 147460

commit v4 on v3

--- a/solution.py
+++ b/solution.py
@@ -63,7 +63,10 @@
 def dispatch_call(capacity, me, tokens, out_grad, index, slots, weights):
     tok_count, width = tokens.shape
     count = lax.axis_size("expert") * capacity
-    arrays = (index, slots, weights, tokens, out_grad)
+    arrays = [
+        pltpu.with_memory_space_constraint(x, pltpu.HBM)
+        for x in (index, slots, weights, tokens, out_grad)
+    ]
     in_vmem = pl.BlockSpec(memory_space=pltpu.VMEM)
     return pl.pallas_call(
         functools.partial(dispatch_kernel, capacity),
@@ -71,19 +74,19 @@
             jax.ShapeDtypeStruct((count, tok_count), jnp.bfloat16),
         ]
         + [jax.ShapeDtypeStruct((capacity, 2 * width), jnp.bfloat16)] * lax.axis_size("expert"),
-        in_specs=[pl.BlockSpec(memory_space=pltpu.SMEM)] + [pl.BlockSpec(memory_space=pl.ANY)] * 5,
+        in_specs=[pl.BlockSpec(memory_space=pltpu.SMEM)] + [pl.BlockSpec(memory_space=pltpu.HBM)] * 5,
         out_specs=[in_vmem] * (1 + lax.axis_size("expert")),
         scratch_shapes=[pltpu.VMEM(x.shape, x.dtype) for x in arrays]
         + [pltpu.SemaphoreType.DMA((5,))],
-        compiler_params=pltpu.CompilerParams(vmem_limit_bytes=58 << 20),
+        compiler_params=pltpu.CompilerParams(vmem_limit_bytes=16 << 20),
         cost_estimate=pl.CostEstimate(flops=0, bytes_accessed=0, transcendentals=0),
-    )(me, tokens, out_grad, index, slots, weights)
+    )(me, arrays[3], arrays[4], *arrays[:3])
 
 
 contract_last = (((1,), (1,)), ((), ()))
 
 
-def chunk_kernel(step, rows, w_in, bias, w_out, hidden, d_pre, kept, leaving, total):
+def chunk_kernel(step, rows, w_in, bias, w_out, before, hidden, d_pre, kept, leaving, total):
     width, units = w_in.shape
     half = kept.shape[0]
     ones = jnp.ones((8, rows.shape[0]), jnp.bfloat16)
@@ -98,7 +101,8 @@
         hidden[:, part] = (pre_act * cdf).astype(jnp.bfloat16)
         density = jnp.exp(-0.5 * pre_act * pre_act) * inv_root_two_pi
         d_pre[:, part] = (d_hidden * (cdf + pre_act * density)).astype(jnp.bfloat16)
-        total[:, part] = jnp.dot(ones, d_pre[:, part], preferred_element_type=jnp.float32)
+        added = jnp.dot(ones, d_pre[:, part], preferred_element_type=jnp.float32)
+        total[:, part] = before[:, part] + added[:1]
     term = lax.dot_general(
         d_pre[...], w_in[...], contract_last, preferred_element_type=jnp.float32
     ).astype(jnp.bfloat16)
@@ -106,7 +110,7 @@
     leaving[...] = term[half:]
 
 
-def chunk_call(rows, w_in, bias, w_out):
+def chunk_call(rows, w_in, bias, w_out, before):
     count = rows.shape[0]
     width, units = w_in.shape
     in_vmem = pl.BlockSpec(memory_space=pltpu.VMEM)
@@ -114,12 +118,12 @@
     return pl.pallas_call(
         functools.partial(chunk_kernel, min(512, units)),
         out_shape=[jax.ShapeDtypeStruct(shape, jnp.bfloat16) for shape in shapes]
-        + [jax.ShapeDtypeStruct((8, units), jnp.float32)],
-        in_specs=[in_vmem] * 4,
+        + [jax.ShapeDtypeStruct((1, units), jnp.float32)],
+        in_specs=[in_vmem] * 5,
         out_specs=[in_vmem] * 5,
         compiler_params=pltpu.CompilerParams(vmem_limit_bytes=24 << 20),
         cost_estimate=pl.CostEstimate(flops=0, bytes_accessed=0, transcendentals=0),
-    )(rows, w_in, bias, w_out)
+    )(rows, w_in, bias, w_out, before)
 
 
 def on_device(tokens, out_grad, expert_index, slots, combine, w_in, b_in, w_out):
@@ -152,10 +156,14 @@
     for part in sets:
         columns.append(joined([run[i] for i in range(len(part[0])) for run in part]))
 
-    made = []
-    for column in columns:
+    made = [None] * len(columns)
+    total = jnp.zeros((1, second_w.shape[0]), jnp.float32)
+    for index in (1, 2, 0):
+        column = columns[index]
         rows_all = jnp.concatenate([column, swap(column, "dp", 1)])
-        made.append((rows_all,) + tuple(chunk_call(rows_all, first_w, b_in, second_w)))
+        made[index] = (rows_all,) + tuple(chunk_call(rows_all, first_w, b_in, second_w, total))
+        total = made[index][5]
+
     row_parts, hidden_parts, slope_parts = [[m[i] for m in made] for i in range(3)]
 
     def first_sum(kept, leaving):
@@ -205,7 +213,7 @@
     d_tokens = lax.dot_general(
         chosen, returned, (((0,), (0,)), ((), ())), preferred_element_type=jnp.float32
     )
-    grad_bias = sum(m[5][:1] for m in made)
+    grad_bias = total
     return (d_tokens.astype(jnp.bfloat16), grad_first[None], grad_second[None], grad_bias)
 
 

time: 95.9 us -> 91.9 us (0.958)
  other arithmetic: 2.35 us -> 0.87 us
  local copies, waits for them, and re-layouts: 2.92 us -> 1.72 us
    unnamed x27 -> x25, local copies, waits for them, and re-layouts: 2.76 us -> 1.55 us
    pallas_call x1, Pallas kernels: 2.79 us -> 1.76 us  [dispatch_call(): pl.pallas_call(functools.partial(dispatch_kernel, capacity), out_shape=[j...]
  transfers between devices with their start and end apart: 26 -> 26, of which waited for: 6 -> 8; matrix products, arithmetic and copies ran while one was open for 14% -> 12% of each run, Pallas kernels for 12% -> 13%
where the time goes in v4:
time: 91.9 us; the launch traced here: 91.7 us
  starting transfers between devices  34.2 us (37%)
  waiting for transfers between devices  29.4 us (32%)
  Pallas kernels  13.3 us (14%)
  matrix products  11 us (12%)
  local copies, waits for them, and re-layouts  1.72 us (2%)
  between operations  1.18 us (1%)
    ppermute x26, starting transfers between devices, swap(): return lax.ppermute(value, axis, [(i, i ^ mask) for i in range(size)])  34.2 us
    ppermute x26, waiting for transfers between devices, swap(): return lax.ppermute(value, axis, [(i, i ^ mask) for i in range(size)])  29.4 us
    pallas_call x3, Pallas kernels, chunk_call(): pl.pallas_call(functools.partial(chunk_kernel, min(512, units)), out_shap...  11.5 us
    dot_general x1, matrix products, on_device(): lax.dot_general(hidden, rows_all[:, width:], (((0,), (0,)), ((), ())), pr...  5.1 us
    dot_general x1, matrix products, on_device(): lax.dot_general(rows_all[:, :width], d_pre, (((0,), (0,)), ((), ())), pre...  4.84 us
  transfers between devices with their start and end apart: 26, of which 8 were waited for; matrix products, arithmetic and copies ran while one was open for 12% of the time, Pallas kernels for 13%

profile of v4, /device:TPU:0, one launch (start us, length us, event | category | flops | bytes accessed | tf_op | source)
XLA Modules:
  0.0 91.7 jit_solution(9498423006255560870)
XLA Ops:
  0.6 1.8 %shard_map.111 = (bf16[192,128]{1,0:T(8,128)(2,1)S(1)}, bf16[24,3328]{1,0:T(8,128)(2,1)S(1)}, bf16[24,3328]{1,0:T(8,128)(2,1)S(1)}, bf16[24,3328]{1,0:T(8,128)(2...) custom-call(s32[1]{0:T(128)} %bitcast.me, ...), custom_call_target="tpu_custom_call" | custom-call | tf_op jit(solution)/shard_map/pallas_call | solution.py:71
  2.4 3.0 %collective-permute-start = (bf16[24,3328]{1,0:T(8,128)(2,1)S(1)}, bf16[24,3328]{1,0:T(8,128)(2,1)S(1)}, u32[]{:S(2)}, u32[]{:S(2)}) collective-permute-start(bf16[24,3328]{1,0:T(8,128)(2,1)S(1)} %get-tuple-element.41), channel_id=1, source_target_pairs={{0,4},{4,0},{8,12},{12,8},{16,20},{20,16},{24,28},{28,24},{1,5},{5... | collective-permute-start | bytes 479240 | tf_op jit(solution)/shard_map/ppermute | solution.py:16
  5.4 1.6 %collective-permute-start.1 = (bf16[24,3328]{1,0:T(8,128)(2,1)S(1)}, bf16[24,3328]{1,0:T(8,128)(2,1)S(1)}, u32[]{:S(2)}, u32[]{:S(2)}) collective-permute-start(bf16[24,3328]{1,0:T(8,128)(2,1)S(1)} %get-tuple-element.42), channel_id=1, source_target_pairs={{0,8},{4,12},{8,0},{12,4},{16,24},{20,28},{24,16},{28,20},{1,9},{5... | collective-permute-start | bytes 479240 | tf_op jit(solution)/shard_map/ppermute | solution.py:16
  7.0 5.0 %collective-permute-start.6 = (bf16[24,3328]{1,0:T(8,128)(2,1)S(1)}, bf16[24,3328]{1,0:T(8,128)(2,1)S(1)}, u32[]{:S(2)}, u32[]{:S(2)}) collective-permute-start(bf16[24,3328]{1,0:T(8,128)(2,1)S(1)} %get-tuple-element.45), channel_id=1, source_target_pairs={{0,28},{4,24},{8,20},{12,16},{16,12},{20,8},{24,4},{28,0},{1,29},{... | collective-permute-start | bytes 479240 | tf_op jit(solution)/shard_map/ppermute | solution.py:16
  12.2 1.3 %collective-permute-start.10 = (bf16[24,3328]{1,0:T(8,128)(2,1)S(1)}, bf16[24,3328]{1,0:T(8,128)(2,1)S(1)}, u32[]{:S(2)}, u32[]{:S(2)}) collective-permute-start(bf16[24,3328]{1,0:T(8,128)(2,1)S(1)} %get-tuple-element.47), channel_id=1, source_target_pairs={{0,20},{4,16},{8,28},{12,24},{16,4},{20,0},{24,12},{28,8},{1,21},{... | collective-permute-start | bytes 479240 | tf_op jit(solution)/shard_map/ppermute | solution.py:16
  13.5 1.5 %collective-permute-start.9 = (bf16[24,3328]{1,0:T(8,128)(2,1)S(1)}, bf16[24,3328]{1,0:T(8,128)(2,1)S(1)}, u32[]{:S(2)}, u32[]{:S(2)}) collective-permute-start(bf16[24,3328]{1,0:T(8,128)(2,1)S(1)} %get-tuple-element.46), channel_id=1, source_target_pairs={{0,16},{4,20},{8,24},{12,28},{16,0},{20,4},{24,8},{28,12},{1,17},{... | collective-permute-start | bytes 479240 | tf_op jit(solution)/shard_map/ppermute | solution.py:16
  15.3 1.6 %collective-permute-start.3 = (bf16[96,3328]{1,0:T(8,128)(2,1)S(1)}, bf16[96,3328]{1,0:T(8,128)(2,1)S(1)}, u32[]{:S(2)}, u32[]{:S(2)}) collective-permute-start(bf16[96,3328]{1,0:T(8,128)(2,1)S(1)} %pad_maximum_fusion.2), channel_id=1, source_target_pairs={{0,2},{1,3},{2,0},{3,1},{4,6},{5,7},{6,4},{7,5},{8,10},{9,11},{10,... | collective-permute-start | bytes 1916936 | tf_op jit(solution)/shard_map/ppermute | solution.py:16
  16.8 5.0 %collective-permute-done.6 = bf16[24,3328]{1,0:T(8,128)(2,1)S(1)} collective-permute-done((bf16[24,3328]{1,0:T(8,128)(2,1)S(1)}, bf16[24,3328]{1,0:T(8,128)(2,1)S(1)}, u32[]{:S(2)}, u32[]{:S(2)}) %collective-permute-start.6) | collective-permute-done | bytes 159776 | tf_op jit(solution)/shard_map/ppermute | solution.py:16
  21.8 3.3 %collective-permute-done.5 = bf16[24,3328]{1,0:T(8,128)(2,1)S(1)} collective-permute-done((bf16[24,3328]{1,0:T(8,128)(2,1)S(1)}, bf16[24,3328]{1,0:T(8,128)(2,1)S(1)}, u32[]{:S(2)}, u32[]{:S(2)}) %collective-permute-start.5) | collective-permute-done | bytes 159776 | tf_op jit(solution)/shard_map/ppermute | solution.py:16
  25.1 1.6 %collective-permute-start.7 = (bf16[48,3328]{1,0:T(8,128)(2,1)S(1)}, bf16[48,3328]{1,0:T(8,128)(2,1)S(1)}, u32[]{:S(2)}, u32[]{:S(2)}) collective-permute-start(bf16[48,3328]{1,0:T(8,128)(2,1)S(1)} %pad_maximum_fusion.5), channel_id=1, source_target_pairs={{0,2},{1,3},{2,0},{3,1},{4,6},{5,7},{6,4},{7,5},{8,10},{9,11},{10,... | collective-permute-start | bytes 958472 | tf_op jit(solution)/shard_map/ppermute | solution.py:16
  26.7 10.3 %collective-permute-done.10 = bf16[24,3328]{1,0:T(8,128)(2,1)S(1)} collective-permute-done((bf16[24,3328]{1,0:T(8,128)(2,1)S(1)}, bf16[24,3328]{1,0:T(8,128)(2,1)S(1)}, u32[]{:S(2)}, u32[]{:S(2)}) %collective-permute-start.10) | collective-permute-done | bytes 159776 | tf_op jit(solution)/shard_map/ppermute | solution.py:16
  37.0 1.8 %collective-permute-done.9 = bf16[24,3328]{1,0:T(8,128)(2,1)S(1)} collective-permute-done((bf16[24,3328]{1,0:T(8,128)(2,1)S(1)}, bf16[24,3328]{1,0:T(8,128)(2,1)S(1)}, u32[]{:S(2)}, u32[]{:S(2)}) %collective-permute-start.9) | collective-permute-done | bytes 159776 | tf_op jit(solution)/shard_map/ppermute | solution.py:16
  38.8 1.6 %collective-permute-start.11 = (bf16[48,3328]{1,0:T(8,128)(2,1)S(1)}, bf16[48,3328]{1,0:T(8,128)(2,1)S(1)}, u32[]{:S(2)}, u32[]{:S(2)}) collective-permute-start(bf16[48,3328]{1,0:T(8,128)(2,1)S(1)} %pad_maximum_fusion.6), channel_id=1, source_target_pairs={{0,2},{1,3},{2,0},{3,1},{4,6},{5,7},{6,4},{7,5},{8,10},{9,11},{10,... | collective-permute-start | bytes 958472 | tf_op jit(solution)/shard_map/ppermute | solution.py:16
  40.5 6.3 %collective-permute-done.11 = bf16[48,3328]{1,0:T(8,128)(2,1)S(1)} collective-permute-done((bf16[48,3328]{1,0:T(8,128)(2,1)S(1)}, bf16[48,3328]{1,0:T(8,128)(2,1)S(1)}, u32[]{:S(2)}, u32[]{:S(2)}) %collective-permute-start.11) | collective-permute-done | bytes 319520 | tf_op jit(solution)/shard_map/ppermute | solution.py:16
  46.9 0.6 collective-permute-start.8
  47.7 1.2 %collective-permute-done.12 = bf16[96,3328]{1,0:T(8,128)(2,1)S(1)} collective-permute-done((bf16[96,3328]{1,0:T(8,128)(2,1)S(1)}, bf16[96,3328]{1,0:T(8,128)(2,1)S(1)}, u32[]{:S(2)}, u32[]{:S(2)}) %collective-permute-start.12) | collective-permute-done | bytes 639008 | tf_op jit(solution)/shard_map/ppermute | solution.py:16
  49.0 0.9 copy-done
  49.9 3.3 %shard_map.112 = (bf16[192,1024]{1,0:T(8,128)(2,1)S(1)}, bf16[192,1024]{1,0:T(8,128)(2,1)S(1)}, bf16[96,1664]{1,0:T(8,128)(2,1)S(1)}, bf16[96,1664]{1,0:T(8,128)(2,1)S(1)}, f32[1,1024]{1,0:T(1,128)S(1)}) custom-call(bf16[192,3328]{1,0:T(8,128)(2,1)S(1)} %pad_maximum_fusion.1.rows, bf16[1664,1024]{1,0:T(8,128)(2,1)S(1)} %bitcast.11, f32[1,1024]{1,0:T(1,128)S(1)} %copy-done.2, ...), custom_call_target="tpu_custom_call" | custom-call | tf_op jit(solution)/shard_map/pallas_call | solution.py:118
  53.4 3.3 %shard_map.113 = (bf16[192,1024]{1,0:T(8,128)(2,1)S(1)}, bf16[192,1024]{1,0:T(8,128)(2,1)S(1)}, bf16[96,1664]{1,0:T(8,128)(2,1)S(1)}, bf16[96,1664]{1,0:T(8,128)(2,1)S(1)}, f32[1,1024]{1,0:T(1,128)S(1)}) custom-call(bf16[192,3328]{1,0:T(8,128)(2,1)S(1)} %pad_maximum_fusion.rows, bf16[1664,1024]{1,0:T(8,128)(2,1)S(1)} %bitcast.12, f32[1,1024]{1,0:T(1,128)S(1)} %copy-done.2, ...), custom_call_target="tpu_custom_call" | custom-call | tf_op jit(solution)/shard_map/pallas_call | solution.py:118
  57.4 1.5 %collective-permute-start.16 = (bf16[48,1664]{1,0:T(8,128)(2,1)S(1)}, bf16[48,1664]{1,0:T(8,128)(2,1)S(1)}, u32[]{:S(2)}, u32[]{:S(2)}) collective-permute-start(bf16[48,1664]{1,0:T(8,128)(2,1)S(1)} %slice.67), channel_id=1, source_target_pairs={{0,2},{1,3},{2,0},{3,1},{4,6},{5,7},{6,4},{7,5},{8,10},{9,11},{10,... | collective-permute-start | bytes 479240 | tf_op jit(solution)/shard_map/ppermute | solution.py:16
  59.0 1.1 %collective-permute-start.23 = (bf16[48,1664]{1,0:T(8,128)(2,1)S(1)}, bf16[48,1664]{1,0:T(8,128)(2,1)S(1)}, u32[]{:S(2)}, u32[]{:S(2)}) collective-permute-start(bf16[48,1664]{1,0:T(8,128)(2,1)S(1)} %slice.76), channel_id=1, source_target_pairs={{0,2},{1,3},{2,0},{3,1},{4,6},{5,7},{6,4},{7,5},{8,10},{9,11},{10,... | collective-permute-start | bytes 479240 | tf_op jit(solution)/shard_map/ppermute | solution.py:16
  60.3 4.9 %shard_map.114 = (bf16[384,1024]{1,0:T(8,128)(2,1)S(1)}, bf16[384,1024]{1,0:T(8,128)(2,1)S(1)}, bf16[192,1664]{1,0:T(8,128)(2,1)S(1)}, bf16[192,1664]{1,0:T(8,128)(2,1)S(1)}, f32[1,1024]{1,0:T(1,128)}) custom-call(bf16[384,3328]{1,0:T(8,128)(2,1)S(1)} %get-tuple-element.75.rows, bf16[1664,1024]{1,0:T(8,128)(2,1)S(1)} %bitcast.13, f32[1,1024]{1,0:T(1,128)S(1)} %copy-done.2, ...), custom_call_target="tpu_custom_call" | custom-call | tf_op jit(solution)/shard_map/pallas_call | solution.py:118
  65.5 1.4 %collective-permute-done.23 = bf16[48,1664]{1,0:T(8,128)(2,1)S(1)} collective-permute-done((bf16[48,1664]{1,0:T(8,128)(2,1)S(1)}, bf16[48,1664]{1,0:T(8,128)(2,1)S(1)}, u32[]{:S(2)}, u32[]{:S(2)}) %collective-permute-start.23) | collective-permute-done | bytes 159776 | tf_op jit(solution)/shard_map/ppermute | solution.py:16
  67.6 1.5 %collective-permute-start.14 = (bf16[96,1664]{1,0:T(8,128)(2,1)S(1)}, bf16[96,1664]{1,0:T(8,128)(2,1)S(1)}, u32[]{:S(2)}, u32[]{:S(2)}) collective-permute-start(bf16[96,1664]{1,0:T(8,128)(2,1)S(1)} %slice.65), channel_id=1, source_target_pairs={{0,2},{1,3},{2,0},{3,1},{4,6},{5,7},{6,4},{7,5},{8,10},{9,11},{10,... | collective-permute-start | bytes 958472 | tf_op jit(solution)/shard_map/ppermute | solution.py:16
  69.2 2.4 %collective-permute-start.18 = (bf16[24,1664]{1,0:T(8,128)(2,1)S(1)}, bf16[24,1664]{1,0:T(8,128)(2,1)S(1)}, u32[]{:S(2)}, u32[]{:S(2)}) collective-permute-start(bf16[24,1664]{1,0:T(8,128)(2,1)S(1)} %get-tuple-element.60), channel_id=1, source_target_pairs={{0,16},{4,20},{8,24},{12,28},{16,0},{20,4},{24,8},{28,12},{1,17},{... | collective-permute-start | bytes 239624 | tf_op jit(solution)/shard_map/ppermute | solution.py:16
  72.1 2.3 %collective-permute-start.24 = (bf16[24,1664]{1,0:T(8,128)(2,1)S(1)}, bf16[24,1664]{1,0:T(8,128)(2,1)S(1)}, u32[]{:S(2)}, u32[]{:S(2)}) collective-permute-start(bf16[24,1664]{1,0:T(8,128)(2,1)S(1)} %get-tuple-element.67), channel_id=1, source_target_pairs={{0,24},{4,28},{8,16},{12,20},{16,8},{20,12},{24,0},{28,4},{1,25},{... | collective-permute-start | bytes 239624 | tf_op jit(solution)/shard_map/ppermute | solution.py:16
  74.4 2.4 %collective-permute-start.25 = (bf16[24,1664]{1,0:T(8,128)(2,1)S(1)}, bf16[24,1664]{1,0:T(8,128)(2,1)S(1)}, u32[]{:S(2)}, u32[]{:S(2)}) collective-permute-start(bf16[24,1664]{1,0:T(8,128)(2,1)S(1)} %get-tuple-element.68), channel_id=1, source_target_pairs={{0,28},{4,24},{8,20},{12,16},{16,12},{20,8},{24,4},{28,0},{1,29},{... | collective-permute-start | bytes 239624 | tf_op jit(solution)/shard_map/ppermute | solution.py:16
  76.8 5.1 %fusion.1 = f32[1024,1664]{1,0:T(8,128)} fusion(bf16[768,3328]{1,0:T(8,128)(2,1)S(1)} %constant_dynamic-update-slice_fusion.11, bf16[192,1024]{1,0:T(8,128)(2,1)S(1)} %get-tuple-element.58, bf16[192,1024]{1,0:T(8,128)(2,1)S(1)} %get-tuple-element.57, bf16[384,1024]{1,0:T(8,128)(2,1)S(1)} %get-tuple-element.56), kind=kOutput, calls=%fused_computation.2 | convolution fusion | flops 2621964288 | bytes 10944512 | tf_op jit(solution)/shard_map/dot_general | solution.py:186
  82.1 0.6 collective-permute-start.17
  82.7 3.0 %collective-permute-start.21 = (bf16[24,1664]{1,0:T(8,128)(2,1)S(1)}, bf16[24,1664]{1,0:T(8,128)(2,1)S(1)}, u32[]{:S(2)}, u32[]{:S(2)}) collective-permute-start(bf16[24,1664]{1,0:T(8,128)(2,1)S(1)} %get-tuple-element.63), channel_id=1, source_target_pairs={{0,12},{4,8},{8,4},{12,0},{16,28},{20,24},{24,20},{28,16},{1,13},{... | collective-permute-start | bytes 239624 | tf_op jit(solution)/shard_map/ppermute | solution.py:16
  85.6 4.8 %convolution_bitcast_fusion = f32[1,1664,1024]{2,1,0:T(8,128)} fusion(bf16[768,3328]{1,0:T(8,128)(2,1)S(1)} %constant_dynamic-update-slice_fusion.11, bf16[192,1024]{1,0:T(8,128)(2,1)S(1)} %get-tuple-element.72, bf16[192,1024]{1,0:T(8,128)(2,1)S(1)} %get-tuple-element.71, bf16[384,1024]{1,0:T(8,128)(2,1)S(1)} %get-tuple-element.70), kind=kOutput, calls=%fused_computation | convolution fusion | flops 2621964288 | bytes 10944512 | tf_op jit(solution)/shard_map/dot_general | solution.py:202
  90.6 1.1 %convolution_convert_fusion = bf16[128,1664]{1,0:T(8,128)(2,1)} fusion(bf16[192,128]{1,0:T(8,128)(2,1)S(1)} %get-tuple-element.39, bf16[192,1664]{1,0:T(8,128)(2,1)S(1)} %constant_dynamic-update-slice_fusion.25), kind=kOutput, calls=%fused_computation.4 | convolution fusion | flops 82001920 | bytes 1114112 | tf_op jit(solution)/shard_map/dot_general | solution.py:213
  (74 shorter events, 3.6 us)
Async XLA Ops:
  2.4 9.8 %collective-permute-start = (bf16[24,3328]{1,0:T(8,128)(2,1)S(1)}, bf16[24,3328]{1,0:T(8,128)(2,1)S(1)}, u32[]{:S(2)}, u32[]{:S(2)}) collective-permute-start(bf16[24,3328]{1,0:T(8,128)(2,1)S(1)} %get-tuple-element.41), channel_id=1, source_target_pairs={{0,4},{4,0},{8,12},{12,8},{16,20},{20,16},{24,28},{28,24},{1,5},{5... | collective-permute-start | bytes 479240 | tf_op jit(solution)/shard_map/ppermute | solution.py:16
  5.4 8.1 %collective-permute-start.1 = (bf16[24,3328]{1,0:T(8,128)(2,1)S(1)}, bf16[24,3328]{1,0:T(8,128)(2,1)S(1)}, u32[]{:S(2)}, u32[]{:S(2)}) collective-permute-start(bf16[24,3328]{1,0:T(8,128)(2,1)S(1)} %get-tuple-element.42), channel_id=1, source_target_pairs={{0,8},{4,12},{8,0},{12,4},{16,24},{20,28},{24,16},{28,20},{1,9},{5... | collective-permute-start | bytes 479240 | tf_op jit(solution)/shard_map/ppermute | solution.py:16
  7.0 8.2 %collective-permute-start.2 = (bf16[24,3328]{1,0:T(8,128)(2,1)S(1)}, bf16[24,3328]{1,0:T(8,128)(2,1)S(1)}, u32[]{:S(2)}, u32[]{:S(2)}) collective-permute-start(bf16[24,3328]{1,0:T(8,128)(2,1)S(1)} %get-tuple-element.43), channel_id=1, source_target_pairs={{0,12},{4,8},{8,4},{12,0},{16,28},{20,24},{24,20},{28,16},{1,13},{... | collective-permute-start | bytes 479240 | tf_op jit(solution)/shard_map/ppermute | solution.py:16
  7.0 14.8 %collective-permute-start.6 = (bf16[24,3328]{1,0:T(8,128)(2,1)S(1)}, bf16[24,3328]{1,0:T(8,128)(2,1)S(1)}, u32[]{:S(2)}, u32[]{:S(2)}) collective-permute-start(bf16[24,3328]{1,0:T(8,128)(2,1)S(1)} %get-tuple-element.45), channel_id=1, source_target_pairs={{0,28},{4,24},{8,20},{12,16},{16,12},{20,8},{24,4},{28,0},{1,29},{... | collective-permute-start | bytes 479240 | tf_op jit(solution)/shard_map/ppermute | solution.py:16
  12.0 13.1 %collective-permute-start.5 = (bf16[24,3328]{1,0:T(8,128)(2,1)S(1)}, bf16[24,3328]{1,0:T(8,128)(2,1)S(1)}, u32[]{:S(2)}, u32[]{:S(2)}) collective-permute-start(bf16[24,3328]{1,0:T(8,128)(2,1)S(1)} %get-tuple-element.44), channel_id=1, source_target_pairs={{0,24},{4,28},{8,16},{12,20},{16,8},{20,12},{24,0},{28,4},{1,25},{... | collective-permute-start | bytes 479240 | tf_op jit(solution)/shard_map/ppermute | solution.py:16
  12.2 24.7 %collective-permute-start.10 = (bf16[24,3328]{1,0:T(8,128)(2,1)S(1)}, bf16[24,3328]{1,0:T(8,128)(2,1)S(1)}, u32[]{:S(2)}, u32[]{:S(2)}) collective-permute-start(bf16[24,3328]{1,0:T(8,128)(2,1)S(1)} %get-tuple-element.47), channel_id=1, source_target_pairs={{0,20},{4,16},{8,28},{12,24},{16,4},{20,0},{24,12},{28,8},{1,21},{... | collective-permute-start | bytes 479240 | tf_op jit(solution)/shard_map/ppermute | solution.py:16
  13.5 25.2 %collective-permute-start.9 = (bf16[24,3328]{1,0:T(8,128)(2,1)S(1)}, bf16[24,3328]{1,0:T(8,128)(2,1)S(1)}, u32[]{:S(2)}, u32[]{:S(2)}) collective-permute-start(bf16[24,3328]{1,0:T(8,128)(2,1)S(1)} %get-tuple-element.46), channel_id=1, source_target_pairs={{0,16},{4,20},{8,24},{12,28},{16,0},{20,4},{24,8},{28,12},{1,17},{... | collective-permute-start | bytes 479240 | tf_op jit(solution)/shard_map/ppermute | solution.py:16
  15.3 32.2 %collective-permute-start.3 = (bf16[96,3328]{1,0:T(8,128)(2,1)S(1)}, bf16[96,3328]{1,0:T(8,128)(2,1)S(1)}, u32[]{:S(2)}, u32[]{:S(2)}) collective-permute-start(bf16[96,3328]{1,0:T(8,128)(2,1)S(1)} %pad_maximum_fusion.2), channel_id=1, source_target_pairs={{0,2},{1,3},{2,0},{3,1},{4,6},{5,7},{6,4},{7,5},{8,10},{9,11},{10,... | collective-permute-start | bytes 1916936 | tf_op jit(solution)/shard_map/ppermute | solution.py:16
  25.1 21.8 %collective-permute-start.7 = (bf16[48,3328]{1,0:T(8,128)(2,1)S(1)}, bf16[48,3328]{1,0:T(8,128)(2,1)S(1)}, u32[]{:S(2)}, u32[]{:S(2)}) collective-permute-start(bf16[48,3328]{1,0:T(8,128)(2,1)S(1)} %pad_maximum_fusion.5), channel_id=1, source_target_pairs={{0,2},{1,3},{2,0},{3,1},{4,6},{5,7},{6,4},{7,5},{8,10},{9,11},{10,... | collective-permute-start | bytes 958472 | tf_op jit(solution)/shard_map/ppermute | solution.py:16
  38.8 7.9 %collective-permute-start.11 = (bf16[48,3328]{1,0:T(8,128)(2,1)S(1)}, bf16[48,3328]{1,0:T(8,128)(2,1)S(1)}, u32[]{:S(2)}, u32[]{:S(2)}) collective-permute-start(bf16[48,3328]{1,0:T(8,128)(2,1)S(1)} %pad_maximum_fusion.6), channel_id=1, source_target_pairs={{0,2},{1,3},{2,0},{3,1},{4,6},{5,7},{6,4},{7,5},{8,10},{9,11},{10,... | collective-permute-start | bytes 958472 | tf_op jit(solution)/shard_map/ppermute | solution.py:16
  46.7 2.3 %copy-start.1 = (bf16[1,1024,1664]{2,1,0:T(8,128)(2,1)S(1)}, bf16[1,1024,1664]{2,1,0:T(8,128)(2,1)}, u32[]{:S(2)}) copy-start(bf16[1,1024,1664]{2,1,0:T(8,128)(2,1)} %param.15) | copy-start | bytes 10223620
  46.8 2.1 %collective-permute-start.12 = (bf16[96,3328]{1,0:T(8,128)(2,1)S(1)}, bf16[96,3328]{1,0:T(8,128)(2,1)S(1)}, u32[]{:S(2)}, u32[]{:S(2)}) collective-permute-start(bf16[96,3328]{1,0:T(8,128)(2,1)S(1)} %pad_maximum_fusion.4), channel_id=1, source_target_pairs={{0,1},{1,0},{2,3},{3,2},{4,5},{5,4},{6,7},{7,6},{8,9},{9,8},{10,11... | collective-permute-start | bytes 1916936 | tf_op jit(solution)/shard_map/ppermute | solution.py:16
  46.9 6.4 %collective-permute-start.8 = (bf16[96,3328]{1,0:T(8,128)(2,1)S(1)}, bf16[96,3328]{1,0:T(8,128)(2,1)S(1)}, u32[]{:S(2)}, u32[]{:S(2)}) collective-permute-start(bf16[96,3328]{1,0:T(8,128)(2,1)S(1)} %pad_maximum_fusion.3), channel_id=1, source_target_pairs={{0,1},{1,0},{2,3},{3,2},{4,5},{5,4},{6,7},{7,6},{8,9},{9,8},{10,11... | collective-permute-start | bytes 1916936 | tf_op jit(solution)/shard_map/ppermute | solution.py:16
  47.5 2.4 %copy-start = (bf16[1,1664,1024]{2,1,0:T(8,128)(2,1)S(1)}, bf16[1,1664,1024]{2,1,0:T(8,128)(2,1)}, u32[]{:S(2)}) copy-start(bf16[1,1664,1024]{2,1,0:T(8,128)(2,1)} %param.13) | copy-start | bytes 10223620
  47.5 2.4 %copy-start.2 = (f32[1,1024]{1,0:T(1,128)S(1)}, f32[1,1024]{1,0:T(1,128)}, u32[]{:S(2)}) copy-start(f32[1,1024]{1,0:T(1,128)} %bias.5) | copy-start | bytes 12292
  47.6 12.6 %collective-permute-start.4 = (bf16[192,3328]{1,0:T(8,128)(2,1)S(1)}, bf16[192,3328]{1,0:T(8,128)(2,1)S(1)}, u32[]{:S(2)}, u32[]{:S(2)}) collective-permute-start(bf16[192,3328]{1,0:T(8,128)(2,1)S(1)} %get-tuple-element.78), channel_id=1, source_target_pairs={{0,1},{1,0},{2,3},{3,2},{4,5},{5,4},{6,7},{7,6},{8,9},{9,8},{10,11... | collective-permute-start | bytes 3833864 | tf_op jit(solution)/shard_map/ppermute | solution.py:16
  53.2 4.0 %collective-permute-start.15 = (bf16[96,1664]{1,0:T(8,128)(2,1)S(1)}, bf16[96,1664]{1,0:T(8,128)(2,1)S(1)}, u32[]{:S(2)}, u32[]{:S(2)}) collective-permute-start(bf16[96,1664]{1,0:T(8,128)(2,1)S(1)} %get-tuple-element.54), channel_id=1, source_target_pairs={{0,1},{1,0},{2,3},{3,2},{4,5},{5,4},{6,7},{7,6},{8,9},{9,8},{10,11... | collective-permute-start | bytes 958472 | tf_op jit(solution)/shard_map/ppermute | solution.py:16
  56.7 2.2 %collective-permute-start.22 = (bf16[96,1664]{1,0:T(8,128)(2,1)S(1)}, bf16[96,1664]{1,0:T(8,128)(2,1)S(1)}, u32[]{:S(2)}, u32[]{:S(2)}) collective-permute-start(bf16[96,1664]{1,0:T(8,128)(2,1)S(1)} %get-tuple-element.65), channel_id=1, source_target_pairs={{0,1},{1,0},{2,3},{3,2},{4,5},{5,4},{6,7},{7,6},{8,9},{9,8},{10,11... | collective-permute-start | bytes 958472 | tf_op jit(solution)/shard_map/ppermute | solution.py:16
  57.4 8.1 %collective-permute-start.16 = (bf16[48,1664]{1,0:T(8,128)(2,1)S(1)}, bf16[48,1664]{1,0:T(8,128)(2,1)S(1)}, u32[]{:S(2)}, u32[]{:S(2)}) collective-permute-start(bf16[48,1664]{1,0:T(8,128)(2,1)S(1)} %slice.67), channel_id=1, source_target_pairs={{0,2},{1,3},{2,0},{3,1},{4,6},{5,7},{6,4},{7,5},{8,10},{9,11},{10,... | collective-permute-start | bytes 479240 | tf_op jit(solution)/shard_map/ppermute | solution.py:16
  59.0 7.9 %collective-permute-start.23 = (bf16[48,1664]{1,0:T(8,128)(2,1)S(1)}, bf16[48,1664]{1,0:T(8,128)(2,1)S(1)}, u32[]{:S(2)}, u32[]{:S(2)}) collective-permute-start(bf16[48,1664]{1,0:T(8,128)(2,1)S(1)} %slice.76), channel_id=1, source_target_pairs={{0,2},{1,3},{2,0},{3,1},{4,6},{5,7},{6,4},{7,5},{8,10},{9,11},{10,... | collective-permute-start | bytes 479240 | tf_op jit(solution)/shard_map/ppermute | solution.py:16
  65.3 2.1 %collective-permute-start.13 = (bf16[192,1664]{1,0:T(8,128)(2,1)S(1)}, bf16[192,1664]{1,0:T(8,128)(2,1)S(1)}, u32[]{:S(2)}, u32[]{:S(2)}) collective-permute-start(bf16[192,1664]{1,0:T(8,128)(2,1)S(1)} %get-tuple-element.51), channel_id=1, source_target_pairs={{0,1},{1,0},{2,3},{3,2},{4,5},{5,4},{6,7},{7,6},{8,9},{9,8},{10,11... | collective-permute-start | bytes 1916936 | tf_op jit(solution)/shard_map/ppermute | solution.py:16
  67.6 14.3 %collective-permute-start.14 = (bf16[96,1664]{1,0:T(8,128)(2,1)S(1)}, bf16[96,1664]{1,0:T(8,128)(2,1)S(1)}, u32[]{:S(2)}, u32[]{:S(2)}) collective-permute-start(bf16[96,1664]{1,0:T(8,128)(2,1)S(1)} %slice.65), channel_id=1, source_target_pairs={{0,2},{1,3},{2,0},{3,1},{4,6},{5,7},{6,4},{7,5},{8,10},{9,11},{10,... | collective-permute-start | bytes 958472 | tf_op jit(solution)/shard_map/ppermute | solution.py:16
  69.2 13.5 %collective-permute-start.18 = (bf16[24,1664]{1,0:T(8,128)(2,1)S(1)}, bf16[24,1664]{1,0:T(8,128)(2,1)S(1)}, u32[]{:S(2)}, u32[]{:S(2)}) collective-permute-start(bf16[24,1664]{1,0:T(8,128)(2,1)S(1)} %get-tuple-element.60), channel_id=1, source_target_pairs={{0,16},{4,20},{8,24},{12,28},{16,0},{20,4},{24,8},{28,12},{1,17},{... | collective-permute-start | bytes 239624 | tf_op jit(solution)/shard_map/ppermute | solution.py:16
  71.6 11.1 %collective-permute-start.20 = (bf16[24,1664]{1,0:T(8,128)(2,1)S(1)}, bf16[24,1664]{1,0:T(8,128)(2,1)S(1)}, u32[]{:S(2)}, u32[]{:S(2)}) collective-permute-start(bf16[24,1664]{1,0:T(8,128)(2,1)S(1)} %get-tuple-element.62), channel_id=1, source_target_pairs={{0,20},{4,16},{8,28},{12,24},{16,4},{20,0},{24,12},{28,8},{1,21},{... | collective-permute-start | bytes 239624 | tf_op jit(solution)/shard_map/ppermute | solution.py:16
  72.1 18.5 %collective-permute-start.24 = (bf16[24,1664]{1,0:T(8,128)(2,1)S(1)}, bf16[24,1664]{1,0:T(8,128)(2,1)S(1)}, u32[]{:S(2)}, u32[]{:S(2)}) collective-permute-start(bf16[24,1664]{1,0:T(8,128)(2,1)S(1)} %get-tuple-element.67), channel_id=1, source_target_pairs={{0,24},{4,28},{8,16},{12,20},{16,8},{20,12},{24,0},{28,4},{1,25},{... | collective-permute-start | bytes 239624 | tf_op jit(solution)/shard_map/ppermute | solution.py:16
  74.4 16.2 %collective-permute-start.25 = (bf16[24,1664]{1,0:T(8,128)(2,1)S(1)}, bf16[24,1664]{1,0:T(8,128)(2,1)S(1)}, u32[]{:S(2)}, u32[]{:S(2)}) collective-permute-start(bf16[24,1664]{1,0:T(8,128)(2,1)S(1)} %get-tuple-element.68), channel_id=1, source_target_pairs={{0,28},{4,24},{8,20},{12,16},{16,12},{20,8},{24,4},{28,0},{1,29},{... | collective-permute-start | bytes 239624 | tf_op jit(solution)/shard_map/ppermute | solution.py:16
  82.1 8.4 %collective-permute-start.17 = (bf16[24,1664]{1,0:T(8,128)(2,1)S(1)}, bf16[24,1664]{1,0:T(8,128)(2,1)S(1)}, u32[]{:S(2)}, u32[]{:S(2)}) collective-permute-start(bf16[24,1664]{1,0:T(8,128)(2,1)S(1)} %get-tuple-element.81), channel_id=1, source_target_pairs={{0,4},{4,0},{8,12},{12,8},{16,20},{20,16},{24,28},{28,24},{1,5},{5... | collective-permute-start | bytes 239624 | tf_op jit(solution)/shard_map/ppermute | solution.py:16
  82.7 7.8 %collective-permute-start.19 = (bf16[24,1664]{1,0:T(8,128)(2,1)S(1)}, bf16[24,1664]{1,0:T(8,128)(2,1)S(1)}, u32[]{:S(2)}, u32[]{:S(2)}) collective-permute-start(bf16[24,1664]{1,0:T(8,128)(2,1)S(1)} %get-tuple-element.61), channel_id=1, source_target_pairs={{0,8},{4,12},{8,0},{12,4},{16,24},{20,28},{24,16},{28,20},{1,9},{5... | collective-permute-start | bytes 239624 | tf_op jit(solution)/shard_map/ppermute | solution.py:16
  82.7 7.8 %collective-permute-start.21 = (bf16[24,1664]{1,0:T(8,128)(2,1)S(1)}, bf16[24,1664]{1,0:T(8,128)(2,1)S(1)}, u32[]{:S(2)}, u32[]{:S(2)}) collective-permute-start(bf16[24,1664]{1,0:T(8,128)(2,1)S(1)} %get-tuple-element.63), channel_id=1, source_target_pairs={{0,12},{4,8},{8,4},{12,0},{16,28},{20,24},{24,20},{28,16},{1,13},{... | collective-permute-start | bytes 239624 | tf_op jit(solution)/shard_map/ppermute | solution.py:16
